TPU v7x, 256 devices: a whole 4x4x8 slice. The times are simulated.
256 devices in a mesh: group: 8 (over y, core), inner: 32 (over x, z).
Axes of the slice: x: 4, y: 4, z: 8, core: 2. Of those that a mesh axis runs over, the one named last changes fastest.
Arguments:
- left_part: bfloat16 [262144, 256], P(('group', 'inner')), may hold values from -12 to 12
- right_part: bfloat16 [262144, 256], P(('group', 'inner')), may hold values from -12 to 12
- relation: bfloat16 [256, 256], replicated, may hold values from -0.19 to 1.19
- src_index: int32 [256, 4, 512], P(('group', 'inner')), may hold values from 0 to 1023
- dst_index: int32 [256, 4, 512], P(('group', 'inner')), may hold values from 0 to 1023
- lengths: int32 [256, 4], P(('group', 'inner')), may hold values from 1 to 512, 1280 in all within a row
Outputs:
- left_out: bfloat16 [262144, 256], P(('group', 'inner'))
- right_out: bfloat16 [262144, 256], P(('group', 'inner'))
- relation_out: float32 [256, 256], replicated
All inputs are finite; a program needn't handle non-finite values.
Results may differ from a plain program's by a relative error of at most 0.012.
The roundings to bfloat16 on the way count: a program that leaves them out, or rounds other values in their place, can miss the bound.
Values may be sent and summed in bfloat16 or wider, within the bound.
No kernel may reach another device: no remote copies, remote signals or barrier semaphores. Data moves between devices by JAX's collectives and lax.ppermute only.
A program may use at most 64 MiB of HBM per device.

v0:
```python
import jax
import jax.numpy as jnp
from jax import lax
from jax.sharding import PartitionSpec as P

MEETINGS = 4


SCORE_SCALE = 0.1875
LR_EMBED = 0.5
LR_RELATION = 0.02


def swapped(value, axis, distance):
    mask = 2**distance
    pairs = [(source, source ^ mask) for source in range(lax.axis_size(axis))]
    return lax.ppermute(value, axis, pairs)


def bucket(left_block, holding, relation, src_row, dst_row, length):
    row_ids = jnp.arange(left_block.shape[0], dtype=jnp.int32)
    src_table = (src_row[:, None] == row_ids[None, :]).astype(jnp.bfloat16)
    picked = jnp.dot(src_table, left_block, preferred_element_type=jnp.float32).astype(jnp.bfloat16)
    queries = jnp.dot(picked, relation, preferred_element_type=jnp.float32).astype(jnp.bfloat16)
    scores = (
        lax.dot_general(
            queries, holding, (((1,), (1,)), ((), ())), preferred_element_type=jnp.float32
        )
        * SCORE_SCALE
    )
    maxima = jnp.max(scores, axis=1, keepdims=True)
    expos = jnp.exp(scores - maxima)
    softmax_w = expos / jnp.sum(expos, axis=1, keepdims=True)
    slot_ids = jnp.arange(src_row.shape[0], dtype=jnp.int32)
    live_mask = (slot_ids < length).astype(jnp.float32)
    columns = jnp.arange(holding.shape[0], dtype=jnp.int32)
    target = (columns[None, :] == dst_row[:, None]).astype(jnp.float32)
    coeffs = ((softmax_w - target) * live_mask[:, None]).astype(jnp.bfloat16)
    held_grad = (
        lax.dot_general(
            coeffs, queries, (((0,), (0,)), ((), ())), preferred_element_type=jnp.float32
        )
        * SCORE_SCALE
    )
    new_holding = (holding.astype(jnp.float32) - LR_EMBED * held_grad).astype(jnp.bfloat16)
    query_grad = (
        jnp.dot(coeffs, holding, preferred_element_type=jnp.float32) * SCORE_SCALE
    ).astype(jnp.bfloat16)
    relation_grad = lax.dot_general(
        picked, query_grad, (((0,), (0,)), ((), ())), preferred_element_type=jnp.float32
    )
    summed_rows = lax.dot_general(
        src_table, query_grad, (((0,), (0,)), ((), ())), preferred_element_type=jnp.float32
    )
    left_grad = lax.dot_general(
        summed_rows,
        relation.astype(jnp.float32),
        (((1,), (1,)), ((), ())),
        precision=lax.Precision.HIGHEST,
        preferred_element_type=jnp.float32,
    )
    new_left = (left_block.astype(jnp.float32) - LR_EMBED * left_grad).astype(jnp.bfloat16)
    return (new_left, new_holding, relation_grad)


def shards(left_part, right_part, relation, src_index, dst_index, lengths):
    log_inner = lax.axis_size("inner").bit_length() - 1
    left_block = left_part
    holding = right_part
    grad_total = jnp.zeros(relation.shape, jnp.float32)
    for meeting in range(MEETINGS):
        holding = swapped(holding, "inner", meeting % log_inner)
        left_block, holding, relation_grad = bucket(
            left_block,
            holding,
            relation,
            src_index[0, meeting],
            dst_index[0, meeting],
            lengths[0, meeting],
        )
        grad_total = grad_total + lax.psum(relation_grad, ("group", "inner"))
    relation_out = relation.astype(jnp.float32) - LR_RELATION * grad_total
    return (left_block, holding, relation_out)


def solution(mesh):
    in_specs = (
        P(("group", "inner"), None),
        P(("group", "inner"), None),
        P(),
        P(("group", "inner"), None, None),
        P(("group", "inner"), None, None),
        P(("group", "inner"), None),
    )
    out_specs = (P(("group", "inner"), None), P(("group", "inner"), None), P())
    return jax.shard_map(shards, mesh=mesh, in_specs=in_specs, out_specs=out_specs, check_vma=False)
```

profile of v0, /device:TPU:1, one launch (start us, length us, event | category | flops | bytes accessed | tf_op | source)
XLA Modules:
  0.0 362.6 jit_solution(15190486029907984446)
XLA Ops:
  7.2 2.5 collective-permute-start
  9.8 1.5 fusion.42
  13.2 0.9 fusion.41
  14.1 0.9 fusion.40
  15.6 1.6 fusion.24
  17.2 1.1 convolution_convert_fusion.3
  18.3 2.4 collective-permute-done
  23.1 3.9 %collective-permute-start.1 = (bf16[1024,256]{1,0:T(8,128)(2,1)S(1)}, bf16[1024,256]{1,0:T(8,128)(2,1)S(1)}, u32[]{:S(2)}, u32[]{:S(2)}) collective-permute-start(bf16[1024,256]{1,0:T(8,128)(2,1)S(1)} %subtract_convert_fusion.3), channel_id=1, source_target_pairs={{0,2},{1,3},{2,0},{3,1},{4,6},{5,7},{6,4},{7,5},{8,10},{9,11},{10,... | collective-permute-start | bytes 1572872 | tf_op jit(solution)/shard_map/ppermute | solution.py:17
  27.4 0.8 fusion.6
  29.9 19.7 %collective-permute-done.1 = bf16[1024,256]{1,0:T(8,128)(2,1)S(1)} collective-permute-done((bf16[1024,256]{1,0:T(8,128)(2,1)S(1)}, bf16[1024,256]{1,0:T(8,128)(2,1)S(1)}, u32[]{:S(2)}, u32[]{:S(2)}) %collective-permute-start.1) | collective-permute-done | bytes 524320 | tf_op jit(solution)/shard_map/ppermute | solution.py:17
  50.7 0.8 multiply_convert_fusion.2
  52.0 6.7 %collective-permute-start.2 = (bf16[1024,256]{1,0:T(8,128)(2,1)S(1)}, bf16[1024,256]{1,0:T(8,128)(2,1)S(1)}, u32[]{:S(2)}, u32[]{:S(2)}) collective-permute-start(bf16[1024,256]{1,0:T(8,128)(2,1)S(1)} %subtract_convert_fusion.2), channel_id=1, source_target_pairs={{0,4},{1,5},{2,6},{3,7},{4,0},{5,1},{6,2},{7,3},{8,12},{9,13},{10,... | collective-permute-start | bytes 1572872 | tf_op jit(solution)/shard_map/ppermute | solution.py:17
  59.2 0.8 fusion.4
  61.7 19.8 %collective-permute-done.2 = bf16[1024,256]{1,0:T(8,128)(2,1)S(1)} collective-permute-done((bf16[1024,256]{1,0:T(8,128)(2,1)S(1)}, bf16[1024,256]{1,0:T(8,128)(2,1)S(1)}, u32[]{:S(2)}, u32[]{:S(2)}) %collective-permute-start.2) | collective-permute-done | bytes 524320 | tf_op jit(solution)/shard_map/ppermute | solution.py:17
  82.5 0.8 multiply_convert_fusion.1
  83.8 1.3 collective-permute-start.3
  85.5 0.8 fusion.2
  88.0 7.8 %collective-permute-done.3 = bf16[1024,256]{1,0:T(8,128)(2,1)S(1)} collective-permute-done((bf16[1024,256]{1,0:T(8,128)(2,1)S(1)}, bf16[1024,256]{1,0:T(8,128)(2,1)S(1)}, u32[]{:S(2)}, u32[]{:S(2)}) %collective-permute-start.3) | collective-permute-done | bytes 524320 | tf_op jit(solution)/shard_map/ppermute | solution.py:17
  98.1 0.8 fusion
  99.0 1.0 convolution_add_fusion
  100.0 1.3 subtract_convert_fusion
  101.3 1.4 fusion.19
  102.7 251.4 %all-reduce.2.cloned.1.call-done = f32[256,256]{1,0:T(8,128)} async-done(((f32[256,256]{1,0:T(8,128)}), f32[256,256]{1,0:T(8,128)}) %all-reduce.2.cloned.1.call-update) | async-done | bytes 262160 | tf_op jit(solution)/shard_map/psum | solution.py:81
  354.1 1.7 multiply_subtract_fusion
  (39 shorter events, 16.8 us)
Async XLA Ops:
  7.2 346.9 %all-reduce.2.cloned.1.call-start = ((), (), s32[]{:S(2)}) async-start(), calls=%async_computation | async-start | bytes 524288 | tf_op jit(solution)/shard_map/psum | solution.py:81
  7.2 13.5 %collective-permute-start = (bf16[1024,256]{1,0:T(8,128)(2,1)}, bf16[1024,256]{1,0:T(8,128)(2,1)S(1)}, u32[]{:S(2)}, u32[]{:S(2)}) collective-permute-start(bf16[1024,256]{1,0:T(8,128)(2,1)} %param.7), channel_id=1, source_target_pairs={{0,1},{1,0},{2,3},{3,2},{4,5},{5,4},{6,7},{7,6},{8,9},{9,8},{10,11... | collective-permute-start | bytes 1572872 | tf_op jit(solution)/shard_map/ppermute | solution.py:17
  23.1 5.2 %copy-start = (bf16[256,256]{1,0:T(8,128)(2,1)S(1)}, bf16[256,256]{1,0:T(8,128)(2,1)}, u32[]{:S(2)}) copy-start(bf16[256,256]{1,0:T(8,128)(2,1)} %param.8) | copy-start | bytes 393220
  23.1 5.2 %copy-start.1 = (bf16[1024,256]{1,0:T(8,128)(2,1)S(1)}, bf16[1024,256]{1,0:T(8,128)(2,1)}, u32[]{:S(2)}) copy-start(bf16[1024,256]{1,0:T(8,128)(2,1)} %param.6) | copy-start | bytes 1572868
  23.1 26.5 %collective-permute-start.1 = (bf16[1024,256]{1,0:T(8,128)(2,1)S(1)}, bf16[1024,256]{1,0:T(8,128)(2,1)S(1)}, u32[]{:S(2)}, u32[]{:S(2)}) collective-permute-start(bf16[1024,256]{1,0:T(8,128)(2,1)S(1)} %subtract_convert_fusion.3), channel_id=1, source_target_pairs={{0,2},{1,3},{2,0},{3,1},{4,6},{5,7},{6,4},{7,5},{8,10},{9,11},{10,... | collective-permute-start | bytes 1572872 | tf_op jit(solution)/shard_map/ppermute | solution.py:17
  52.0 29.4 %collective-permute-start.2 = (bf16[1024,256]{1,0:T(8,128)(2,1)S(1)}, bf16[1024,256]{1,0:T(8,128)(2,1)S(1)}, u32[]{:S(2)}, u32[]{:S(2)}) collective-permute-start(bf16[1024,256]{1,0:T(8,128)(2,1)S(1)} %subtract_convert_fusion.2), channel_id=1, source_target_pairs={{0,4},{1,5},{2,6},{3,7},{4,0},{5,1},{6,2},{7,3},{8,12},{9,13},{10,... | collective-permute-start | bytes 1572872 | tf_op jit(solution)/shard_map/ppermute | solution.py:17
  83.8 12.0 %collective-permute-start.3 = (bf16[1024,256]{1,0:T(8,128)(2,1)S(1)}, bf16[1024,256]{1,0:T(8,128)(2,1)S(1)}, u32[]{:S(2)}, u32[]{:S(2)}) collective-permute-start(bf16[1024,256]{1,0:T(8,128)(2,1)S(1)} %subtract_convert_fusion.1), channel_id=1, source_target_pairs={{0,8},{1,9},{2,10},{3,11},{4,12},{5,13},{6,14},{7,15},{8,0},{9,1},... | collective-permute-start | bytes 1572872 | tf_op jit(solution)/shard_map/ppermute | solution.py:17
Sparse Core Ops, SparseCore 0:
  100.1 253.9 all-reduce.1
where the time goes:
time: 364 us; the launch traced here: 363 us
  waiting for transfers between devices  301 us (83%)
  matrix products  20 us (5%)
  starting transfers between devices  14.5 us (4%)
  between operations  14.3 us (4%)
  other arithmetic  9.64 us (3%)
    psum x1, waiting for transfers between devices, shards(): grad_total = grad_total + lax.psum(relation_grad, ('group', 'inner'))  251 us
    ppermute x4, waiting for transfers between devices, swapped(): return lax.ppermute(value, axis, pairs)  49.6 us
    ppermute x4, starting transfers between devices, swapped(): return lax.ppermute(value, axis, pairs)  14.4 us
  transfers between devices with their start and end apart: 5, of which 5 were waited for; matrix products, arithmetic and copies ran while one was open for 5% of the time, Pallas kernels for 0%

commit v1 on v0

--- a/solution.py
+++ b/solution.py
@@ -15,6 +15,17 @@
     mask = 2**distance
     pairs = [(source, source ^ mask) for source in range(lax.axis_size(axis))]
     return lax.ppermute(value, axis, pairs)
+
+
+def summed_over_all(partial):
+    axes = ("group", "inner")
+    rows, width = partial.shape
+    pieces = partial.astype(jnp.bfloat16).reshape(rows, 1, width)
+    pieces = lax.all_to_all(pieces, axes, 0, 0)
+    own_row = jnp.sum(pieces.astype(jnp.float32), axis=0).astype(jnp.bfloat16)
+    copies = jnp.broadcast_to(own_row[None], (rows, 1, width))
+    gathered = lax.all_to_all(copies, axes, 0, 0)
+    return gathered.reshape(rows, width).astype(jnp.float32)
 
 
 def bucket(left_block, holding, relation, src_row, dst_row, length):
@@ -78,7 +89,8 @@
             dst_index[0, meeting],
             lengths[0, meeting],
         )
-        grad_total = grad_total + lax.psum(relation_grad, ("group", "inner"))
+        grad_total = grad_total + relation_grad
+    grad_total = summed_over_all(grad_total)
     relation_out = relation.astype(jnp.float32) - LR_RELATION * grad_total
     return (left_block, holding, relation_out)
 

time: 364 us -> 143 us (0.39)
  waiting for transfers between devices: 301 us -> 72.1 us
  starting transfers between devices: 14.5 us -> 33.1 us
  between operations: 14.3 us -> 0.98 us
    psum x1 -> x0, waiting for transfers between devices: 251 us -> none  [shards(): grad_total = grad_total + lax.psum(relation_grad, ('group', 'inner'))]
    all_to_all x0 -> x2, waiting for transfers between devices: none -> 22.6 us  [the longest x1 11.7 us: summed_over_all(): gathered = lax.all_to_all(copies, axes, 0, 0)]
    all_to_all x0 -> x2, starting transfers between devices: none -> 18.6 us  [the longest x1 13 us: summed_over_all(): pieces = lax.all_to_all(pieces, axes, 0, 0)]
  transfers between devices with their start and end apart: 5 -> 6, of which waited for: 5 -> 6; matrix products, arithmetic and copies ran while one was open for 5% -> 15% of each run, Pallas kernels for 0% -> 0%
where the time goes in v1:
time: 143 us; the launch traced here: 142 us
  waiting for transfers between devices  72.1 us (50%)
  starting transfers between devices  33.1 us (23%)
  matrix products  19.3 us (13%)
  other arithmetic  11.5 us (8%)
  local copies, waits for them, and re-layouts  5.33 us (4%)
    ppermute x4, waiting for transfers between devices, swapped(): return lax.ppermute(value, axis, pairs)  49.6 us
    ppermute x4, starting transfers between devices, swapped(): return lax.ppermute(value, axis, pairs)  14.5 us
    all_to_all x1, starting transfers between devices, summed_over_all(): pieces = lax.all_to_all(pieces, axes, 0, 0)  13 us
    all_to_all x1, waiting for transfers between devices, summed_over_all(): gathered = lax.all_to_all(copies, axes, 0, 0)  11.7 us
    all_to_all x1, waiting for transfers between devices, summed_over_all(): pieces = lax.all_to_all(pieces, axes, 0, 0)  10.9 us
    all_to_all x1, starting transfers between devices, summed_over_all(): gathered = lax.all_to_all(copies, axes, 0, 0)  5.54 us
    dot_general x4, matrix products, bucket(): lax.dot_general(summed_rows, relation.astype(jnp.float32), (((1,), (1,)),...  3.36 us
    dot_general x4, matrix products, bucket(): lax.dot_general(src_table, query_grad, (((0,), (0,)), ((), ())), preferre...  3.27 us
  transfers between devices with their start and end apart: 6, of which 6 were waited for; matrix products, arithmetic and copies ran while one was open for 15% of the time, Pallas kernels for 0%

profile of v1, /device:TPU:1, one launch (start us, length us, event | category | flops | bytes accessed | tf_op | source)
XLA Modules:
  0.0 142.2 jit_solution(1545039782911385649)
XLA Ops:
  0.6 2.5 %collective-permute-start = (bf16[1024,256]{1,0:T(8,128)(2,1)}, bf16[1024,256]{1,0:T(8,128)(2,1)S(1)}, u32[]{:S(2)}, u32[]{:S(2)}) collective-permute-start(bf16[1024,256]{1,0:T(8,128)(2,1)} %param.7), channel_id=1, source_target_pairs={{0,1},{1,0},{2,3},{3,2},{4,5},{5,4},{6,7},{7,6},{8,9},{9,8},{10,11... | collective-permute-start | bytes 1572872 | tf_op jit(solution)/shard_map/ppermute | solution.py:17
  3.2 1.5 %fusion.44 = (s32[1,1]{1,0:T(1,128)}, s32[1,1]{1,0:T(1,128)}, s32[1,1]{1,0:T(1,128)}, s32[1,1]{1,0:T(1,128)}) fusion(s32[1,4]{1,0:T(1,128)} %param.11), kind=kLoop, calls=%fused_computation.93 | loop fusion | bytes 32 | tf_op jit(solution)/shard_map/slice | solution.py:90
  6.6 0.9 fusion.43
  7.5 0.9 fusion.42
  9.0 1.6 %fusion.24 = bf16[512,256]{1,0:T(8,128)(2,1)S(1)} fusion(bf16[1024,256]{1,0:T(8,128)(2,1)} %param.6, s32[512]{0:T(512)S(1)} %bitcast.82), kind=kOutput, calls=%fused_computation.56 | convolution fusion | flops 269090816 | bytes 788480 | tf_op jit(solution)/shard_map/dot_general | solution.py:34
  10.6 1.1 convolution_convert_fusion.3
  11.7 2.4 %collective-permute-done = bf16[1024,256]{1,0:T(8,128)(2,1)S(1)} collective-permute-done((bf16[1024,256]{1,0:T(8,128)(2,1)}, bf16[1024,256]{1,0:T(8,128)(2,1)S(1)}, u32[]{:S(2)}, u32[]{:S(2)}) %collective-permute-start) | collective-permute-done | bytes 524320 | tf_op jit(solution)/shard_map/ppermute | solution.py:17
  16.5 3.9 %collective-permute-start.1 = (bf16[1024,256]{1,0:T(8,128)(2,1)S(1)}, bf16[1024,256]{1,0:T(8,128)(2,1)S(1)}, u32[]{:S(2)}, u32[]{:S(2)}) collective-permute-start(bf16[1024,256]{1,0:T(8,128)(2,1)S(1)} %subtract_convert_fusion.3), channel_id=1, source_target_pairs={{0,2},{1,3},{2,0},{3,1},{4,6},{5,7},{6,4},{7,5},{8,10},{9,11},{10,... | collective-permute-start | bytes 1572872 | tf_op jit(solution)/shard_map/ppermute | solution.py:17
  20.8 0.8 fusion.6
  23.3 19.7 %collective-permute-done.1 = bf16[1024,256]{1,0:T(8,128)(2,1)S(1)} collective-permute-done((bf16[1024,256]{1,0:T(8,128)(2,1)S(1)}, bf16[1024,256]{1,0:T(8,128)(2,1)S(1)}, u32[]{:S(2)}, u32[]{:S(2)}) %collective-permute-start.1) | collective-permute-done | bytes 524320 | tf_op jit(solution)/shard_map/ppermute | solution.py:17
  45.4 6.8 %collective-permute-start.2 = (bf16[1024,256]{1,0:T(8,128)(2,1)S(1)}, bf16[1024,256]{1,0:T(8,128)(2,1)S(1)}, u32[]{:S(2)}, u32[]{:S(2)}) collective-permute-start(bf16[1024,256]{1,0:T(8,128)(2,1)S(1)} %subtract_convert_fusion.2), channel_id=1, source_target_pairs={{0,4},{1,5},{2,6},{3,7},{4,0},{5,1},{6,2},{7,3},{8,12},{9,13},{10,... | collective-permute-start | bytes 1572872 | tf_op jit(solution)/shard_map/ppermute | solution.py:17
  52.6 0.8 fusion.4
  55.1 19.8 %collective-permute-done.2 = bf16[1024,256]{1,0:T(8,128)(2,1)S(1)} collective-permute-done((bf16[1024,256]{1,0:T(8,128)(2,1)S(1)}, bf16[1024,256]{1,0:T(8,128)(2,1)S(1)}, u32[]{:S(2)}, u32[]{:S(2)}) %collective-permute-start.2) | collective-permute-done | bytes 524320 | tf_op jit(solution)/shard_map/ppermute | solution.py:17
  77.3 1.3 collective-permute-start.3
  79.0 0.8 fusion.2
  81.5 7.8 %collective-permute-done.3 = bf16[1024,256]{1,0:T(8,128)(2,1)S(1)} collective-permute-done((bf16[1024,256]{1,0:T(8,128)(2,1)S(1)}, bf16[1024,256]{1,0:T(8,128)(2,1)S(1)}, u32[]{:S(2)}, u32[]{:S(2)}) %collective-permute-start.3) | collective-permute-done | bytes 524320 | tf_op jit(solution)/shard_map/ppermute | solution.py:17
  93.7 13.0 %all-to-all-start = ((bf16[256,2,128]{2,1,0:T(2,128)(2,1)}), bf16[256,2,128]{2,1,0:T(2,128)(2,1)S(1)}, u32[]{:S(2)}, u32[]{:S(2)}) async-start(bf16[256,2,128]{2,1,0:T(2,128)(2,1)} %reshape.55), calls=%async_computation | async-start | bytes 262144 | tf_op jit(solution)/shard_map/all_to_all | solution.py:24
  106.8 1.3 subtract_convert_fusion
  108.1 0.8 fusion
  108.9 10.9 %all-to-all-done = bf16[256,2,128]{2,1,0:T(2,128)(2,1)S(1)} async-done(((bf16[256,2,128]{2,1,0:T(2,128)(2,1)}), bf16[256,2,128]{2,1,0:T(2,128)(2,1)S(1)}, u32[]{:S(2)}, u32[]{:S(2)}) %all-to-all-start) | async-done | bytes 131104 | tf_op jit(solution)/shard_map/all_to_all | solution.py:24
  120.3 1.4 reduce.3
  122.4 5.5 %all-to-all-start.1 = ((bf16[256,2,128]{2,1,0:T(2,128)(2,1)}), bf16[256,2,128]{2,1,0:T(2,128)(2,1)S(1)}, u32[]{:S(2)}, u32[]{:S(2)}) async-start(bf16[256,2,128]{2,1,0:T(2,128)(2,1)} %reshape.57), calls=%async_computation.1 | async-start | bytes 262144 | tf_op jit(solution)/shard_map/all_to_all | solution.py:27
  127.9 1.4 %fusion.19 = bf16[1024,256]{1,0:T(8,128)(2,1)} fusion(f32[1024,256]{1,0:T(8,128)S(1)} %fusion, bf16[256,256]{1,0:T(8,128)(2,1)S(1)} %copy-done, bf16[1024,256]{1,0:T(8,128)(2,1)S(1)} %fusion.18), kind=kOutput, calls=%fused_computation.47 | convolution fusion | flops 806354944 | bytes 2228224 | tf_op jit(solution)/shard_map/dot_general | solution.py:66
  129.4 11.7 %all-to-all-done.1 = bf16[256,2,128]{2,1,0:T(2,128)(2,1)S(1)} async-done(((bf16[256,2,128]{2,1,0:T(2,128)(2,1)}), bf16[256,2,128]{2,1,0:T(2,128)(2,1)S(1)}, u32[]{:S(2)}, u32[]{:S(2)}) %all-to-all-start.1) | async-done | bytes 131104 | tf_op jit(solution)/shard_map/all_to_all | solution.py:27
  (50 shorter events, 22.8 us)
Async XLA Ops:
  0.6 13.5 %collective-permute-start = (bf16[1024,256]{1,0:T(8,128)(2,1)}, bf16[1024,256]{1,0:T(8,128)(2,1)S(1)}, u32[]{:S(2)}, u32[]{:S(2)}) collective-permute-start(bf16[1024,256]{1,0:T(8,128)(2,1)} %param.7), channel_id=1, source_target_pairs={{0,1},{1,0},{2,3},{3,2},{4,5},{5,4},{6,7},{7,6},{8,9},{9,8},{10,11... | collective-permute-start | bytes 1572872 | tf_op jit(solution)/shard_map/ppermute | solution.py:17
  16.5 5.2 %copy-start = (bf16[256,256]{1,0:T(8,128)(2,1)S(1)}, bf16[256,256]{1,0:T(8,128)(2,1)}, u32[]{:S(2)}) copy-start(bf16[256,256]{1,0:T(8,128)(2,1)} %param.8) | copy-start | bytes 393220
  16.5 5.2 %copy-start.1 = (bf16[1024,256]{1,0:T(8,128)(2,1)S(1)}, bf16[1024,256]{1,0:T(8,128)(2,1)}, u32[]{:S(2)}) copy-start(bf16[1024,256]{1,0:T(8,128)(2,1)} %param.6) | copy-start | bytes 1572868
  16.5 26.5 %collective-permute-start.1 = (bf16[1024,256]{1,0:T(8,128)(2,1)S(1)}, bf16[1024,256]{1,0:T(8,128)(2,1)S(1)}, u32[]{:S(2)}, u32[]{:S(2)}) collective-permute-start(bf16[1024,256]{1,0:T(8,128)(2,1)S(1)} %subtract_convert_fusion.3), channel_id=1, source_target_pairs={{0,2},{1,3},{2,0},{3,1},{4,6},{5,7},{6,4},{7,5},{8,10},{9,11},{10,... | collective-permute-start | bytes 1572872 | tf_op jit(solution)/shard_map/ppermute | solution.py:17
  45.4 29.5 %collective-permute-start.2 = (bf16[1024,256]{1,0:T(8,128)(2,1)S(1)}, bf16[1024,256]{1,0:T(8,128)(2,1)S(1)}, u32[]{:S(2)}, u32[]{:S(2)}) collective-permute-start(bf16[1024,256]{1,0:T(8,128)(2,1)S(1)} %subtract_convert_fusion.2), channel_id=1, source_target_pairs={{0,4},{1,5},{2,6},{3,7},{4,0},{5,1},{6,2},{7,3},{8,12},{9,13},{10,... | collective-permute-start | bytes 1572872 | tf_op jit(solution)/shard_map/ppermute | solution.py:17
  77.3 12.0 %collective-permute-start.3 = (bf16[1024,256]{1,0:T(8,128)(2,1)S(1)}, bf16[1024,256]{1,0:T(8,128)(2,1)S(1)}, u32[]{:S(2)}, u32[]{:S(2)}) collective-permute-start(bf16[1024,256]{1,0:T(8,128)(2,1)S(1)} %subtract_convert_fusion.1), channel_id=1, source_target_pairs={{0,8},{1,9},{2,10},{3,11},{4,12},{5,13},{6,14},{7,15},{8,0},{9,1},... | collective-permute-start | bytes 1572872 | tf_op jit(solution)/shard_map/ppermute | solution.py:17
  93.7 26.0 %all-to-all-start = ((bf16[256,2,128]{2,1,0:T(2,128)(2,1)}), bf16[256,2,128]{2,1,0:T(2,128)(2,1)S(1)}, u32[]{:S(2)}, u32[]{:S(2)}) async-start(bf16[256,2,128]{2,1,0:T(2,128)(2,1)} %reshape.55), calls=%async_computation | async-start | bytes 262144 | tf_op jit(solution)/shard_map/all_to_all | solution.py:24
  122.4 18.7 %all-to-all-start.1 = ((bf16[256,2,128]{2,1,0:T(2,128)(2,1)}), bf16[256,2,128]{2,1,0:T(2,128)(2,1)S(1)}, u32[]{:S(2)}, u32[]{:S(2)}) async-start(bf16[256,2,128]{2,1,0:T(2,128)(2,1)} %reshape.57), calls=%async_computation.1 | async-start | bytes 262144 | tf_op jit(solution)/shard_map/all_to_all | solution.py:27

commit v2 on v0

v2 whole, which is shorter than its diff:
```python
import jax
import jax.numpy as jnp
from jax import lax
from jax.sharding import PartitionSpec as P

SCORE_SCALE = 0.1875
LR_EMBED = 0.5
LR_RELATION = 0.02
AXES = ("group", "inner")


def moved(value, mask):
    pairs = [(source, source ^ mask) for source in range(lax.axis_size("inner"))]
    return lax.ppermute(value, "inner", pairs)


def matmul(a, b, dims):
    return lax.dot_general(a, b, (dims, ((), ())), preferred_element_type=jnp.float32)


def summed_over_all(partial):
    rows, width = partial.shape
    pieces = partial.astype(jnp.bfloat16).reshape(rows, 2, width // 2)
    pieces = lax.all_to_all(pieces, AXES, 0, 0)
    own_row = jnp.sum(pieces.astype(jnp.float32), axis=0).astype(jnp.bfloat16)
    copies = jnp.broadcast_to(own_row[None], pieces.shape)
    gathered = lax.all_to_all(copies, AXES, 0, 0)
    return gathered.reshape(rows, width).astype(jnp.float32)


def source_table(src_row, rows):
    return (src_row[:, None] == jnp.arange(rows, dtype=jnp.int32)[None, :]).astype(jnp.bfloat16)


def picked_rows(left_block, table):
    return matmul(table, left_block, ((1,), (0,))).astype(jnp.bfloat16)


def edge_coeffs(picked, relation, holding, target):
    queries = matmul(picked, relation, ((1,), (0,))).astype(jnp.bfloat16)
    scores = matmul(queries, holding, ((1,), (1,))) * SCORE_SCALE
    maxima = jnp.max(scores, axis=1, keepdims=True)
    expos = jnp.exp(scores - maxima)
    softmax_w = expos / jnp.sum(expos, axis=1, keepdims=True)
    live_mask = (target >= 0).astype(jnp.float32)
    columns = jnp.arange(holding.shape[0], dtype=jnp.int32)
    onehot = (columns[None, :] == target[:, None]).astype(jnp.float32)
    coeffs = ((softmax_w - onehot) * live_mask[:, None]).astype(jnp.bfloat16)
    return queries, coeffs


def updated_holding(holding, coeffs, queries):
    held_grad = matmul(coeffs, queries, ((0,), (0,))) * SCORE_SCALE
    return (holding.astype(jnp.float32) - LR_EMBED * held_grad).astype(jnp.bfloat16)


def query_gradient(coeffs, holding):
    return (matmul(coeffs, holding, ((1,), (0,))) * SCORE_SCALE).astype(jnp.bfloat16)


def updated_left(left_block, table, query_grad, relation):
    summed_rows = matmul(table, query_grad, ((0,), (0,)))
    high = summed_rows.astype(jnp.bfloat16)
    low = (summed_rows - high.astype(jnp.float32)).astype(jnp.bfloat16)
    left_grad = matmul(high, relation, ((1,), (1,))) + matmul(low, relation, ((1,), (1,)))
    return (left_block.astype(jnp.float32) - LR_EMBED * left_grad).astype(jnp.bfloat16)


def shards(left_part, right_part, relation, src_index, dst_index, lengths):
    rows = left_part.shape[0]
    slots = jnp.arange(src_index.shape[2], dtype=jnp.int32)
    targets = jnp.where(slots[None, :] < lengths[0][:, None], dst_index[0], -1)
    tables = [source_table(src_index[0, meeting], rows) for meeting in range(4)]

    held = moved(right_part, 1)
    picked, targets = lax.optimization_barrier((picked_rows(left_part, tables[0]), targets))
    target1 = moved(targets[1], 2)
    target3 = moved(targets[3], 8)
    queries, coeffs = edge_coeffs(picked, relation, held, targets[0])
    query_grad = query_gradient(coeffs, held)
    left = updated_left(left_part, tables[0], query_grad, relation)
    relation_grad = matmul(picked, query_grad, ((0,), (0,)))
    held = updated_holding(held, coeffs, queries)

    picked = moved(picked_rows(left, tables[1]), 2)
    queries, coeffs = edge_coeffs(picked, relation, held, target1)
    new_held, coeffs = lax.optimization_barrier((updated_holding(held, coeffs, queries), coeffs))
    query_grad = query_gradient(coeffs, held)
    relation_grad = relation_grad + matmul(picked, query_grad, ((0,), (0,)))
    held = moved(new_held, 6)
    left = updated_left(left, tables[1], moved(query_grad, 2), relation)

    picked = picked_rows(left, tables[2])
    queries, coeffs = edge_coeffs(picked, relation, held, targets[2])
    query_grad = query_gradient(coeffs, held)
    left = updated_left(left, tables[2], query_grad, relation)
    relation_grad = relation_grad + matmul(picked, query_grad, ((0,), (0,)))
    held = updated_holding(held, coeffs, queries)

    picked = moved(picked_rows(left, tables[3]), 8)
    queries, coeffs = edge_coeffs(picked, relation, held, target3)
    query_grad = query_gradient(coeffs, held)
    relation_grad = relation_grad + matmul(picked, query_grad, ((0,), (0,)))
    relation_grad, query_grad = lax.optimization_barrier((relation_grad, query_grad))
    total = summed_over_all(relation_grad)
    held = moved(updated_holding(held, coeffs, queries), 8)
    left = updated_left(left, tables[3], moved(query_grad, 8), relation)

    relation_out = relation.astype(jnp.float32) - LR_RELATION * total
    return (left, held, relation_out)


def solution(mesh):
    in_specs = (
        P(AXES, None),
        P(AXES, None),
        P(),
        P(AXES, None, None),
        P(AXES, None, None),
        P(AXES, None),
    )
    out_specs = (P(AXES, None), P(AXES, None), P())
    return jax.shard_map(shards, mesh=mesh, in_specs=in_specs, out_specs=out_specs, check_vma=False)
```

time: 364 us -> 130 us (0.36)
  waiting for transfers between devices: 301 us -> 55.7 us
  starting transfers between devices: 14.5 us -> 42.7 us
  between operations: 14.3 us -> 0.97 us
    psum x1 -> x0, waiting for transfers between devices: 251 us -> none  [shards(): grad_total = grad_total + lax.psum(relation_grad, ('group', 'inner'))]
    all_to_all x0 -> x2, waiting for transfers between devices: none -> 20.7 us  [the longest x1 10.8 us: summed_over_all(): pieces = lax.all_to_all(pieces, AXES, 0, 0)]
    all_to_all x0 -> x2, starting transfers between devices: none -> 20.2 us  [the longest x1 14.7 us: summed_over_all(): pieces = lax.all_to_all(pieces, AXES, 0, 0)]
    ppermute x4 -> x9, waiting for transfers between devices: 49.6 us -> 35 us  [moved(): return lax.ppermute(value, 'inner', pairs)]
    ppermute x4 -> x9, starting transfers between devices: 14.4 us -> 22.5 us  [moved(): return lax.ppermute(value, 'inner', pairs)]
    dot_general x32 -> x36, matrix products: 20 us -> 19.6 us  [matmul(): lax.dot_general(a, b, (dims, ((), ())), preferred_element_type=jnp.float32)]
  transfers between devices with their start and end apart: 5 -> 11, of which waited for: 5 -> 7; matrix products, arithmetic and copies ran while one was open for 5% -> 11% of each run, Pallas kernels for 0% -> 0%
where the time goes in v2:
time: 130 us; the launch traced here: 129 us
  waiting for transfers between devices  55.7 us (43%)
  starting transfers between devices  42.7 us (33%)
  matrix products  19.6 us (15%)
  other arithmetic  7.26 us (6%)
  local copies, waits for them, and re-layouts  3.09 us (2%)
    ppermute x9, waiting for transfers between devices, moved(): return lax.ppermute(value, 'inner', pairs)  35 us
    ppermute x9, starting transfers between devices, moved(): return lax.ppermute(value, 'inner', pairs)  22.5 us
    dot_general x36, matrix products, matmul(): lax.dot_general(a, b, (dims, ((), ())), preferred_element_type=jnp.float32)  19.6 us
    all_to_all x1, starting transfers between devices, summed_over_all(): pieces = lax.all_to_all(pieces, AXES, 0, 0)  14.7 us
    all_to_all x1, waiting for transfers between devices, summed_over_all(): pieces = lax.all_to_all(pieces, AXES, 0, 0)  10.8 us
    all_to_all x1, waiting for transfers between devices, summed_over_all(): gathered = lax.all_to_all(copies, AXES, 0, 0)  9.84 us
    all_to_all x1, starting transfers between devices, summed_over_all(): gathered = lax.all_to_all(copies, AXES, 0, 0)  5.54 us
    convert_element_type x4, other arithmetic, edge_coeffs(): coeffs = ((softmax_w - onehot) * live_mask[:, None]).astype(jnp.bfloat16)  3.22 us
  transfers between devices with their start and end apart: 11, of which 7 were waited for; matrix products, arithmetic and copies ran while one was open for 11% of the time, Pallas kernels for 0%

profile of v2, /device:TPU:1, one launch (start us, length us, event | category | flops | bytes accessed | tf_op | source)
XLA Modules:
  0.0 129.4 jit_solution(14087035046787603650)
XLA Ops:
  0.6 2.5 %collective-permute-start = (bf16[1024,256]{1,0:T(8,128)(2,1)}, bf16[1024,256]{1,0:T(8,128)(2,1)S(1)}, u32[]{:S(2)}, u32[]{:S(2)}) collective-permute-start(bf16[1024,256]{1,0:T(8,128)(2,1)} %param.7), channel_id=1, source_target_pairs={{0,1},{1,0},{2,3},{3,2},{4,5},{5,4},{6,7},{7,6},{8,9},{9,8},{10,11... | collective-permute-start | bytes 1572872 | tf_op jit(solution)/shard_map/ppermute | solution.py:14
  3.2 0.9 fusion.53
  4.0 1.5 %fusion.28 = bf16[512,256]{1,0:T(8,128)(2,1)S(1)} fusion(bf16[1024,256]{1,0:T(8,128)(2,1)} %param.6, s32[512]{0:T(512)S(1)} %bitcast.81), kind=kOutput, calls=%fused_computation.60 | convolution fusion | flops 269090816 | bytes 788480 | tf_op jit(solution)/shard_map/dot_general | solution.py:18
  6.4 3.1 %collective-permute-start.2 = (s32[512]{0:T(512)S(1)}, s32[512]{0:T(512)S(1)}, u32[]{:S(2)}, u32[]{:S(2)}) collective-permute-start(s32[512]{0:T(512)S(1)} %bitcast.84), channel_id=1, source_target_pairs={{0,2},{1,3},{2,0},{3,1},{4,6},{5,7},{6,4},{7,5},{8,10},{9,11},{10,... | collective-permute-start | bytes 6152 | tf_op jit(solution)/shard_map/ppermute | solution.py:14
  9.4 1.2 collective-permute-start.6
  10.7 1.1 convolution_convert_fusion.3
  11.8 2.3 %collective-permute-done.2 = s32[512]{0:T(512)S(1)} collective-permute-done((s32[512]{0:T(512)S(1)}, s32[512]{0:T(512)S(1)}, u32[]{:S(2)}, u32[]{:S(2)}) %collective-permute-start.2) | collective-permute-done | bytes 2080 | tf_op jit(solution)/shard_map/ppermute | solution.py:14
  16.5 0.8 fusion.6
  18.5 3.9 %collective-permute-start.1 = (bf16[512,256]{1,0:T(8,128)(2,1)S(1)}, bf16[512,256]{1,0:T(8,128)(2,1)S(1)}, u32[]{:S(2)}, u32[]{:S(2)}) collective-permute-start(bf16[512,256]{1,0:T(8,128)(2,1)S(1)} %fusion.29), channel_id=1, source_target_pairs={{0,2},{1,3},{2,0},{3,1},{4,6},{5,7},{6,4},{7,5},{8,10},{9,11},{10,... | collective-permute-start | bytes 786440 | tf_op jit(solution)/shard_map/ppermute | solution.py:14
  22.9 10.4 %collective-permute-done.1 = bf16[512,256]{1,0:T(8,128)(2,1)S(1)} collective-permute-done((bf16[512,256]{1,0:T(8,128)(2,1)S(1)}, bf16[512,256]{1,0:T(8,128)(2,1)S(1)}, u32[]{:S(2)}, u32[]{:S(2)}) %collective-permute-start.1) | collective-permute-done | bytes 262176 | tf_op jit(solution)/shard_map/ppermute | solution.py:14
  36.7 7.4 %collective-permute-start.4 = (bf16[1024,256]{1,0:T(8,128)(2,1)S(1)}, bf16[1024,256]{1,0:T(8,128)(2,1)S(1)}, u32[]{:S(2)}, u32[]{:S(2)}) collective-permute-start(bf16[1024,256]{1,0:T(8,128)(2,1)S(1)} %subtract_convert_fusion.5), channel_id=1, source_target_pairs={{0,6},{1,7},{2,4},{3,5},{4,2},{5,3},{6,0},{7,1},{8,14},{9,15},{10,... | collective-permute-start | bytes 1572872 | tf_op jit(solution)/shard_map/ppermute | solution.py:14
  44.4 1.6 %collective-permute-done.3 = bf16[512,256]{1,0:T(8,128)(2,1)S(1)} collective-permute-done((bf16[512,256]{1,0:T(8,128)(2,1)S(1)}, bf16[512,256]{1,0:T(8,128)(2,1)S(1)}, u32[]{:S(2)}, u32[]{:S(2)}) %collective-permute-start.3) | collective-permute-done | bytes 262176 | tf_op jit(solution)/shard_map/ppermute | solution.py:14
  48.2 16.9 %collective-permute-done.4 = bf16[1024,256]{1,0:T(8,128)(2,1)S(1)} collective-permute-done((bf16[1024,256]{1,0:T(8,128)(2,1)S(1)}, bf16[1024,256]{1,0:T(8,128)(2,1)S(1)}, u32[]{:S(2)}, u32[]{:S(2)}) %collective-permute-start.4) | collective-permute-done | bytes 524320 | tf_op jit(solution)/shard_map/ppermute | solution.py:14
  67.4 0.8 fusion.2
  69.5 1.3 %collective-permute-start.5 = (bf16[512,256]{1,0:T(8,128)(2,1)S(1)}, bf16[512,256]{1,0:T(8,128)(2,1)S(1)}, u32[]{:S(2)}, u32[]{:S(2)}) collective-permute-start(bf16[512,256]{1,0:T(8,128)(2,1)S(1)} %fusion.31), channel_id=1, source_target_pairs={{0,8},{1,9},{2,10},{3,11},{4,12},{5,13},{6,14},{7,15},{8,0},{9,1},... | collective-permute-start | bytes 786440 | tf_op jit(solution)/shard_map/ppermute | solution.py:14
  71.6 3.9 %collective-permute-done.5 = bf16[512,256]{1,0:T(8,128)(2,1)S(1)} collective-permute-done((bf16[512,256]{1,0:T(8,128)(2,1)S(1)}, bf16[512,256]{1,0:T(8,128)(2,1)S(1)}, u32[]{:S(2)}, u32[]{:S(2)}) %collective-permute-start.5) | collective-permute-done | bytes 262176 | tf_op jit(solution)/shard_map/ppermute | solution.py:14
  78.3 1.4 %collective-permute-start.7 = (bf16[512,256]{1,0:T(8,128)(2,1)S(1)}, bf16[512,256]{1,0:T(8,128)(2,1)}, u32[]{:S(2)}, u32[]{:S(2)}) collective-permute-start(bf16[512,256]{1,0:T(8,128)(2,1)S(1)} %fusion.27), channel_id=1, source_target_pairs={{0,8},{1,9},{2,10},{3,11},{4,12},{5,13},{6,14},{7,15},{8,0},{9,1},... | collective-permute-start | bytes 786440 | tf_op jit(solution)/shard_map/ppermute | solution.py:14
  80.4 14.7 %all-to-all-start = ((bf16[256,2,128]{2,1,0:T(2,128)(2,1)}), bf16[256,2,128]{2,1,0:T(2,128)(2,1)S(1)}, u32[]{:S(2)}, u32[]{:S(2)}) async-start(bf16[256,2,128]{2,1,0:T(2,128)(2,1)} %reshape.45), calls=%async_computation | async-start | bytes 262144 | tf_op jit(solution)/shard_map/all_to_all | solution.py:24
  95.6 1.7 %collective-permute-start.8 = (bf16[1024,256]{1,0:T(8,128)(2,1)S(1)}, bf16[1024,256]{1,0:T(8,128)(2,1)S(1)}, u32[]{:S(2)}, u32[]{:S(2)}) collective-permute-start(bf16[1024,256]{1,0:T(8,128)(2,1)S(1)} %subtract_convert_fusion), channel_id=1, source_target_pairs={{0,8},{1,9},{2,10},{3,11},{4,12},{5,13},{6,14},{7,15},{8,0},{9,1},... | collective-permute-start | bytes 1572872 | tf_op jit(solution)/shard_map/ppermute | solution.py:14
  97.2 10.8 %all-to-all-done = bf16[256,2,128]{2,1,0:T(2,128)(2,1)S(1)} async-done(((bf16[256,2,128]{2,1,0:T(2,128)(2,1)}), bf16[256,2,128]{2,1,0:T(2,128)(2,1)S(1)}, u32[]{:S(2)}, u32[]{:S(2)}) %all-to-all-start) | async-done | bytes 131104 | tf_op jit(solution)/shard_map/all_to_all | solution.py:24
  109.1 5.5 %all-to-all-start.1 = ((bf16[256,2,128]{2,1,0:T(2,128)(2,1)}), bf16[256,2,128]{2,1,0:T(2,128)(2,1)S(1)}, u32[]{:S(2)}, u32[]{:S(2)}) async-start(bf16[256,2,128]{2,1,0:T(2,128)(2,1)} %broadcast_in_dim.7), calls=%async_computation.1 | async-start | bytes 262144 | tf_op jit(solution)/shard_map/all_to_all | solution.py:27
  114.6 1.8 %fusion = f32[1024,256]{1,0:T(8,128)S(1)} fusion(bf16[512,256]{1,0:T(8,128)(2,1)} %collective-permute-done.7, s32[512]{0:T(512)S(1)} %bitcast.76), kind=kOutput, calls=%fused_computation.4 | convolution fusion | flops 268959744 | bytes 1312768 | tf_op jit(solution)/shard_map/dot_general | solution.py:18
  116.7 1.2 fusion.23
  117.9 9.8 %all-to-all-done.1 = bf16[256,2,128]{2,1,0:T(2,128)(2,1)S(1)} async-done(((bf16[256,2,128]{2,1,0:T(2,128)(2,1)}), bf16[256,2,128]{2,1,0:T(2,128)(2,1)S(1)}, u32[]{:S(2)}, u32[]{:S(2)}) %all-to-all-start.1) | async-done | bytes 131104 | tf_op jit(solution)/shard_map/all_to_all | solution.py:27
  (59 shorter events, 22.0 us)
Async XLA Ops:
  0.6 13.5 %collective-permute-start = (bf16[1024,256]{1,0:T(8,128)(2,1)}, bf16[1024,256]{1,0:T(8,128)(2,1)S(1)}, u32[]{:S(2)}, u32[]{:S(2)}) collective-permute-start(bf16[1024,256]{1,0:T(8,128)(2,1)} %param.7), channel_id=1, source_target_pairs={{0,1},{1,0},{2,3},{3,2},{4,5},{5,4},{6,7},{7,6},{8,9},{9,8},{10,11... | collective-permute-start | bytes 1572872 | tf_op jit(solution)/shard_map/ppermute | solution.py:14
  6.4 7.7 %collective-permute-start.2 = (s32[512]{0:T(512)S(1)}, s32[512]{0:T(512)S(1)}, u32[]{:S(2)}, u32[]{:S(2)}) collective-permute-start(s32[512]{0:T(512)S(1)} %bitcast.84), channel_id=1, source_target_pairs={{0,2},{1,3},{2,0},{3,1},{4,6},{5,7},{6,4},{7,5},{8,10},{9,11},{10,... | collective-permute-start | bytes 6152 | tf_op jit(solution)/shard_map/ppermute | solution.py:14
  9.4 4.7 %collective-permute-start.6 = (s32[512]{0:T(512)S(1)}, s32[512]{0:T(512)S(1)}, u32[]{:S(2)}, u32[]{:S(2)}) collective-permute-start(s32[512]{0:T(512)S(1)} %bitcast.83), channel_id=1, source_target_pairs={{0,8},{1,9},{2,10},{3,11},{4,12},{5,13},{6,14},{7,15},{8,0},{9,1},... | collective-permute-start | bytes 6152 | tf_op jit(solution)/shard_map/ppermute | solution.py:14
  16.0 1.3 %copy-start = (bf16[256,256]{1,0:T(8,128)(2,1)S(1)}, bf16[256,256]{1,0:T(8,128)(2,1)}, u32[]{:S(2)}) copy-start(bf16[256,256]{1,0:T(8,128)(2,1)} %param.8) | copy-start | bytes 393220
  16.5 1.2 copy-start.1
  18.5 14.8 %collective-permute-start.1 = (bf16[512,256]{1,0:T(8,128)(2,1)S(1)}, bf16[512,256]{1,0:T(8,128)(2,1)S(1)}, u32[]{:S(2)}, u32[]{:S(2)}) collective-permute-start(bf16[512,256]{1,0:T(8,128)(2,1)S(1)} %fusion.29), channel_id=1, source_target_pairs={{0,2},{1,3},{2,0},{3,1},{4,6},{5,7},{6,4},{7,5},{8,10},{9,11},{10,... | collective-permute-start | bytes 786440 | tf_op jit(solution)/shard_map/ppermute | solution.py:14
  36.4 9.6 %collective-permute-start.3 = (bf16[512,256]{1,0:T(8,128)(2,1)S(1)}, bf16[512,256]{1,0:T(8,128)(2,1)S(1)}, u32[]{:S(2)}, u32[]{:S(2)}) collective-permute-start(bf16[512,256]{1,0:T(8,128)(2,1)S(1)} %fusion.25), channel_id=1, source_target_pairs={{0,2},{1,3},{2,0},{3,1},{4,6},{5,7},{6,4},{7,5},{8,10},{9,11},{10,... | collective-permute-start | bytes 786440 | tf_op jit(solution)/shard_map/ppermute | solution.py:14
  36.7 28.4 %collective-permute-start.4 = (bf16[1024,256]{1,0:T(8,128)(2,1)S(1)}, bf16[1024,256]{1,0:T(8,128)(2,1)S(1)}, u32[]{:S(2)}, u32[]{:S(2)}) collective-permute-start(bf16[1024,256]{1,0:T(8,128)(2,1)S(1)} %subtract_convert_fusion.5), channel_id=1, source_target_pairs={{0,6},{1,7},{2,4},{3,5},{4,2},{5,3},{6,0},{7,1},{8,14},{9,15},{10,... | collective-permute-start | bytes 1572872 | tf_op jit(solution)/shard_map/ppermute | solution.py:14
  69.5 6.0 %collective-permute-start.5 = (bf16[512,256]{1,0:T(8,128)(2,1)S(1)}, bf16[512,256]{1,0:T(8,128)(2,1)S(1)}, u32[]{:S(2)}, u32[]{:S(2)}) collective-permute-start(bf16[512,256]{1,0:T(8,128)(2,1)S(1)} %fusion.31), channel_id=1, source_target_pairs={{0,8},{1,9},{2,10},{3,11},{4,12},{5,13},{6,14},{7,15},{8,0},{9,1},... | collective-permute-start | bytes 786440 | tf_op jit(solution)/shard_map/ppermute | solution.py:14
  78.3 36.3 %collective-permute-start.7 = (bf16[512,256]{1,0:T(8,128)(2,1)S(1)}, bf16[512,256]{1,0:T(8,128)(2,1)}, u32[]{:S(2)}, u32[]{:S(2)}) collective-permute-start(bf16[512,256]{1,0:T(8,128)(2,1)S(1)} %fusion.27), channel_id=1, source_target_pairs={{0,8},{1,9},{2,10},{3,11},{4,12},{5,13},{6,14},{7,15},{8,0},{9,1},... | collective-permute-start | bytes 786440 | tf_op jit(solution)/shard_map/ppermute | solution.py:14
  80.4 27.7 %all-to-all-start = ((bf16[256,2,128]{2,1,0:T(2,128)(2,1)}), bf16[256,2,128]{2,1,0:T(2,128)(2,1)S(1)}, u32[]{:S(2)}, u32[]{:S(2)}) async-start(bf16[256,2,128]{2,1,0:T(2,128)(2,1)} %reshape.45), calls=%async_computation | async-start | bytes 262144 | tf_op jit(solution)/shard_map/all_to_all | solution.py:24
  95.6 33.1 %collective-permute-start.8 = (bf16[1024,256]{1,0:T(8,128)(2,1)S(1)}, bf16[1024,256]{1,0:T(8,128)(2,1)S(1)}, u32[]{:S(2)}, u32[]{:S(2)}) collective-permute-start(bf16[1024,256]{1,0:T(8,128)(2,1)S(1)} %subtract_convert_fusion), channel_id=1, source_target_pairs={{0,8},{1,9},{2,10},{3,11},{4,12},{5,13},{6,14},{7,15},{8,0},{9,1},... | collective-permute-start | bytes 1572872 | tf_op jit(solution)/shard_map/ppermute | solution.py:14
  109.1 18.7 %all-to-all-start.1 = ((bf16[256,2,128]{2,1,0:T(2,128)(2,1)}), bf16[256,2,128]{2,1,0:T(2,128)(2,1)S(1)}, u32[]{:S(2)}, u32[]{:S(2)}) async-start(bf16[256,2,128]{2,1,0:T(2,128)(2,1)} %broadcast_in_dim.7), calls=%async_computation.1 | async-start | bytes 262144 | tf_op jit(solution)/shard_map/all_to_all | solution.py:27

commit v3 on v2

v3 whole, which is shorter than its diff:
```python
import functools
import jax
import jax.numpy as jnp
from jax import lax
from jax.experimental import pallas as pl
from jax.experimental.pallas import tpu as pltpu
from jax.sharding import PartitionSpec as P

SCORE_SCALE = 0.1875
LR_EMBED = 0.5
LR_RELATION = 0.02
EXP_SCALE = SCORE_SCALE * 1.4426950408889634
CODE_ROWS = 16
AXES = ("group", "inner")
VM = pltpu.VMEM
TE = 256


def dot(a, b, dims):
    return lax.dot_general(a, b, (dims, ((), ())), preferred_element_type=jnp.float32)


RC = 64


def fill_coeffs(queries, held_ref, target_ref, first, coeffs_ref, scores_ref):
    rows = held_ref.shape[0]
    edges = queries.shape[0]
    parts = [slice(start, start + TE) for start in range(0, edges, TE)]
    chunks = [slice(start, start + RC) for start in range(0, rows, RC)]
    fold = lambda value, op: functools.reduce(op, [value[k:k + 8] for k in range(0, value.shape[0], 8)])
    for part in parts:
        scores_ref[:, part] = dot(held_ref[...], queries[part], ((1,), (1,)))
    for part in parts:
        top = functools.reduce(jnp.maximum, [fold(scores_ref[c, part], jnp.maximum) for c in chunks])
        top = jnp.max(top, axis=0, keepdims=True)
        total = None
        for c in chunks:
            expos = jnp.exp2((scores_ref[c, part] - top) * EXP_SCALE)
            scores_ref[c, part] = expos
            folded = fold(expos, jnp.add)
            total = folded if total is None else total + folded
        high, low = first + part.start // TE, first + (edges + part.start) // TE
        target = target_ref[high:high + 1, :].astype(jnp.float32) * 32.0 + target_ref[low:low + 1, :].astype(jnp.float32)
        live = (target >= 0.0).astype(jnp.float32)
        weight = live / jnp.sum(total, axis=0, keepdims=True)
        ids = lax.broadcasted_iota(jnp.int32, (RC, TE), 0).astype(jnp.float32)
        for c in chunks:
            softmax_w = scores_ref[c, part] * weight
            coeffs = jnp.where(ids == target - float(c.start), softmax_w - 1.0, softmax_w)
            coeffs_ref[c, part] = coeffs.astype(jnp.bfloat16)


def gradient_of_queries(coeffs_ref, held_ref):
    return (dot(coeffs_ref[...], held_ref[...], ((0,), (0,))) * SCORE_SCALE).astype(jnp.bfloat16)


def local_kernel(meeting, queries_ref, held_ref, codes_ref, relation_ref, same_ref, base_ref, coeffs_ref, grad_ref, next_ref, scores_ref):
    edges = queries_ref.shape[0]
    fill_coeffs(queries_ref[...], held_ref, codes_ref, CODE_ROWS * meeting, coeffs_ref, scores_ref)
    grad = gradient_of_queries(coeffs_ref, held_ref)
    grad_ref[...] = grad
    row_grad = dot(grad, relation_ref[...], ((1,), (1,)))
    high = row_grad.astype(jnp.bfloat16)
    low = (row_grad - high.astype(jnp.float32)).astype(jnp.bfloat16)
    summed = dot(same_ref[...], high, ((1,), (0,))) + dot(same_ref[...], low, ((1,), (0,)))
    next_ref[edges:, :] = codes_ref[CODE_ROWS * (meeting + 1):CODE_ROWS * (meeting + 2), :]
    next_ref[:edges, :] = (base_ref[...].astype(jnp.float32) - LR_EMBED * summed).astype(jnp.bfloat16)


def held_kernel(picked_ref, held_ref, relation_ref, new_ref, coeffs_ref, scores_ref):
    edges = coeffs_ref.shape[1]
    queries = dot(picked_ref[:edges, :], relation_ref[...], ((1,), (0,))).astype(jnp.bfloat16)
    fill_coeffs(queries, held_ref, picked_ref, edges, coeffs_ref, scores_ref)
    held_grad = dot(coeffs_ref[...], queries, ((1,), (0,)))
    new_ref[...] = (held_ref[...].astype(jnp.float32) - (LR_EMBED * SCORE_SCALE) * held_grad).astype(jnp.bfloat16)


def last_kernel(picked_ref, held_ref, relation_ref, before_ref, pieces_ref, coeffs_ref, grad_ref, queries_ref, scores_ref):
    edges = coeffs_ref.shape[1]
    picked = picked_ref[:edges, :]
    queries = dot(picked, relation_ref[...], ((1,), (0,))).astype(jnp.bfloat16)
    queries_ref[...] = queries
    fill_coeffs(queries, held_ref, picked_ref, edges, coeffs_ref, scores_ref)
    grad = gradient_of_queries(coeffs_ref, held_ref)
    grad_ref[...] = grad
    total = before_ref[...] + dot(picked, grad, ((0,), (0,)))
    half = total.shape[1] // 2
    pieces_ref[:total.shape[0], :] = total[:, :half].astype(jnp.bfloat16)
    pieces_ref[total.shape[0]:, :] = total[:, half:].astype(jnp.bfloat16)


def sum_kernel(pieces_ref, copies_ref):
    pairs = [pieces_ref[k:k + 64, :].astype(jnp.float32) for k in range(0, pieces_ref.shape[0], 64)]
    total = functools.reduce(jnp.add, pairs)
    total = functools.reduce(jnp.add, [total[k:k + 8] for k in range(0, 64, 8)])
    first = total[0:1] + total[2:3] + total[4:5] + total[6:7]
    second = total[1:2] + total[3:4] + total[5:6] + total[7:8]
    parity = lax.broadcasted_iota(jnp.int32, (16, total.shape[1]), 0) % 2
    tile = jnp.where(parity == 0, first, second).astype(jnp.bfloat16)
    for k in range(0, copies_ref.shape[0], 16):
        copies_ref[k:k + 16, :] = tile


def finish_kernel(gathered_ref, relation_ref, out_ref):
    rows, width = out_ref.shape
    half = width // 2
    for k in range(2):
        columns = slice(k * half, (k + 1) * half)
        total = gathered_ref[k * rows:(k + 1) * rows, :].astype(jnp.float32)
        out_ref[:, columns] = relation_ref[:, columns].astype(jnp.float32) - LR_RELATION * total


def copy_kernel(source_ref, out_ref):
    out_ref[...] = source_ref[...]


def call(kernel, outs, *args, scratch=()):
    spec = pl.BlockSpec(memory_space=VM)
    return pl.pallas_call(
        kernel,
        out_shape=outs,
        in_specs=[spec] * len(args),
        out_specs=jax.tree.map(lambda _: spec, outs),
        scratch_shapes=list(scratch),
        compiler_params=pltpu.CompilerParams(vmem_limit_bytes=16 << 20),
    )(*args)


def vmem(*shape):
    return VM(shape, jnp.bfloat16)


def local_meeting(meeting, queries, held, codes, relation, same, base):
    (edges, width), rows = queries.shape, held.shape[0]
    outs = (vmem(rows, edges), vmem(edges, width), vmem(edges + CODE_ROWS, width))
    scratch = [VM((rows, edges), jnp.float32)]
    return call(functools.partial(local_kernel, meeting), outs, queries, held, codes, relation, same, base, scratch=scratch)


def held_meeting(picked, held, relation, edges):
    rows, width = held.shape
    outs = (vmem(rows, width), vmem(rows, edges))
    return call(held_kernel, outs, picked, held, relation, scratch=[VM((rows, edges), jnp.float32)])


def last_meeting(picked, held, relation, before, edges):
    rows, width = held.shape
    outs = (vmem(2 * width, width // 2), vmem(rows, edges), vmem(edges, width), vmem(edges, width))
    scratch = [VM((rows, edges), jnp.float32)]
    return call(last_kernel, outs, picked, held, relation, before, scratch=scratch)


def shared_sums(pieces):
    devices = lax.axis_size(AXES)
    rows, lanes = pieces.shape
    shape = (devices, rows // devices, lanes)
    pieces = lax.all_to_all(pieces.reshape(shape), AXES, 0, 0).reshape(rows, lanes)
    copies = call(sum_kernel, vmem(rows, lanes), pieces)
    return lax.all_to_all(copies.reshape(shape), AXES, 0, 0).reshape(rows, lanes)


def moved(value, mask):
    pairs = [(source, source ^ mask) for source in range(lax.axis_size("inner"))]
    return lax.ppermute(value, "inner", pairs)


def source_table(src_row, rows):
    return (src_row[:, None] == jnp.arange(rows, dtype=jnp.int32)[None, :]).astype(jnp.bfloat16)


def same_source(rows, columns):
    return (rows[:, None] == columns[None, :]).astype(jnp.bfloat16)


def picked_rows(left_block, table):
    return dot(table, left_block, ((1,), (0,))).astype(jnp.bfloat16)


def queries_of(picked, relation):
    return dot(picked, relation, ((1,), (0,))).astype(jnp.bfloat16)


def updated_holding(holding, coeffs, queries):
    held_grad = dot(coeffs, queries, ((1,), (0,)))
    return (holding.astype(jnp.float32) - (LR_EMBED * SCORE_SCALE) * held_grad).astype(jnp.bfloat16)


def query_gradient(coeffs, holding):
    return (dot(coeffs, holding, ((0,), (0,))) * SCORE_SCALE).astype(jnp.bfloat16)


def relation_gradient(picked, query_grad):
    return dot(picked, query_grad, ((0,), (0,)))


def updated_left(left_block, table, query_grad, relation):
    summed_rows = dot(table, query_grad, ((0,), (0,)))
    high = summed_rows.astype(jnp.bfloat16)
    low = (summed_rows - high.astype(jnp.float32)).astype(jnp.bfloat16)
    left_grad = dot(high, relation, ((1,), (1,))) + dot(low, relation, ((1,), (1,)))
    return (left_block.astype(jnp.float32) - LR_EMBED * left_grad).astype(jnp.bfloat16)


def coded(targets):
    meetings = targets.shape[0]
    lines = jnp.concatenate([targets // 32, targets % 32], axis=1).astype(jnp.bfloat16)
    lines = lines.reshape(meetings, -1, TE)
    lines = jnp.pad(lines, ((0, 0), (0, CODE_ROWS - lines.shape[1]), (0, 0)))
    return lines.reshape(meetings * CODE_ROWS, TE)


def shards(left_part, right_part, relation, src_index, dst_index, lengths):
    rows = left_part.shape[0]
    edges = src_index.shape[2]
    sources = src_index[0]

    held = moved(right_part, 1)
    slots = jnp.arange(edges, dtype=jnp.int32)
    targets = jnp.where(slots[None, :] < lengths[0][:, None], dst_index[0], -1)
    codes = coded(targets)
    tables = [source_table(sources[meeting], rows) for meeting in range(4)]
    picked0 = picked_rows(left_part, tables[0])
    queries0 = queries_of(picked0, relation)
    base = picked_rows(left_part, tables[1])
    same = same_source(sources[1], sources[0])
    coeffs, query_grad, picked1 = local_meeting(0, queries0, held, codes, relation, same, base)

    rows1 = moved(picked1, 2)
    held = updated_holding(held, coeffs, queries0)
    left = updated_left(left_part, tables[0], query_grad, relation)
    relation_grad = relation_gradient(picked0, query_grad)
    new_held, coeffs = held_meeting(rows1, held, relation, edges)
    arriving = moved(new_held, 6)
    query_grad = query_gradient(coeffs, held)
    relation_grad = relation_grad + relation_gradient(rows1[:edges], query_grad)
    left = updated_left(left, tables[1], moved(query_grad, 2), relation)

    held = arriving
    picked2 = picked_rows(left, tables[2])
    queries2 = queries_of(picked2, relation)
    base = picked_rows(left, tables[3])
    same = same_source(sources[3], sources[2])
    coeffs, query_grad, picked3 = local_meeting(2, queries2, held, codes, relation, same, base)

    rows3 = moved(picked3, 8)
    held = updated_holding(held, coeffs, queries2)
    left = updated_left(left, tables[2], query_grad, relation)
    relation_grad = relation_grad + relation_gradient(picked2, query_grad)
    pieces, coeffs, query_grad, queries3 = last_meeting(rows3, held, relation, relation_grad, edges)
    sums = shared_sums(pieces)
    held = moved(updated_holding(held, coeffs, queries3), 8)
    left = updated_left(left, tables[3], moved(query_grad, 8), relation)
    held = call(copy_kernel, jax.ShapeDtypeStruct(held.shape, held.dtype), held)
    relation, held, left = lax.optimization_barrier((relation, held, left))
    relation_out = call(finish_kernel, jax.ShapeDtypeStruct(relation.shape, jnp.float32), sums, relation)
    return (left, held, relation_out)


def solution(mesh):
    in_specs = (
        P(AXES, None),
        P(AXES, None),
        P(),
        P(AXES, None, None),
        P(AXES, None, None),
        P(AXES, None),
    )
    out_specs = (P(AXES, None), P(AXES, None), P())
    return jax.shard_map(shards, mesh=mesh, in_specs=in_specs, out_specs=out_specs, check_vma=False)
```

time: 130 us -> 125 us (0.962)
  Pallas kernels: 0 us -> 12.4 us
  other arithmetic: 7.26 us -> 1.09 us
  starting transfers between devices: 42.7 us -> 37.8 us
  matrix products: 19.6 us -> 14.7 us
    pallas_call x0 -> x7, Pallas kernels: none -> 12.4 us  [call(): pl.pallas_call(kernel, out_shape=outs, in_specs=[spec] * len(args), out_s...]
    ppermute x9 -> x7, starting transfers between devices: 22.5 us -> 17.4 us  [moved(): return lax.ppermute(value, 'inner', pairs)]
    dot_general x36 -> x25, matrix products: 19.6 us -> 14.7 us  [dot(): lax.dot_general(a, b, (dims, ((), ())), preferred_element_type=jnp.float32)]
    convert_element_type x8 -> x2, other arithmetic: 3.24 us -> 0.3 us  [same_source(): return (rows[:, None] == columns[None, :]).astype(jnp.bfloat16)]
    reduce_sum x5 -> x0, other arithmetic: 2.39 us -> none  [the longest x4 2.11 us: edge_coeffs(): softmax_w = expos / jnp.sum(expos, axis=1, keepdims=True)]
    ppermute x9 -> x7, waiting for transfers between devices: 35 us -> 35.9 us  [moved(): return lax.ppermute(value, 'inner', pairs)]
  transfers between devices with their start and end apart: 11 -> 9, of which waited for: 7 -> 7; matrix products, arithmetic and copies ran while one was open for 11% -> 14% of each run, Pallas kernels for 0% -> 1%
where the time goes in v3:
time: 125 us; the launch traced here: 124 us
  waiting for transfers between devices  55.3 us (44%)
  starting transfers between devices  37.8 us (30%)
  matrix products  14.7 us (12%)
  Pallas kernels  12.4 us (10%)
  local copies, waits for them, and re-layouts  2.02 us (2%)
    ppermute x7, waiting for transfers between devices, moved(): return lax.ppermute(value, 'inner', pairs)  35.9 us
    ppermute x7, starting transfers between devices, moved(): return lax.ppermute(value, 'inner', pairs)  17.4 us
    dot_general x25, matrix products, dot(): lax.dot_general(a, b, (dims, ((), ())), preferred_element_type=jnp.float32)  14.7 us
    all_to_all x1, starting transfers between devices, shared_sums(): lax.all_to_all(pieces.reshape(shape), AXES, 0, 0).reshape(rows, lanes)  14.6 us
    pallas_call x7, Pallas kernels, call(): pl.pallas_call(kernel, out_shape=outs, in_specs=[spec] * len(args), out_s...  12.4 us
    all_to_all x1, waiting for transfers between devices, shared_sums(): lax.all_to_all(pieces.reshape(shape), AXES, 0, 0).reshape(rows, lanes)  10.4 us
    all_to_all x1, waiting for transfers between devices, shared_sums(): lax.all_to_all(copies.reshape(shape), AXES, 0, 0).reshape(rows, lanes)  9.04 us
    all_to_all x1, starting transfers between devices, shared_sums(): lax.all_to_all(copies.reshape(shape), AXES, 0, 0).reshape(rows, lanes)  5.76 us
  transfers between devices with their start and end apart: 9, of which 7 were waited for; matrix products, arithmetic and copies ran while one was open for 14% of the time, Pallas kernels for 1%

profile of v3, /device:TPU:1, one launch (start us, length us, event | category | flops | bytes accessed | tf_op | source)
XLA Modules:
  0.0 124.2 jit_solution(3213895368041709819)
XLA Ops:
  0.6 2.5 %collective-permute-start = (bf16[1024,256]{1,0:T(8,128)(2,1)}, bf16[1024,256]{1,0:T(8,128)(2,1)S(1)}, u32[]{:S(2)}, u32[]{:S(2)}) collective-permute-start(bf16[1024,256]{1,0:T(8,128)(2,1)} %param.7), channel_id=1, source_target_pairs={{0,1},{1,0},{2,3},{3,2},{4,5},{5,4},{6,7},{7,6},{8,9},{9,8},{10,11... | collective-permute-start | bytes 1572872 | tf_op jit(solution)/shard_map/ppermute | solution.py:165
  3.2 0.9 fusion.55
  5.5 1.6 %fusion.23 = bf16[512,256]{1,0:T(8,128)(2,1)S(1)} fusion(bf16[1024,256]{1,0:T(8,128)(2,1)} %param.6, s32[512]{0:T(512)S(1)} %bitcast.56), kind=kOutput, calls=%fused_computation.35 | convolution fusion | flops 269090816 | bytes 788480 | tf_op jit(solution)/shard_map/dot_general | solution.py:20
  8.7 5.4 %collective-permute-done.held_ref = bf16[1024,256]{1,0:T(8,128)(2,1)S(1)} collective-permute-done((bf16[1024,256]{1,0:T(8,128)(2,1)}, bf16[1024,256]{1,0:T(8,128)(2,1)S(1)}, u32[]{:S(2)}, u32[]{:S(2)}) %collective-permute-start) | collective-permute-done | bytes 524320 | tf_op jit(solution)/shard_map/ppermute | solution.py:165
  14.1 2.7 %shard_map.85 = (bf16[1024,512]{1,0:T(8,128)(2,1)S(1)}, bf16[512,256]{1,0:T(8,128)(2,1)S(1)}, bf16[528,256]{1,0:T(8,128)(2,1)S(1)}) custom-call(bf16[512,256]{1,0:T(8,128)(2,1)S(1)} %convolution_convert_fusion.1.queries_ref, bf16[1024,256]{1,0:T(8,128)(2,1)S(1)} %collective-permute-done.held_ref, bf16[64,256]{1,0:T(8,128)(2,1)S(1)} %bitcast.45, ...), custom_call_target="tpu_custom_call" | custom-call | tf_op jit(solution)/shard_map/pallas_call | solution.py:120
  16.8 3.9 %collective-permute-start.1 = (bf16[528,256]{1,0:T(8,128)(2,1)S(1)}, bf16[528,256]{1,0:T(8,128)(2,1)S(1)}, u32[]{:S(2)}, u32[]{:S(2)}) collective-permute-start(bf16[528,256]{1,0:T(8,128)(2,1)S(1)} %get-tuple-element.18), channel_id=1, source_target_pairs={{0,2},{1,3},{2,0},{3,1},{4,6},{5,7},{6,4},{7,5},{8,10},{9,11},{10,... | collective-permute-start | bytes 811016 | tf_op jit(solution)/shard_map/ppermute | solution.py:165
  22.3 10.1 %collective-permute-done.1.picked_ref = bf16[528,256]{1,0:T(8,128)(2,1)S(1)} collective-permute-done((bf16[528,256]{1,0:T(8,128)(2,1)S(1)}, bf16[528,256]{1,0:T(8,128)(2,1)S(1)}, u32[]{:S(2)}, u32[]{:S(2)}) %collective-permute-start.1) | collective-permute-done | bytes 270368 | tf_op jit(solution)/shard_map/ppermute | solution.py:165
  32.4 1.9 %shard_map.86 = (bf16[1024,256]{1,0:T(8,128)(2,1)S(1)}, bf16[1024,512]{1,0:T(8,128)(2,1)S(1)}) custom-call(bf16[528,256]{1,0:T(8,128)(2,1)S(1)} %collective-permute-done.1.picked_ref, bf16[1024,256]{1,0:T(8,128)(2,1)S(1)} %subtract_convert_fusion.6.held_ref, bf16[256,256]{1,0:T(8,128)(2,1)S(1)} %copy-done), custom_call_target="tpu_custom_call" | custom-call | tf_op jit(solution)/shard_map/pallas_call | solution.py:120
  35.2 7.0 %collective-permute-start.2 = (bf16[1024,256]{1,0:T(8,128)(2,1)S(1)}, bf16[1024,256]{1,0:T(8,128)(2,1)S(1)}, u32[]{:S(2)}, u32[]{:S(2)}) collective-permute-start(bf16[1024,256]{1,0:T(8,128)(2,1)S(1)} %get-tuple-element.20), channel_id=1, source_target_pairs={{0,6},{1,7},{2,4},{3,5},{4,2},{5,3},{6,0},{7,1},{8,14},{9,15},{10,... | collective-permute-start | bytes 1572872 | tf_op jit(solution)/shard_map/ppermute | solution.py:165
  42.5 2.6 %collective-permute-done.3 = bf16[512,256]{1,0:T(8,128)(2,1)S(1)} collective-permute-done((bf16[512,256]{1,0:T(8,128)(2,1)S(1)}, bf16[512,256]{1,0:T(8,128)(2,1)S(1)}, u32[]{:S(2)}, u32[]{:S(2)}) %collective-permute-start.3) | collective-permute-done | bytes 262176 | tf_op jit(solution)/shard_map/ppermute | solution.py:165
  47.9 15.4 %collective-permute-done.2.held_ref = bf16[1024,256]{1,0:T(8,128)(2,1)S(1)} collective-permute-done((bf16[1024,256]{1,0:T(8,128)(2,1)S(1)}, bf16[1024,256]{1,0:T(8,128)(2,1)S(1)}, u32[]{:S(2)}, u32[]{:S(2)}) %collective-permute-start.2) | collective-permute-done | bytes 524320 | tf_op jit(solution)/shard_map/ppermute | solution.py:165
  63.2 2.7 %shard_map.87 = (bf16[1024,512]{1,0:T(8,128)(2,1)S(1)}, bf16[512,256]{1,0:T(8,128)(2,1)S(1)}, bf16[528,256]{1,0:T(8,128)(2,1)S(1)}) custom-call(bf16[512,256]{1,0:T(8,128)(2,1)S(1)} %convolution_convert_fusion.queries_ref, bf16[1024,256]{1,0:T(8,128)(2,1)S(1)} %collective-permute-done.2.held_ref, bf16[64,256]{1,0:T(8,128)(2,1)S(1)} %bitcast.46, ...), custom_call_target="tpu_custom_call" | custom-call | tf_op jit(solution)/shard_map/pallas_call | solution.py:120
  65.9 1.3 %collective-permute-start.4 = (bf16[528,256]{1,0:T(8,128)(2,1)S(1)}, bf16[528,256]{1,0:T(8,128)(2,1)S(1)}, u32[]{:S(2)}, u32[]{:S(2)}) collective-permute-start(bf16[528,256]{1,0:T(8,128)(2,1)S(1)} %get-tuple-element.24), channel_id=1, source_target_pairs={{0,8},{1,9},{2,10},{3,11},{4,12},{5,13},{6,14},{7,15},{8,0},{9,1},... | collective-permute-start | bytes 811016 | tf_op jit(solution)/shard_map/ppermute | solution.py:165
  69.7 2.4 %collective-permute-done.4.picked_ref = bf16[528,256]{1,0:T(8,128)(2,1)S(1)} collective-permute-done((bf16[528,256]{1,0:T(8,128)(2,1)S(1)}, bf16[528,256]{1,0:T(8,128)(2,1)S(1)}, u32[]{:S(2)}, u32[]{:S(2)}) %collective-permute-start.4) | collective-permute-done | bytes 270368 | tf_op jit(solution)/shard_map/ppermute | solution.py:165
  72.1 2.9 %shard_map.88 = (bf16[512,128]{1,0:T(8,128)(2,1)}, bf16[1024,512]{1,0:T(8,128)(2,1)S(1)}, bf16[512,256]{1,0:T(8,128)(2,1)S(1)}, bf16[512,256]{1,0:T(8,128)(2,1)S(1)}) custom-call(bf16[528,256]{1,0:T(8,128)(2,1)S(1)} %collective-permute-done.4.picked_ref, bf16[1024,256]{1,0:T(8,128)(2,1)S(1)} %subtract_convert_fusion.3.held_ref, ...), custom_call_target="tpu_custom_call" | custom-call | tf_op jit(solution)/shard_map/pallas_call | solution.py:120
  75.0 1.2 %collective-permute-start.6 = (bf16[512,256]{1,0:T(8,128)(2,1)S(1)}, bf16[512,256]{1,0:T(8,128)(2,1)}, u32[]{:S(2)}, u32[]{:S(2)}) collective-permute-start(bf16[512,256]{1,0:T(8,128)(2,1)S(1)} %get-tuple-element.28), channel_id=1, source_target_pairs={{0,8},{1,9},{2,10},{3,11},{4,12},{5,13},{6,14},{7,15},{8,0},{9,1},... | collective-permute-start | bytes 786440 | tf_op jit(solution)/shard_map/ppermute | solution.py:165
  76.2 14.6 %all-to-all-start = ((bf16[256,2,128]{2,1,0:T(2,128)(2,1)}), bf16[256,2,128]{2,1,0:T(2,128)(2,1)S(1)}, u32[]{:S(2)}, u32[]{:S(2)}) async-start(bf16[256,2,128]{2,1,0:T(2,128)(2,1)} %bitcast.6), calls=%async_computation | async-start | bytes 262144 | tf_op jit(solution)/shard_map/all_to_all | solution.py:158
  90.8 1.2 subtract_convert_fusion.2
  92.1 1.4 %collective-permute-start.5 = (bf16[1024,256]{1,0:T(8,128)(2,1)}, bf16[1024,256]{1,0:T(8,128)(2,1)S(1)}, u32[]{:S(2)}, u32[]{:S(2)}) collective-permute-start(bf16[1024,256]{1,0:T(8,128)(2,1)} %subtract_convert_fusion.2), channel_id=1, source_target_pairs={{0,8},{1,9},{2,10},{3,11},{4,12},{5,13},{6,14},{7,15},{8,0},{9,1},... | collective-permute-start | bytes 1572872 | tf_op jit(solution)/shard_map/ppermute | solution.py:165
  93.4 10.4 %all-to-all-done = bf16[256,2,128]{2,1,0:T(2,128)(2,1)S(1)} async-done(((bf16[256,2,128]{2,1,0:T(2,128)(2,1)}), bf16[256,2,128]{2,1,0:T(2,128)(2,1)S(1)}, u32[]{:S(2)}, u32[]{:S(2)}) %all-to-all-start) | async-done | bytes 131104 | tf_op jit(solution)/shard_map/all_to_all | solution.py:158
  104.5 5.8 %all-to-all-start.1 = ((bf16[256,2,128]{2,1,0:T(2,128)(2,1)}), bf16[256,2,128]{2,1,0:T(2,128)(2,1)S(1)}, u32[]{:S(2)}, u32[]{:S(2)}) async-start(bf16[256,2,128]{2,1,0:T(2,128)(2,1)} %bitcast.8), calls=%async_computation.1 | async-start | bytes 262144 | tf_op jit(solution)/shard_map/all_to_all | solution.py:160
  110.3 1.8 %fusion = f32[1024,256]{1,0:T(8,128)S(1)} fusion(bf16[512,256]{1,0:T(8,128)(2,1)} %collective-permute-done.6, s32[512]{0:T(512)S(1)} %bitcast.49), kind=kOutput, calls=%fused_computation.1 | convolution fusion | flops 268959744 | bytes 1312768 | tf_op jit(solution)/shard_map/dot_general | solution.py:20
  112.4 1.1 fusion.21
  114.4 9.0 %all-to-all-done.1 = bf16[256,2,128]{2,1,0:T(2,128)(2,1)S(1)} async-done(((bf16[256,2,128]{2,1,0:T(2,128)(2,1)}), bf16[256,2,128]{2,1,0:T(2,128)(2,1)S(1)}, u32[]{:S(2)}, u32[]{:S(2)}) %all-to-all-start.1) | async-done | bytes 131104 | tf_op jit(solution)/shard_map/all_to_all | solution.py:160
  (38 shorter events, 13.5 us)
Async XLA Ops:
  0.6 13.5 %collective-permute-start = (bf16[1024,256]{1,0:T(8,128)(2,1)}, bf16[1024,256]{1,0:T(8,128)(2,1)S(1)}, u32[]{:S(2)}, u32[]{:S(2)}) collective-permute-start(bf16[1024,256]{1,0:T(8,128)(2,1)} %param.7), channel_id=1, source_target_pairs={{0,1},{1,0},{2,3},{3,2},{4,5},{5,4},{6,7},{7,6},{8,9},{9,8},{10,11... | collective-permute-start | bytes 1572872 | tf_op jit(solution)/shard_map/ppermute | solution.py:165
  5.5 2.0 %copy-start = (bf16[256,256]{1,0:T(8,128)(2,1)S(1)}, bf16[256,256]{1,0:T(8,128)(2,1)}, u32[]{:S(2)}) copy-start(bf16[256,256]{1,0:T(8,128)(2,1)} %relation_ref.8) | copy-start | bytes 393220
  7.1 1.0 copy-start.1
  16.8 15.6 %collective-permute-start.1 = (bf16[528,256]{1,0:T(8,128)(2,1)S(1)}, bf16[528,256]{1,0:T(8,128)(2,1)S(1)}, u32[]{:S(2)}, u32[]{:S(2)}) collective-permute-start(bf16[528,256]{1,0:T(8,128)(2,1)S(1)} %get-tuple-element.18), channel_id=1, source_target_pairs={{0,2},{1,3},{2,0},{3,1},{4,6},{5,7},{6,4},{7,5},{8,10},{9,11},{10,... | collective-permute-start | bytes 811016 | tf_op jit(solution)/shard_map/ppermute | solution.py:165
  34.8 10.3 %collective-permute-start.3 = (bf16[512,256]{1,0:T(8,128)(2,1)S(1)}, bf16[512,256]{1,0:T(8,128)(2,1)S(1)}, u32[]{:S(2)}, u32[]{:S(2)}) collective-permute-start(bf16[512,256]{1,0:T(8,128)(2,1)S(1)} %fusion.22), channel_id=1, source_target_pairs={{0,2},{1,3},{2,0},{3,1},{4,6},{5,7},{6,4},{7,5},{8,10},{9,11},{10,... | collective-permute-start | bytes 786440 | tf_op jit(solution)/shard_map/ppermute | solution.py:165
  35.2 28.0 %collective-permute-start.2 = (bf16[1024,256]{1,0:T(8,128)(2,1)S(1)}, bf16[1024,256]{1,0:T(8,128)(2,1)S(1)}, u32[]{:S(2)}, u32[]{:S(2)}) collective-permute-start(bf16[1024,256]{1,0:T(8,128)(2,1)S(1)} %get-tuple-element.20), channel_id=1, source_target_pairs={{0,6},{1,7},{2,4},{3,5},{4,2},{5,3},{6,0},{7,1},{8,14},{9,15},{10,... | collective-permute-start | bytes 1572872 | tf_op jit(solution)/shard_map/ppermute | solution.py:165
  65.9 6.2 %collective-permute-start.4 = (bf16[528,256]{1,0:T(8,128)(2,1)S(1)}, bf16[528,256]{1,0:T(8,128)(2,1)S(1)}, u32[]{:S(2)}, u32[]{:S(2)}) collective-permute-start(bf16[528,256]{1,0:T(8,128)(2,1)S(1)} %get-tuple-element.24), channel_id=1, source_target_pairs={{0,8},{1,9},{2,10},{3,11},{4,12},{5,13},{6,14},{7,15},{8,0},{9,1},... | collective-permute-start | bytes 811016 | tf_op jit(solution)/shard_map/ppermute | solution.py:165
  75.0 35.3 %collective-permute-start.6 = (bf16[512,256]{1,0:T(8,128)(2,1)S(1)}, bf16[512,256]{1,0:T(8,128)(2,1)}, u32[]{:S(2)}, u32[]{:S(2)}) collective-permute-start(bf16[512,256]{1,0:T(8,128)(2,1)S(1)} %get-tuple-element.28), channel_id=1, source_target_pairs={{0,8},{1,9},{2,10},{3,11},{4,12},{5,13},{6,14},{7,15},{8,0},{9,1},... | collective-permute-start | bytes 786440 | tf_op jit(solution)/shard_map/ppermute | solution.py:165
  76.2 27.6 %all-to-all-start = ((bf16[256,2,128]{2,1,0:T(2,128)(2,1)}), bf16[256,2,128]{2,1,0:T(2,128)(2,1)S(1)}, u32[]{:S(2)}, u32[]{:S(2)}) async-start(bf16[256,2,128]{2,1,0:T(2,128)(2,1)} %bitcast.6), calls=%async_computation | async-start | bytes 262144 | tf_op jit(solution)/shard_map/all_to_all | solution.py:158
  92.1 21.5 %collective-permute-start.5 = (bf16[1024,256]{1,0:T(8,128)(2,1)}, bf16[1024,256]{1,0:T(8,128)(2,1)S(1)}, u32[]{:S(2)}, u32[]{:S(2)}) collective-permute-start(bf16[1024,256]{1,0:T(8,128)(2,1)} %subtract_convert_fusion.2), channel_id=1, source_target_pairs={{0,8},{1,9},{2,10},{3,11},{4,12},{5,13},{6,14},{7,15},{8,0},{9,1},... | collective-permute-start | bytes 1572872 | tf_op jit(solution)/shard_map/ppermute | solution.py:165
  104.5 18.9 %all-to-all-start.1 = ((bf16[256,2,128]{2,1,0:T(2,128)(2,1)}), bf16[256,2,128]{2,1,0:T(2,128)(2,1)S(1)}, u32[]{:S(2)}, u32[]{:S(2)}) async-start(bf16[256,2,128]{2,1,0:T(2,128)(2,1)} %bitcast.8), calls=%async_computation.1 | async-start | bytes 262144 | tf_op jit(solution)/shard_map/all_to_all | solution.py:160

commit v4 on v3

--- a/solution.py
+++ b/solution.py
@@ -91,15 +91,11 @@
 
 
 def sum_kernel(pieces_ref, copies_ref):
-    pairs = [pieces_ref[k:k + 64, :].astype(jnp.float32) for k in range(0, pieces_ref.shape[0], 64)]
-    total = functools.reduce(jnp.add, pairs)
-    total = functools.reduce(jnp.add, [total[k:k + 8] for k in range(0, 64, 8)])
-    first = total[0:1] + total[2:3] + total[4:5] + total[6:7]
-    second = total[1:2] + total[3:4] + total[5:6] + total[7:8]
-    parity = lax.broadcasted_iota(jnp.int32, (16, total.shape[1]), 0) % 2
-    tile = jnp.where(parity == 0, first, second).astype(jnp.bfloat16)
-    for k in range(0, copies_ref.shape[0], 16):
-        copies_ref[k:k + 16, :] = tile
+    lines = CODE_ROWS
+    parts = [pieces_ref[k:k + lines, :].astype(jnp.float32) for k in range(0, pieces_ref.shape[0], lines)]
+    total = functools.reduce(jnp.add, parts).astype(jnp.bfloat16)
+    for k in range(0, copies_ref.shape[0], lines):
+        copies_ref[k:k + lines, :] = total
 
 
 def finish_kernel(gathered_ref, relation_ref, out_ref):
@@ -151,13 +147,23 @@
     return call(last_kernel, outs, picked, held, relation, before, scratch=scratch)
 
 
+def exchanged(pieces, axes, groups):
+    rows, lanes = pieces.shape
+    pieces = pieces.reshape(len(groups[0]), -1, lanes)
+    return lax.all_to_all(pieces, axes, 0, 0, axis_index_groups=groups).reshape(rows, lanes)
+
+
 def shared_sums(pieces):
-    devices = lax.axis_size(AXES)
+    n_group, n_inner = lax.axis_size("group"), lax.axis_size("inner")
+    depth = 8
+    columns = range(n_inner // depth)
+    planes = [[g * n_inner + x * depth + z for g in range(n_group) for x in columns] for z in range(depth)]
+    lines = [[x * depth + z for z in range(depth)] for x in columns]
     rows, lanes = pieces.shape
-    shape = (devices, rows // devices, lanes)
-    pieces = lax.all_to_all(pieces.reshape(shape), AXES, 0, 0).reshape(rows, lanes)
-    copies = call(sum_kernel, vmem(rows, lanes), pieces)
-    return lax.all_to_all(copies.reshape(shape), AXES, 0, 0).reshape(rows, lanes)
+    pieces = exchanged(pieces, AXES, planes)
+    copies = call(sum_kernel, vmem(depth * CODE_ROWS, lanes), pieces)
+    copies = call(sum_kernel, vmem(rows, lanes), exchanged(copies, "inner", lines))
+    return exchanged(copies, AXES, planes)
 
 
 def moved(value, mask):

time: 125 us -> 122 us (0.976)
  waiting for transfers between devices: 55.3 us -> 49.5 us
  matrix products: 14.7 us -> 16.2 us
    all_to_all x2 -> x3, waiting for transfers between devices: 19.4 us -> 13.2 us  [exchanged(): lax.all_to_all(pieces, axes, 0, 0, axis_index_groups=groups)]
    dot_general x25, matrix products: 14.7 us -> 16.2 us  [dot(): lax.dot_general(a, b, (dims, ((), ())), preferred_element_type=jnp.float32)]
    all_to_all x2 -> x3, starting transfers between devices: 20.3 us -> 21.2 us  [exchanged(): lax.all_to_all(pieces, axes, 0, 0, axis_index_groups=groups)]
    pallas_call x7 -> x8, Pallas kernels: 12.4 us -> 13 us  [call(): pl.pallas_call(kernel, out_shape=outs, in_specs=[spec] * len(args), out_s...]
  transfers between devices with their start and end apart: 9 -> 10, of which waited for: 7 -> 8; matrix products, arithmetic and copies ran while one was open for 14% -> 14% of each run, Pallas kernels for 1% -> 2%
where the time goes in v4:
time: 122 us; the launch traced here: 121 us
  waiting for transfers between devices  49.5 us (41%)
  starting transfers between devices  37.8 us (31%)
  matrix products  16.2 us (13%)
  Pallas kernels  13 us (11%)
  local copies, waits for them, and re-layouts  2.95 us (2%)
    ppermute x7, waiting for transfers between devices, moved(): return lax.ppermute(value, 'inner', pairs)  36.3 us
    all_to_all x3, starting transfers between devices, exchanged(): lax.all_to_all(pieces, axes, 0, 0, axis_index_groups=groups)  21.2 us
    ppermute x7, starting transfers between devices, moved(): return lax.ppermute(value, 'inner', pairs)  16.6 us
    dot_general x25, matrix products, dot(): lax.dot_general(a, b, (dims, ((), ())), preferred_element_type=jnp.float32)  16.2 us
    all_to_all x3, waiting for transfers between devices, exchanged(): lax.all_to_all(pieces, axes, 0, 0, axis_index_groups=groups)  13.2 us
    pallas_call x8, Pallas kernels, call(): pl.pallas_call(kernel, out_shape=outs, in_specs=[spec] * len(args), out_s...  13 us
  transfers between devices with their start and end apart: 10, of which 8 were waited for; matrix products, arithmetic and copies ran while one was open for 14% of the time, Pallas kernels for 2%

profile of v4, /device:TPU:1, one launch (start us, length us, event | category | flops | bytes accessed | tf_op | source)
XLA Modules:
  0.0 121.5 jit_solution(5736561725681375908)
XLA Ops:
  0.6 2.5 %collective-permute-start = (bf16[1024,256]{1,0:T(8,128)(2,1)}, bf16[1024,256]{1,0:T(8,128)(2,1)S(1)}, u32[]{:S(2)}, u32[]{:S(2)}) collective-permute-start(bf16[1024,256]{1,0:T(8,128)(2,1)} %param.7), channel_id=1, source_target_pairs={{0,1},{1,0},{2,3},{3,2},{4,5},{5,4},{6,7},{7,6},{8,9},{9,8},{10,11... | collective-permute-start | bytes 1572872 | tf_op jit(solution)/shard_map/ppermute | solution.py:171
  5.5 1.6 %fusion.23 = bf16[512,256]{1,0:T(8,128)(2,1)S(1)} fusion(bf16[1024,256]{1,0:T(8,128)(2,1)} %param.6, s32[512]{0:T(512)S(1)} %bitcast.59), kind=kOutput, calls=%fused_computation.35 | convolution fusion | flops 269090816 | bytes 788480 | tf_op jit(solution)/shard_map/dot_general | solution.py:20
  8.7 5.4 %collective-permute-done.held_ref = bf16[1024,256]{1,0:T(8,128)(2,1)S(1)} collective-permute-done((bf16[1024,256]{1,0:T(8,128)(2,1)}, bf16[1024,256]{1,0:T(8,128)(2,1)S(1)}, u32[]{:S(2)}, u32[]{:S(2)}) %collective-permute-start) | collective-permute-done | bytes 524320 | tf_op jit(solution)/shard_map/ppermute | solution.py:171
  14.1 2.7 %shard_map.85 = (bf16[1024,512]{1,0:T(8,128)(2,1)S(1)}, bf16[512,256]{1,0:T(8,128)(2,1)S(1)}, bf16[528,256]{1,0:T(8,128)(2,1)S(1)}) custom-call(bf16[512,256]{1,0:T(8,128)(2,1)S(1)} %convolution_convert_fusion.1.queries_ref, bf16[1024,256]{1,0:T(8,128)(2,1)S(1)} %collective-permute-done.held_ref, bf16[64,256]{1,0:T(8,128)(2,1)S(1)} %bitcast.47, ...), custom_call_target="tpu_custom_call" | custom-call | tf_op jit(solution)/shard_map/pallas_call | solution.py:116
  16.8 3.9 %collective-permute-start.1 = (bf16[528,256]{1,0:T(8,128)(2,1)S(1)}, bf16[528,256]{1,0:T(8,128)(2,1)S(1)}, u32[]{:S(2)}, u32[]{:S(2)}) collective-permute-start(bf16[528,256]{1,0:T(8,128)(2,1)S(1)} %get-tuple-element.18), channel_id=1, source_target_pairs={{0,2},{1,3},{2,0},{3,1},{4,6},{5,7},{6,4},{7,5},{8,10},{9,11},{10,... | collective-permute-start | bytes 811016 | tf_op jit(solution)/shard_map/ppermute | solution.py:171
  22.3 10.1 %collective-permute-done.1.picked_ref = bf16[528,256]{1,0:T(8,128)(2,1)S(1)} collective-permute-done((bf16[528,256]{1,0:T(8,128)(2,1)S(1)}, bf16[528,256]{1,0:T(8,128)(2,1)S(1)}, u32[]{:S(2)}, u32[]{:S(2)}) %collective-permute-start.1) | collective-permute-done | bytes 270368 | tf_op jit(solution)/shard_map/ppermute | solution.py:171
  32.4 1.9 %shard_map.86 = (bf16[1024,256]{1,0:T(8,128)(2,1)S(1)}, bf16[1024,512]{1,0:T(8,128)(2,1)S(1)}) custom-call(bf16[528,256]{1,0:T(8,128)(2,1)S(1)} %collective-permute-done.1.picked_ref, bf16[1024,256]{1,0:T(8,128)(2,1)S(1)} %subtract_convert_fusion.6.held_ref, bf16[256,256]{1,0:T(8,128)(2,1)S(1)} %copy-done), custom_call_target="tpu_custom_call" | custom-call | tf_op jit(solution)/shard_map/pallas_call | solution.py:116
  35.2 7.0 %collective-permute-start.2 = (bf16[1024,256]{1,0:T(8,128)(2,1)S(1)}, bf16[1024,256]{1,0:T(8,128)(2,1)S(1)}, u32[]{:S(2)}, u32[]{:S(2)}) collective-permute-start(bf16[1024,256]{1,0:T(8,128)(2,1)S(1)} %get-tuple-element.20), channel_id=1, source_target_pairs={{0,6},{1,7},{2,4},{3,5},{4,2},{5,3},{6,0},{7,1},{8,14},{9,15},{10,... | collective-permute-start | bytes 1572872 | tf_op jit(solution)/shard_map/ppermute | solution.py:171
  42.5 2.6 %collective-permute-done.3 = bf16[512,256]{1,0:T(8,128)(2,1)S(1)} collective-permute-done((bf16[512,256]{1,0:T(8,128)(2,1)S(1)}, bf16[512,256]{1,0:T(8,128)(2,1)S(1)}, u32[]{:S(2)}, u32[]{:S(2)}) %collective-permute-start.3) | collective-permute-done | bytes 262176 | tf_op jit(solution)/shard_map/ppermute | solution.py:171
  47.9 15.3 %collective-permute-done.2.held_ref = bf16[1024,256]{1,0:T(8,128)(2,1)S(1)} collective-permute-done((bf16[1024,256]{1,0:T(8,128)(2,1)S(1)}, bf16[1024,256]{1,0:T(8,128)(2,1)S(1)}, u32[]{:S(2)}, u32[]{:S(2)}) %collective-permute-start.2) | collective-permute-done | bytes 524320 | tf_op jit(solution)/shard_map/ppermute | solution.py:171
  63.2 2.7 %shard_map.87 = (bf16[1024,512]{1,0:T(8,128)(2,1)S(1)}, bf16[512,256]{1,0:T(8,128)(2,1)S(1)}, bf16[528,256]{1,0:T(8,128)(2,1)S(1)}) custom-call(bf16[512,256]{1,0:T(8,128)(2,1)S(1)} %convolution_convert_fusion.queries_ref, bf16[1024,256]{1,0:T(8,128)(2,1)S(1)} %collective-permute-done.2.held_ref, bf16[64,256]{1,0:T(8,128)(2,1)S(1)} %bitcast.48, ...), custom_call_target="tpu_custom_call" | custom-call | tf_op jit(solution)/shard_map/pallas_call | solution.py:116
  67.0 1.3 %collective-permute-start.4 = (bf16[528,256]{1,0:T(8,128)(2,1)S(1)}, bf16[528,256]{1,0:T(8,128)(2,1)S(1)}, u32[]{:S(2)}, u32[]{:S(2)}) collective-permute-start(bf16[528,256]{1,0:T(8,128)(2,1)S(1)} %get-tuple-element.24), channel_id=1, source_target_pairs={{0,8},{1,9},{2,10},{3,11},{4,12},{5,13},{6,14},{7,15},{8,0},{9,1},... | collective-permute-start | bytes 811016 | tf_op jit(solution)/shard_map/ppermute | solution.py:171
  69.0 1.3 %fusion.42 = f32[1024,256]{1,0:T(8,128)} fusion(bf16[256,256]{1,0:T(8,128)(2,1)S(1)} %copy-done, f32[1024,256]{1,0:T(8,128)S(1)} %fusion.2), kind=kOutput, calls=%fused_computation.66 | convolution fusion | flops 134479872 | bytes 2228224 | tf_op jit(solution)/shard_map/dot_general | solution.py:20
  70.4 2.8 %collective-permute-done.4.picked_ref = bf16[528,256]{1,0:T(8,128)(2,1)S(1)} collective-permute-done((bf16[528,256]{1,0:T(8,128)(2,1)S(1)}, bf16[528,256]{1,0:T(8,128)(2,1)S(1)}, u32[]{:S(2)}, u32[]{:S(2)}) %collective-permute-start.4) | collective-permute-done | bytes 270368 | tf_op jit(solution)/shard_map/ppermute | solution.py:171
  73.2 2.9 %shard_map.88 = (bf16[512,128]{1,0:T(8,128)(2,1)}, bf16[1024,512]{1,0:T(8,128)(2,1)S(1)}, bf16[512,256]{1,0:T(8,128)(2,1)S(1)}, bf16[512,256]{1,0:T(8,128)(2,1)S(1)}) custom-call(bf16[528,256]{1,0:T(8,128)(2,1)S(1)} %collective-permute-done.4.picked_ref, bf16[1024,256]{1,0:T(8,128)(2,1)S(1)} %subtract_convert_fusion.3.held_ref, ...), custom_call_target="tpu_custom_call" | custom-call | tf_op jit(solution)/shard_map/pallas_call | solution.py:116
  76.1 9.9 %all-to-all-start = ((bf16[32,16,128]{2,1,0:T(8,128)(2,1)}), bf16[32,16,128]{2,1,0:T(8,128)(2,1)S(1)}, u32[]{:S(2)}, u32[]{:S(2)}) async-start(bf16[32,16,128]{2,1,0:T(8,128)(2,1)} %bitcast.6), calls=%async_computation | async-start | bytes 262144 | tf_op jit(solution)/shard_map/all_to_all | solution.py:153
  86.0 2.7 %fusion.20 = f32[1024,256]{1,0:T(8,128)} fusion(f32[1024,256]{1,0:T(8,128)} %fusion.42, bf16[256,256]{1,0:T(8,128)(2,1)S(1)} %copy-done, bf16[1024,256]{1,0:T(8,128)(2,1)} %copy-done.2, f32[1024,256]{1,0:T(8,128)S(1)} %fusion.2), kind=kOutput, calls=%fused_computation.31 | convolution fusion | flops 136839168 | bytes 3801088 | tf_op jit(solution)/shard_map/dot_general | solution.py:20
  88.7 1.3 %collective-permute-start.6 = (bf16[512,256]{1,0:T(8,128)(2,1)S(1)}, bf16[512,256]{1,0:T(8,128)(2,1)S(1)}, u32[]{:S(2)}, u32[]{:S(2)}) collective-permute-start(bf16[512,256]{1,0:T(8,128)(2,1)S(1)} %get-tuple-element.28), channel_id=1, source_target_pairs={{0,8},{1,9},{2,10},{3,11},{4,12},{5,13},{6,14},{7,15},{8,0},{9,1},... | collective-permute-start | bytes 786440 | tf_op jit(solution)/shard_map/ppermute | solution.py:171
  90.1 3.6 %all-to-all-done = bf16[32,16,128]{2,1,0:T(8,128)(2,1)S(1)} async-done(((bf16[32,16,128]{2,1,0:T(8,128)(2,1)}), bf16[32,16,128]{2,1,0:T(8,128)(2,1)S(1)}, u32[]{:S(2)}, u32[]{:S(2)}) %all-to-all-start) | async-done | bytes 131104 | tf_op jit(solution)/shard_map/all_to_all | solution.py:153
  94.3 5.8 %all-to-all-start.1 = ((bf16[8,16,128]{2,1,0:T(8,128)(2,1)}), bf16[8,16,128]{2,1,0:T(8,128)(2,1)S(1)}, u32[]{:S(2)}, u32[]{:S(2)}) async-start(bf16[8,16,128]{2,1,0:T(8,128)(2,1)} %bitcast.8), calls=%async_computation.1 | async-start | bytes 65536 | tf_op jit(solution)/shard_map/all_to_all | solution.py:153
  100.9 6.1 %all-to-all-done.1 = bf16[8,16,128]{2,1,0:T(8,128)(2,1)S(1)} async-done(((bf16[8,16,128]{2,1,0:T(8,128)(2,1)}), bf16[8,16,128]{2,1,0:T(8,128)(2,1)S(1)}, u32[]{:S(2)}, u32[]{:S(2)}) %all-to-all-start.1) | async-done | bytes 32800 | tf_op jit(solution)/shard_map/all_to_all | solution.py:153
  107.7 5.4 %all-to-all-start.2 = ((bf16[32,16,128]{2,1,0:T(8,128)(2,1)}), bf16[32,16,128]{2,1,0:T(8,128)(2,1)S(1)}, u32[]{:S(2)}, u32[]{:S(2)}) async-start(bf16[32,16,128]{2,1,0:T(8,128)(2,1)} %bitcast.10), calls=%async_computation.2 | async-start | bytes 262144 | tf_op jit(solution)/shard_map/all_to_all | solution.py:153
  115.2 1.1 fusion.21
  117.2 3.6 %all-to-all-done.2 = bf16[32,16,128]{2,1,0:T(8,128)(2,1)S(1)} async-done(((bf16[32,16,128]{2,1,0:T(8,128)(2,1)}), bf16[32,16,128]{2,1,0:T(8,128)(2,1)S(1)}, u32[]{:S(2)}, u32[]{:S(2)}) %all-to-all-start.2) | async-done | bytes 131104 | tf_op jit(solution)/shard_map/all_to_all | solution.py:153
  (45 shorter events, 16.9 us)
Async XLA Ops:
  0.6 13.5 %collective-permute-start = (bf16[1024,256]{1,0:T(8,128)(2,1)}, bf16[1024,256]{1,0:T(8,128)(2,1)S(1)}, u32[]{:S(2)}, u32[]{:S(2)}) collective-permute-start(bf16[1024,256]{1,0:T(8,128)(2,1)} %param.7), channel_id=1, source_target_pairs={{0,1},{1,0},{2,3},{3,2},{4,5},{5,4},{6,7},{7,6},{8,9},{9,8},{10,11... | collective-permute-start | bytes 1572872 | tf_op jit(solution)/shard_map/ppermute | solution.py:171
  5.5 2.0 %copy-start = (bf16[256,256]{1,0:T(8,128)(2,1)S(1)}, bf16[256,256]{1,0:T(8,128)(2,1)}, u32[]{:S(2)}) copy-start(bf16[256,256]{1,0:T(8,128)(2,1)} %relation_ref.8) | copy-start | bytes 393220
  7.1 1.0 copy-start.3
  16.8 15.6 %collective-permute-start.1 = (bf16[528,256]{1,0:T(8,128)(2,1)S(1)}, bf16[528,256]{1,0:T(8,128)(2,1)S(1)}, u32[]{:S(2)}, u32[]{:S(2)}) collective-permute-start(bf16[528,256]{1,0:T(8,128)(2,1)S(1)} %get-tuple-element.18), channel_id=1, source_target_pairs={{0,2},{1,3},{2,0},{3,1},{4,6},{5,7},{6,4},{7,5},{8,10},{9,11},{10,... | collective-permute-start | bytes 811016 | tf_op jit(solution)/shard_map/ppermute | solution.py:171
  34.8 10.3 %collective-permute-start.3 = (bf16[512,256]{1,0:T(8,128)(2,1)S(1)}, bf16[512,256]{1,0:T(8,128)(2,1)S(1)}, u32[]{:S(2)}, u32[]{:S(2)}) collective-permute-start(bf16[512,256]{1,0:T(8,128)(2,1)S(1)} %fusion.22), channel_id=1, source_target_pairs={{0,2},{1,3},{2,0},{3,1},{4,6},{5,7},{6,4},{7,5},{8,10},{9,11},{10,... | collective-permute-start | bytes 786440 | tf_op jit(solution)/shard_map/ppermute | solution.py:171
  35.2 28.0 %collective-permute-start.2 = (bf16[1024,256]{1,0:T(8,128)(2,1)S(1)}, bf16[1024,256]{1,0:T(8,128)(2,1)S(1)}, u32[]{:S(2)}, u32[]{:S(2)}) collective-permute-start(bf16[1024,256]{1,0:T(8,128)(2,1)S(1)} %get-tuple-element.20), channel_id=1, source_target_pairs={{0,6},{1,7},{2,4},{3,5},{4,2},{5,3},{6,0},{7,1},{8,14},{9,15},{10,... | collective-permute-start | bytes 1572872 | tf_op jit(solution)/shard_map/ppermute | solution.py:171
  46.6 0.8 copy-start.2
  67.0 6.2 %collective-permute-start.4 = (bf16[528,256]{1,0:T(8,128)(2,1)S(1)}, bf16[528,256]{1,0:T(8,128)(2,1)S(1)}, u32[]{:S(2)}, u32[]{:S(2)}) collective-permute-start(bf16[528,256]{1,0:T(8,128)(2,1)S(1)} %get-tuple-element.24), channel_id=1, source_target_pairs={{0,8},{1,9},{2,10},{3,11},{4,12},{5,13},{6,14},{7,15},{8,0},{9,1},... | collective-permute-start | bytes 811016 | tf_op jit(solution)/shard_map/ppermute | solution.py:171
  76.1 17.5 %all-to-all-start = ((bf16[32,16,128]{2,1,0:T(8,128)(2,1)}), bf16[32,16,128]{2,1,0:T(8,128)(2,1)S(1)}, u32[]{:S(2)}, u32[]{:S(2)}) async-start(bf16[32,16,128]{2,1,0:T(8,128)(2,1)} %bitcast.6), calls=%async_computation | async-start | bytes 262144 | tf_op jit(solution)/shard_map/all_to_all | solution.py:153
  88.7 24.4 %collective-permute-start.6 = (bf16[512,256]{1,0:T(8,128)(2,1)S(1)}, bf16[512,256]{1,0:T(8,128)(2,1)S(1)}, u32[]{:S(2)}, u32[]{:S(2)}) collective-permute-start(bf16[512,256]{1,0:T(8,128)(2,1)S(1)} %get-tuple-element.28), channel_id=1, source_target_pairs={{0,8},{1,9},{2,10},{3,11},{4,12},{5,13},{6,14},{7,15},{8,0},{9,1},... | collective-permute-start | bytes 786440 | tf_op jit(solution)/shard_map/ppermute | solution.py:171
  94.3 12.7 %all-to-all-start.1 = ((bf16[8,16,128]{2,1,0:T(8,128)(2,1)}), bf16[8,16,128]{2,1,0:T(8,128)(2,1)S(1)}, u32[]{:S(2)}, u32[]{:S(2)}) async-start(bf16[8,16,128]{2,1,0:T(8,128)(2,1)} %bitcast.8), calls=%async_computation.1 | async-start | bytes 65536 | tf_op jit(solution)/shard_map/all_to_all | solution.py:153
  100.6 15.8 %collective-permute-start.5 = (bf16[1024,256]{1,0:T(8,128)(2,1)S(1)}, bf16[1024,256]{1,0:T(8,128)(2,1)S(1)}, u32[]{:S(2)}, u32[]{:S(2)}) collective-permute-start(bf16[1024,256]{1,0:T(8,128)(2,1)S(1)} %subtract_convert_fusion.2), channel_id=1, source_target_pairs={{0,8},{1,9},{2,10},{3,11},{4,12},{5,13},{6,14},{7,15},{8,0},{9,1},... | collective-permute-start | bytes 1572872 | tf_op jit(solution)/shard_map/ppermute | solution.py:171
  107.7 13.1 %all-to-all-start.2 = ((bf16[32,16,128]{2,1,0:T(8,128)(2,1)}), bf16[32,16,128]{2,1,0:T(8,128)(2,1)S(1)}, u32[]{:S(2)}, u32[]{:S(2)}) async-start(bf16[32,16,128]{2,1,0:T(8,128)(2,1)} %bitcast.10), calls=%async_computation.2 | async-start | bytes 262144 | tf_op jit(solution)/shard_map/all_to_all | solution.py:153
  114.0 1.2 %copy-start.1 = (f32[1024,256]{1,0:T(8,128)S(1)}, f32[1024,256]{1,0:T(8,128)}, u32[]{:S(2)}) copy-start(f32[1024,256]{1,0:T(8,128)} %fusion.20) | copy-start | bytes 3145732

commit v5 on v4

--- a/solution.py
+++ b/solution.py
@@ -20,58 +20,71 @@
     return lax.dot_general(a, b, (dims, ((), ())), preferred_element_type=jnp.float32)
 
 
-RC = 64
-
-
-def fill_coeffs(queries, held_ref, target_ref, first, coeffs_ref, scores_ref):
-    rows = held_ref.shape[0]
-    edges = queries.shape[0]
-    parts = [slice(start, start + TE) for start in range(0, edges, TE)]
+RC = 128
+
+
+def scores_of(queries, held_ref, scores_ref, part):
+    scores_ref[:, part] = dot(held_ref[...], queries[part], ((1,), (1,)))
+
+
+def fill_coeffs(codes_ref, first, coeffs_ref, scores_ref, part):
+    rows, edges = coeffs_ref.shape
     chunks = [slice(start, start + RC) for start in range(0, rows, RC)]
     fold = lambda value, op: functools.reduce(op, [value[k:k + 8] for k in range(0, value.shape[0], 8)])
-    for part in parts:
-        scores_ref[:, part] = dot(held_ref[...], queries[part], ((1,), (1,)))
-    for part in parts:
-        top = functools.reduce(jnp.maximum, [fold(scores_ref[c, part], jnp.maximum) for c in chunks])
-        top = jnp.max(top, axis=0, keepdims=True)
-        total = None
-        for c in chunks:
-            expos = jnp.exp2((scores_ref[c, part] - top) * EXP_SCALE)
-            scores_ref[c, part] = expos
-            folded = fold(expos, jnp.add)
-            total = folded if total is None else total + folded
-        high, low = first + part.start // TE, first + (edges + part.start) // TE
-        target = target_ref[high:high + 1, :].astype(jnp.float32) * 32.0 + target_ref[low:low + 1, :].astype(jnp.float32)
-        live = (target >= 0.0).astype(jnp.float32)
-        weight = live / jnp.sum(total, axis=0, keepdims=True)
-        ids = lax.broadcasted_iota(jnp.int32, (RC, TE), 0).astype(jnp.float32)
-        for c in chunks:
-            softmax_w = scores_ref[c, part] * weight
-            coeffs = jnp.where(ids == target - float(c.start), softmax_w - 1.0, softmax_w)
-            coeffs_ref[c, part] = coeffs.astype(jnp.bfloat16)
-
-
-def gradient_of_queries(coeffs_ref, held_ref):
-    return (dot(coeffs_ref[...], held_ref[...], ((0,), (0,))) * SCORE_SCALE).astype(jnp.bfloat16)
+    top = functools.reduce(jnp.maximum, [fold(scores_ref[c, part], jnp.maximum) for c in chunks])
+    top = jnp.max(top, axis=0, keepdims=True)
+    total = None
+    for c in chunks:
+        expos = jnp.exp2((scores_ref[c, part] - top) * EXP_SCALE)
+        scores_ref[c, part] = expos
+        folded = fold(expos, jnp.add)
+        total = folded if total is None else total + folded
+    high, low = first + part.start // TE, first + (edges + part.start) // TE
+    target = codes_ref[high:high + 1, :].astype(jnp.float32) * 32.0 + codes_ref[low:low + 1, :].astype(jnp.float32)
+    live = (target >= 0.0).astype(jnp.float32)
+    weight = live / jnp.sum(total, axis=0, keepdims=True)
+    ids = lax.broadcasted_iota(jnp.int32, (RC, TE), 0).astype(jnp.float32)
+    for c in chunks:
+        softmax_w = scores_ref[c, part] * weight
+        coeffs = jnp.where(ids == target - float(c.start), softmax_w - 1.0, softmax_w)
+        coeffs_ref[c, part] = coeffs.astype(jnp.bfloat16)
+
+
+def parts_of(edges):
+    return [slice(start, start + TE) for start in range(0, edges, TE)]
+
+
+def fill_gradient(coeffs_ref, held_ref, grad_ref, part):
+    grad = dot(coeffs_ref[:, part], held_ref[...], ((0,), (0,))) * SCORE_SCALE
+    grad_ref[part, :] = grad.astype(jnp.bfloat16)
+
+
+def meeting_body(queries, held_ref, codes_ref, first, coeffs_ref, scores_ref, then):
+    parts = parts_of(coeffs_ref.shape[1])
+    scores_of(queries, held_ref, scores_ref, parts[0])
+    for k, part in enumerate(parts):
+        if k + 1 < len(parts):
+            scores_of(queries, held_ref, scores_ref, parts[k + 1])
+        fill_coeffs(codes_ref, first, coeffs_ref, scores_ref, part)
+        then(part)
 
 
 def local_kernel(meeting, queries_ref, held_ref, codes_ref, relation_ref, same_ref, base_ref, coeffs_ref, grad_ref, next_ref, scores_ref):
     edges = queries_ref.shape[0]
-    fill_coeffs(queries_ref[...], held_ref, codes_ref, CODE_ROWS * meeting, coeffs_ref, scores_ref)
-    grad = gradient_of_queries(coeffs_ref, held_ref)
-    grad_ref[...] = grad
-    row_grad = dot(grad, relation_ref[...], ((1,), (1,)))
-    high = row_grad.astype(jnp.bfloat16)
-    low = (row_grad - high.astype(jnp.float32)).astype(jnp.bfloat16)
-    summed = dot(same_ref[...], high, ((1,), (0,))) + dot(same_ref[...], low, ((1,), (0,)))
+    then = lambda part: fill_gradient(coeffs_ref, held_ref, grad_ref, part)
+    meeting_body(queries_ref[...], held_ref, codes_ref, CODE_ROWS * meeting, coeffs_ref, scores_ref, then)
+    summed = dot(same_ref[...], grad_ref[...], ((1,), (0,)))
+    high = summed.astype(jnp.bfloat16)
+    low = (summed - high.astype(jnp.float32)).astype(jnp.bfloat16)
+    change = dot(high, relation_ref[...], ((1,), (1,))) + dot(low, relation_ref[...], ((1,), (1,)))
     next_ref[edges:, :] = codes_ref[CODE_ROWS * (meeting + 1):CODE_ROWS * (meeting + 2), :]
-    next_ref[:edges, :] = (base_ref[...].astype(jnp.float32) - LR_EMBED * summed).astype(jnp.bfloat16)
+    next_ref[:edges, :] = (base_ref[...].astype(jnp.float32) - LR_EMBED * change).astype(jnp.bfloat16)
 
 
 def held_kernel(picked_ref, held_ref, relation_ref, new_ref, coeffs_ref, scores_ref):
     edges = coeffs_ref.shape[1]
     queries = dot(picked_ref[:edges, :], relation_ref[...], ((1,), (0,))).astype(jnp.bfloat16)
-    fill_coeffs(queries, held_ref, picked_ref, edges, coeffs_ref, scores_ref)
+    meeting_body(queries, held_ref, picked_ref, edges, coeffs_ref, scores_ref, lambda part: None)
     held_grad = dot(coeffs_ref[...], queries, ((1,), (0,)))
     new_ref[...] = (held_ref[...].astype(jnp.float32) - (LR_EMBED * SCORE_SCALE) * held_grad).astype(jnp.bfloat16)
 
@@ -81,13 +94,25 @@
     picked = picked_ref[:edges, :]
     queries = dot(picked, relation_ref[...], ((1,), (0,))).astype(jnp.bfloat16)
     queries_ref[...] = queries
-    fill_coeffs(queries, held_ref, picked_ref, edges, coeffs_ref, scores_ref)
-    grad = gradient_of_queries(coeffs_ref, held_ref)
-    grad_ref[...] = grad
-    total = before_ref[...] + dot(picked, grad, ((0,), (0,)))
+    then = lambda part: fill_gradient(coeffs_ref, held_ref, grad_ref, part)
+    meeting_body(queries, held_ref, picked_ref, edges, coeffs_ref, scores_ref, then)
+    total = before_ref[...] + dot(picked, grad_ref[...], ((0,), (0,)))
     half = total.shape[1] // 2
     pieces_ref[:total.shape[0], :] = total[:, :half].astype(jnp.bfloat16)
     pieces_ref[total.shape[0]:, :] = total[:, half:].astype(jnp.bfloat16)
+
+
+def left_kernel(left_ref, source_ref, grad_ref, relation_ref, out_ref):
+    rows = left_ref.shape[0]
+    for start in range(0, rows, TE):
+        part = slice(start, start + TE)
+        ids = lax.broadcasted_iota(jnp.int32, (TE, source_ref.shape[1]), 0) + start
+        table = (ids == source_ref[...]).astype(jnp.float32).astype(jnp.bfloat16)
+        summed = dot(table, grad_ref[...], ((1,), (0,)))
+        high = summed.astype(jnp.bfloat16)
+        low = (summed - high.astype(jnp.float32)).astype(jnp.bfloat16)
+        change = dot(high, relation_ref[...], ((1,), (1,))) + dot(low, relation_ref[...], ((1,), (1,)))
+        out_ref[part, :] = (left_ref[part, :].astype(jnp.float32) - LR_EMBED * change).astype(jnp.bfloat16)
 
 
 def sum_kernel(pieces_ref, copies_ref):
@@ -200,12 +225,8 @@
     return dot(picked, query_grad, ((0,), (0,)))
 
 
-def updated_left(left_block, table, query_grad, relation):
-    summed_rows = dot(table, query_grad, ((0,), (0,)))
-    high = summed_rows.astype(jnp.bfloat16)
-    low = (summed_rows - high.astype(jnp.float32)).astype(jnp.bfloat16)
-    left_grad = dot(high, relation, ((1,), (1,))) + dot(low, relation, ((1,), (1,)))
-    return (left_block.astype(jnp.float32) - LR_EMBED * left_grad).astype(jnp.bfloat16)
+def updated_left(left_block, source, query_grad, relation, out):
+    return call(left_kernel, out, left_block, source.reshape(1, -1), query_grad, relation)
 
 
 def coded(targets):
@@ -234,13 +255,13 @@
 
     rows1 = moved(picked1, 2)
     held = updated_holding(held, coeffs, queries0)
-    left = updated_left(left_part, tables[0], query_grad, relation)
+    left = updated_left(left_part, sources[0], query_grad, relation, vmem(*left_part.shape))
     relation_grad = relation_gradient(picked0, query_grad)
     new_held, coeffs = held_meeting(rows1, held, relation, edges)
     arriving = moved(new_held, 6)
     query_grad = query_gradient(coeffs, held)
     relation_grad = relation_grad + relation_gradient(rows1[:edges], query_grad)
-    left = updated_left(left, tables[1], moved(query_grad, 2), relation)
+    left = updated_left(left, sources[1], moved(query_grad, 2), relation, vmem(*left.shape))
 
     held = arriving
     picked2 = picked_rows(left, tables[2])
@@ -251,12 +272,14 @@
 
     rows3 = moved(picked3, 8)
     held = updated_holding(held, coeffs, queries2)
-    left = updated_left(left, tables[2], query_grad, relation)
+    left = updated_left(left, sources[2], query_grad, relation, vmem(*left.shape))
     relation_grad = relation_grad + relation_gradient(picked2, query_grad)
     pieces, coeffs, query_grad, queries3 = last_meeting(rows3, held, relation, relation_grad, edges)
     sums = shared_sums(pieces)
-    held = moved(updated_holding(held, coeffs, queries3), 8)
-    left = updated_left(left, tables[3], moved(query_grad, 8), relation)
+    held = updated_holding(held, coeffs, queries3)
+    held = moved(held, 8)
+    last = jax.ShapeDtypeStruct(left.shape, left.dtype)
+    left = updated_left(left, sources[3], moved(query_grad, 8), relation, last)
     held = call(copy_kernel, jax.ShapeDtypeStruct(held.shape, held.dtype), held)
     relation, held, left = lax.optimization_barrier((relation, held, left))
     relation_out = call(finish_kernel, jax.ShapeDtypeStruct(relation.shape, jnp.float32), sums, relation)

time: 122 us -> 125 us (1.025)
  blocking collectives: 0 us -> 13.9 us
  matrix products: 16.2 us -> 6.14 us
  starting transfers between devices: 37.8 us -> 32.8 us
  Pallas kernels: 13 us -> 15.9 us
  waiting for transfers between devices: 49.5 us -> 51.5 us
    all_to_all x0 -> x1, blocking collectives: none -> 13.9 us  [exchanged(): lax.all_to_all(pieces, axes, 0, 0, axis_index_groups=groups)]
    dot_general x25 -> x13, matrix products: 16.2 us -> 6.14 us  [dot(): lax.dot_general(a, b, (dims, ((), ())), preferred_element_type=jnp.float32)]
    all_to_all x3 -> x2, starting transfers between devices: 21.2 us -> 15.1 us  [exchanged(): lax.all_to_all(pieces, axes, 0, 0, axis_index_groups=groups)]
    ppermute x7, waiting for transfers between devices: 36.3 us -> 39.2 us  [moved(): return lax.ppermute(value, 'inner', pairs)]
    pallas_call x8 -> x12, Pallas kernels: 13 us -> 15.9 us  [call(): pl.pallas_call(kernel, out_shape=outs, in_specs=[spec] * len(args), out_s...]
    all_to_all x3 -> x2, waiting for transfers between devices: 13.2 us -> 12.3 us  [exchanged(): lax.all_to_all(pieces, axes, 0, 0, axis_index_groups=groups)]
  transfers between devices with their start and end apart: 10 -> 9, of which waited for: 8 -> 7; matrix products, arithmetic and copies ran while one was open for 14% -> 6% of each run, Pallas kernels for 2% -> 5%
where the time goes in v5:
time: 125 us; the launch traced here: 124 us
  waiting for transfers between devices  51.5 us (41%)
  starting transfers between devices  32.8 us (26%)
  Pallas kernels  15.9 us (13%)
  blocking collectives  13.9 us (11%)
  matrix products  6.14 us (5%)
  local copies, waits for them, and re-layouts  2.19 us (2%)
    ppermute x7, waiting for transfers between devices, moved(): return lax.ppermute(value, 'inner', pairs)  39.2 us
    ppermute x7, starting transfers between devices, moved(): return lax.ppermute(value, 'inner', pairs)  17.6 us
    pallas_call x12, Pallas kernels, call(): pl.pallas_call(kernel, out_shape=outs, in_specs=[spec] * len(args), out_s...  15.9 us
    all_to_all x2, starting transfers between devices, exchanged(): lax.all_to_all(pieces, axes, 0, 0, axis_index_groups=groups)  15.1 us
    all_to_all x1, blocking collectives, exchanged(): lax.all_to_all(pieces, axes, 0, 0, axis_index_groups=groups)  13.9 us
    all_to_all x2, waiting for transfers between devices, exchanged(): lax.all_to_all(pieces, axes, 0, 0, axis_index_groups=groups)  12.3 us
    dot_general x13, matrix products, dot(): lax.dot_general(a, b, (dims, ((), ())), preferred_element_type=jnp.float32)  6.14 us
  transfers between devices with their start and end apart: 9, of which 7 were waited for; matrix products, arithmetic and copies ran while one was open for 6% of the time, Pallas kernels for 5%

profile of v5, /device:TPU:1, one launch (start us, length us, event | category | flops | bytes accessed | tf_op | source)
XLA Modules:
  0.0 124.3 jit_solution(17818191629152257051)
XLA Ops:
  0.6 2.5 %collective-permute-start = (bf16[1024,256]{1,0:T(8,128)(2,1)}, bf16[1024,256]{1,0:T(8,128)(2,1)S(1)}, u32[]{:S(2)}, u32[]{:S(2)}) collective-permute-start(bf16[1024,256]{1,0:T(8,128)(2,1)} %param.7), channel_id=1, source_target_pairs={{0,1},{1,0},{2,3},{3,2},{4,5},{5,4},{6,7},{7,6},{8,9},{9,8},{10,11... | collective-permute-start | bytes 1572872 | tf_op jit(solution)/shard_map/ppermute | solution.py:196
  5.5 1.6 %fusion.8 = bf16[512,256]{1,0:T(8,128)(2,1)S(1)} fusion(bf16[1024,256]{1,0:T(8,128)(2,1)} %left_ref.1, s32[512]{0:T(512)S(1)} %bitcast.53), kind=kOutput, calls=%fused_computation.16 | convolution fusion | flops 269090816 | bytes 788480 | tf_op jit(solution)/shard_map/dot_general | solution.py:20
  8.7 5.4 %collective-permute-done.held_ref = bf16[1024,256]{1,0:T(8,128)(2,1)S(1)} collective-permute-done((bf16[1024,256]{1,0:T(8,128)(2,1)}, bf16[1024,256]{1,0:T(8,128)(2,1)S(1)}, u32[]{:S(2)}, u32[]{:S(2)}) %collective-permute-start) | collective-permute-done | bytes 524320 | tf_op jit(solution)/shard_map/ppermute | solution.py:196
  14.1 2.3 %shard_map.85 = (bf16[1024,512]{1,0:T(8,128)(2,1)S(1)}, bf16[512,256]{1,0:T(8,128)(2,1)S(1)}, bf16[528,256]{1,0:T(8,128)(2,1)S(1)}) custom-call(bf16[512,256]{1,0:T(8,128)(2,1)S(1)} %convolution_convert_fusion.1.queries_ref, bf16[1024,256]{1,0:T(8,128)(2,1)S(1)} %collective-permute-done.held_ref, bf16[64,256]{1,0:T(8,128)(2,1)S(1)} %bitcast.43, ...), custom_call_target="tpu_custom_call" | custom-call | tf_op jit(solution)/shard_map/pallas_call | solution.py:141
  16.4 3.9 %collective-permute-start.1 = (bf16[528,256]{1,0:T(8,128)(2,1)S(1)}, bf16[528,256]{1,0:T(8,128)(2,1)S(1)}, u32[]{:S(2)}, u32[]{:S(2)}) collective-permute-start(bf16[528,256]{1,0:T(8,128)(2,1)S(1)} %get-tuple-element.18), channel_id=1, source_target_pairs={{0,2},{1,3},{2,0},{3,1},{4,6},{5,7},{6,4},{7,5},{8,10},{9,11},{10,... | collective-permute-start | bytes 811016 | tf_op jit(solution)/shard_map/ppermute | solution.py:196
  20.8 11.3 %collective-permute-done.1.picked_ref = bf16[528,256]{1,0:T(8,128)(2,1)S(1)} collective-permute-done((bf16[528,256]{1,0:T(8,128)(2,1)S(1)}, bf16[528,256]{1,0:T(8,128)(2,1)S(1)}, u32[]{:S(2)}, u32[]{:S(2)}) %collective-permute-start.1) | collective-permute-done | bytes 270368 | tf_op jit(solution)/shard_map/ppermute | solution.py:196
  32.1 1.9 %shard_map.86 = (bf16[1024,256]{1,0:T(8,128)(2,1)S(1)}, bf16[1024,512]{1,0:T(8,128)(2,1)S(1)}) custom-call(bf16[528,256]{1,0:T(8,128)(2,1)S(1)} %collective-permute-done.1.picked_ref, bf16[1024,256]{1,0:T(8,128)(2,1)S(1)} %subtract_convert_fusion.2.held_ref, bf16[256,256]{1,0:T(8,128)(2,1)S(1)} %copy-done), custom_call_target="tpu_custom_call" | custom-call | tf_op jit(solution)/shard_map/pallas_call | solution.py:141
  34.7 0.9 shard_map.87.left_ref
  35.6 7.0 %collective-permute-start.2 = (bf16[1024,256]{1,0:T(8,128)(2,1)S(1)}, bf16[1024,256]{1,0:T(8,128)(2,1)S(1)}, u32[]{:S(2)}, u32[]{:S(2)}) collective-permute-start(bf16[1024,256]{1,0:T(8,128)(2,1)S(1)} %get-tuple-element.20), channel_id=1, source_target_pairs={{0,6},{1,7},{2,4},{3,5},{4,2},{5,3},{6,0},{7,1},{8,14},{9,15},{10,... | collective-permute-start | bytes 1572872 | tf_op jit(solution)/shard_map/ppermute | solution.py:196
  42.9 2.6 %collective-permute-done.3.grad_ref = bf16[512,256]{1,0:T(8,128)(2,1)S(1)} collective-permute-done((bf16[512,256]{1,0:T(8,128)(2,1)S(1)}, bf16[512,256]{1,0:T(8,128)(2,1)S(1)}, u32[]{:S(2)}, u32[]{:S(2)}) %collective-permute-start.3) | collective-permute-done | bytes 262176 | tf_op jit(solution)/shard_map/ppermute | solution.py:196
  45.5 0.9 shard_map.88.left_ref
  47.6 16.0 %collective-permute-done.2.held_ref = bf16[1024,256]{1,0:T(8,128)(2,1)S(1)} collective-permute-done((bf16[1024,256]{1,0:T(8,128)(2,1)S(1)}, bf16[1024,256]{1,0:T(8,128)(2,1)S(1)}, u32[]{:S(2)}, u32[]{:S(2)}) %collective-permute-start.2) | collective-permute-done | bytes 524320 | tf_op jit(solution)/shard_map/ppermute | solution.py:196
  63.6 2.4 %shard_map.89 = (bf16[1024,512]{1,0:T(8,128)(2,1)S(1)}, bf16[512,256]{1,0:T(8,128)(2,1)S(1)}, bf16[528,256]{1,0:T(8,128)(2,1)S(1)}) custom-call(bf16[512,256]{1,0:T(8,128)(2,1)S(1)} %convolution_convert_fusion.queries_ref, bf16[1024,256]{1,0:T(8,128)(2,1)S(1)} %collective-permute-done.2.held_ref, bf16[64,256]{1,0:T(8,128)(2,1)S(1)} %bitcast.44, ...), custom_call_target="tpu_custom_call" | custom-call | tf_op jit(solution)/shard_map/pallas_call | solution.py:141
  66.0 1.3 %collective-permute-start.4 = (bf16[528,256]{1,0:T(8,128)(2,1)S(1)}, bf16[528,256]{1,0:T(8,128)(2,1)S(1)}, u32[]{:S(2)}, u32[]{:S(2)}) collective-permute-start(bf16[528,256]{1,0:T(8,128)(2,1)S(1)} %get-tuple-element.24), channel_id=1, source_target_pairs={{0,8},{1,9},{2,10},{3,11},{4,12},{5,13},{6,14},{7,15},{8,0},{9,1},... | collective-permute-start | bytes 811016 | tf_op jit(solution)/shard_map/ppermute | solution.py:196
  68.3 3.9 %collective-permute-done.4.picked_ref = bf16[528,256]{1,0:T(8,128)(2,1)S(1)} collective-permute-done((bf16[528,256]{1,0:T(8,128)(2,1)S(1)}, bf16[528,256]{1,0:T(8,128)(2,1)S(1)}, u32[]{:S(2)}, u32[]{:S(2)}) %collective-permute-start.4) | collective-permute-done | bytes 270368 | tf_op jit(solution)/shard_map/ppermute | solution.py:196
  72.1 2.7 %shard_map.90 = (bf16[512,128]{1,0:T(8,128)(2,1)}, bf16[1024,512]{1,0:T(8,128)(2,1)S(1)}, bf16[512,256]{1,0:T(8,128)(2,1)S(1)}, bf16[512,256]{1,0:T(8,128)(2,1)S(1)}) custom-call(bf16[528,256]{1,0:T(8,128)(2,1)S(1)} %collective-permute-done.4.picked_ref, bf16[1024,256]{1,0:T(8,128)(2,1)S(1)} %subtract_convert_fusion.1.held_ref, ...), custom_call_target="tpu_custom_call" | custom-call | tf_op jit(solution)/shard_map/pallas_call | solution.py:141
  75.3 1.3 %collective-permute-start.5 = (bf16[1024,256]{1,0:T(8,128)(2,1)S(1)}, bf16[1024,256]{1,0:T(8,128)(2,1)S(1)}, u32[]{:S(2)}, u32[]{:S(2)}) collective-permute-start(bf16[1024,256]{1,0:T(8,128)(2,1)S(1)} %subtract_convert_fusion), channel_id=1, source_target_pairs={{0,8},{1,9},{2,10},{3,11},{4,12},{5,13},{6,14},{7,15},{8,0},{9,1},... | collective-permute-start | bytes 1572872 | tf_op jit(solution)/shard_map/ppermute | solution.py:196
  76.6 9.9 %all-to-all-start = ((bf16[32,16,128]{2,1,0:T(8,128)(2,1)}), bf16[32,16,128]{2,1,0:T(8,128)(2,1)S(1)}, u32[]{:S(2)}, u32[]{:S(2)}) async-start(bf16[32,16,128]{2,1,0:T(8,128)(2,1)} %bitcast.10), calls=%async_computation | async-start | bytes 262144 | tf_op jit(solution)/shard_map/all_to_all | solution.py:178
  86.5 1.4 %collective-permute-start.6 = (bf16[512,256]{1,0:T(8,128)(2,1)S(1)}, bf16[512,256]{1,0:T(8,128)(2,1)S(1)}, u32[]{:S(2)}, u32[]{:S(2)}) collective-permute-start(bf16[512,256]{1,0:T(8,128)(2,1)S(1)} %get-tuple-element.28), channel_id=1, source_target_pairs={{0,8},{1,9},{2,10},{3,11},{4,12},{5,13},{6,14},{7,15},{8,0},{9,1},... | collective-permute-start | bytes 786440 | tf_op jit(solution)/shard_map/ppermute | solution.py:196
  87.9 8.1 %all-to-all-done = bf16[32,16,128]{2,1,0:T(8,128)(2,1)S(1)} async-done(((bf16[32,16,128]{2,1,0:T(8,128)(2,1)}), bf16[32,16,128]{2,1,0:T(8,128)(2,1)S(1)}, u32[]{:S(2)}, u32[]{:S(2)}) %all-to-all-start) | async-done | bytes 131104 | tf_op jit(solution)/shard_map/all_to_all | solution.py:178
  96.1 13.9 %all_to_all.15 = bf16[8,16,128]{2,1,0:T(8,128)(2,1)S(1)} all-to-all(bf16[8,16,128]{2,1,0:T(8,128)(2,1)S(1)} %bitcast.45), channel_id=1, replica_groups={{0,1,2,3,4,5,6,7},{8,9,10,11,12,13,14,15},{16,17,18,19,20,21,22,23},{24..., dimensions={0} | all-to-all | bytes 65536 | tf_op jit(solution)/shard_map/all_to_all | solution.py:178
  110.7 5.3 %all-to-all-start.2 = ((bf16[32,16,128]{2,1,0:T(8,128)(2,1)}), bf16[32,16,128]{2,1,0:T(8,128)(2,1)S(1)}, u32[]{:S(2)}, u32[]{:S(2)}) async-start(bf16[32,16,128]{2,1,0:T(8,128)(2,1)} %bitcast.14), calls=%async_computation.2 | async-start | bytes 262144 | tf_op jit(solution)/shard_map/all_to_all | solution.py:178
  116.9 1.7 %shard_map.93 = bf16[1024,256]{1,0:T(8,128)(2,1)} custom-call(bf16[1024,256]{1,0:T(8,128)(2,1)S(1)} %shard_map.92.left_ref, s32[1,512]{1,0:T(1,128)S(1)} %get-tuple-element.35.source_ref, bf16[512,256]{1,0:T(8,128)(2,1)S(1)} %collective-permute-done.6.grad_ref, bf16[256,256]{1,0:T(8,128)(2,1)S(1)} %copy-done), custom_call_target="tpu_custom_call" | custom-call | tf_op jit(solution)/shard_map/pallas_call | solution.py:141
  119.4 4.2 %all-to-all-done.2 = bf16[32,16,128]{2,1,0:T(8,128)(2,1)S(1)} async-done(((bf16[32,16,128]{2,1,0:T(8,128)(2,1)}), bf16[32,16,128]{2,1,0:T(8,128)(2,1)S(1)}, u32[]{:S(2)}, u32[]{:S(2)}) %all-to-all-start.2) | async-done | bytes 131104 | tf_op jit(solution)/shard_map/all_to_all | solution.py:178
  (32 shorter events, 11.1 us)
Async XLA Ops:
  0.6 13.5 %collective-permute-start = (bf16[1024,256]{1,0:T(8,128)(2,1)}, bf16[1024,256]{1,0:T(8,128)(2,1)S(1)}, u32[]{:S(2)}, u32[]{:S(2)}) collective-permute-start(bf16[1024,256]{1,0:T(8,128)(2,1)} %param.7), channel_id=1, source_target_pairs={{0,1},{1,0},{2,3},{3,2},{4,5},{5,4},{6,7},{7,6},{8,9},{9,8},{10,11... | collective-permute-start | bytes 1572872 | tf_op jit(solution)/shard_map/ppermute | solution.py:196
  5.5 1.8 %copy-start = (bf16[256,256]{1,0:T(8,128)(2,1)S(1)}, bf16[256,256]{1,0:T(8,128)(2,1)}, u32[]{:S(2)}) copy-start(bf16[256,256]{1,0:T(8,128)(2,1)} %relation_ref.16) | copy-start | bytes 393220
  7.1 1.0 copy-start.1
  16.4 15.6 %collective-permute-start.1 = (bf16[528,256]{1,0:T(8,128)(2,1)S(1)}, bf16[528,256]{1,0:T(8,128)(2,1)S(1)}, u32[]{:S(2)}, u32[]{:S(2)}) collective-permute-start(bf16[528,256]{1,0:T(8,128)(2,1)S(1)} %get-tuple-element.18), channel_id=1, source_target_pairs={{0,2},{1,3},{2,0},{3,1},{4,6},{5,7},{6,4},{7,5},{8,10},{9,11},{10,... | collective-permute-start | bytes 811016 | tf_op jit(solution)/shard_map/ppermute | solution.py:196
  34.4 11.0 %collective-permute-start.3 = (bf16[512,256]{1,0:T(8,128)(2,1)S(1)}, bf16[512,256]{1,0:T(8,128)(2,1)S(1)}, u32[]{:S(2)}, u32[]{:S(2)}) collective-permute-start(bf16[512,256]{1,0:T(8,128)(2,1)S(1)} %fusion.4), channel_id=1, source_target_pairs={{0,2},{1,3},{2,0},{3,1},{4,6},{5,7},{6,4},{7,5},{8,10},{9,11},{10,... | collective-permute-start | bytes 786440 | tf_op jit(solution)/shard_map/ppermute | solution.py:196
  35.6 28.0 %collective-permute-start.2 = (bf16[1024,256]{1,0:T(8,128)(2,1)S(1)}, bf16[1024,256]{1,0:T(8,128)(2,1)S(1)}, u32[]{:S(2)}, u32[]{:S(2)}) collective-permute-start(bf16[1024,256]{1,0:T(8,128)(2,1)S(1)} %get-tuple-element.20), channel_id=1, source_target_pairs={{0,6},{1,7},{2,4},{3,5},{4,2},{5,3},{6,0},{7,1},{8,14},{9,15},{10,... | collective-permute-start | bytes 1572872 | tf_op jit(solution)/shard_map/ppermute | solution.py:196
  66.0 6.2 %collective-permute-start.4 = (bf16[528,256]{1,0:T(8,128)(2,1)S(1)}, bf16[528,256]{1,0:T(8,128)(2,1)S(1)}, u32[]{:S(2)}, u32[]{:S(2)}) collective-permute-start(bf16[528,256]{1,0:T(8,128)(2,1)S(1)} %get-tuple-element.24), channel_id=1, source_target_pairs={{0,8},{1,9},{2,10},{3,11},{4,12},{5,13},{6,14},{7,15},{8,0},{9,1},... | collective-permute-start | bytes 811016 | tf_op jit(solution)/shard_map/ppermute | solution.py:196
  75.3 43.3 %collective-permute-start.5 = (bf16[1024,256]{1,0:T(8,128)(2,1)S(1)}, bf16[1024,256]{1,0:T(8,128)(2,1)S(1)}, u32[]{:S(2)}, u32[]{:S(2)}) collective-permute-start(bf16[1024,256]{1,0:T(8,128)(2,1)S(1)} %subtract_convert_fusion), channel_id=1, source_target_pairs={{0,8},{1,9},{2,10},{3,11},{4,12},{5,13},{6,14},{7,15},{8,0},{9,1},... | collective-permute-start | bytes 1572872 | tf_op jit(solution)/shard_map/ppermute | solution.py:196
  76.6 19.4 %all-to-all-start = ((bf16[32,16,128]{2,1,0:T(8,128)(2,1)}), bf16[32,16,128]{2,1,0:T(8,128)(2,1)S(1)}, u32[]{:S(2)}, u32[]{:S(2)}) async-start(bf16[32,16,128]{2,1,0:T(8,128)(2,1)} %bitcast.10), calls=%async_computation | async-start | bytes 262144 | tf_op jit(solution)/shard_map/all_to_all | solution.py:178
  86.5 30.4 %collective-permute-start.6 = (bf16[512,256]{1,0:T(8,128)(2,1)S(1)}, bf16[512,256]{1,0:T(8,128)(2,1)S(1)}, u32[]{:S(2)}, u32[]{:S(2)}) collective-permute-start(bf16[512,256]{1,0:T(8,128)(2,1)S(1)} %get-tuple-element.28), channel_id=1, source_target_pairs={{0,8},{1,9},{2,10},{3,11},{4,12},{5,13},{6,14},{7,15},{8,0},{9,1},... | collective-permute-start | bytes 786440 | tf_op jit(solution)/shard_map/ppermute | solution.py:196
  110.7 12.9 %all-to-all-start.2 = ((bf16[32,16,128]{2,1,0:T(8,128)(2,1)}), bf16[32,16,128]{2,1,0:T(8,128)(2,1)S(1)}, u32[]{:S(2)}, u32[]{:S(2)}) async-start(bf16[32,16,128]{2,1,0:T(8,128)(2,1)} %bitcast.14), calls=%async_computation.2 | async-start | bytes 262144 | tf_op jit(solution)/shard_map/all_to_all | solution.py:178

commit v6 on v5

--- a/solution.py
+++ b/solution.py
@@ -27,8 +27,8 @@
     scores_ref[:, part] = dot(held_ref[...], queries[part], ((1,), (1,)))
 
 
-def fill_coeffs(codes_ref, first, coeffs_ref, scores_ref, part):
-    rows, edges = coeffs_ref.shape
+def fill_coeffs(codes_ref, high, low, coeffs_ref, scores_ref, part):
+    rows = coeffs_ref.shape[0]
     chunks = [slice(start, start + RC) for start in range(0, rows, RC)]
     fold = lambda value, op: functools.reduce(op, [value[k:k + 8] for k in range(0, value.shape[0], 8)])
     top = functools.reduce(jnp.maximum, [fold(scores_ref[c, part], jnp.maximum) for c in chunks])
@@ -39,7 +39,6 @@
         scores_ref[c, part] = expos
         folded = fold(expos, jnp.add)
         total = folded if total is None else total + folded
-    high, low = first + part.start // TE, first + (edges + part.start) // TE
     target = codes_ref[high:high + 1, :].astype(jnp.float32) * 32.0 + codes_ref[low:low + 1, :].astype(jnp.float32)
     live = (target >= 0.0).astype(jnp.float32)
     weight = live / jnp.sum(total, axis=0, keepdims=True)
@@ -50,65 +49,68 @@
         coeffs_ref[c, part] = coeffs.astype(jnp.bfloat16)
 
 
-def parts_of(edges):
-    return [slice(start, start + TE) for start in range(0, edges, TE)]
-
-
 def fill_gradient(coeffs_ref, held_ref, grad_ref, part):
     grad = dot(coeffs_ref[:, part], held_ref[...], ((0,), (0,))) * SCORE_SCALE
     grad_ref[part, :] = grad.astype(jnp.bfloat16)
 
 
-def meeting_body(queries, held_ref, codes_ref, first, coeffs_ref, scores_ref, then):
-    parts = parts_of(coeffs_ref.shape[1])
-    scores_of(queries, held_ref, scores_ref, parts[0])
+def local_kernel(meeting, queries_ref, held_ref, codes_ref, relation_ref, same_ref, base_ref, coeffs_ref, grad_ref, first_ref, second_ref, scores_ref):
+    edges = queries_ref.shape[0]
+    parts = [slice(start, start + TE) for start in range(0, edges, TE)]
+    code = CODE_ROWS * meeting
+    scores_of(queries_ref[...], held_ref, scores_ref, parts[0])
     for k, part in enumerate(parts):
         if k + 1 < len(parts):
-            scores_of(queries, held_ref, scores_ref, parts[k + 1])
-        fill_coeffs(codes_ref, first, coeffs_ref, scores_ref, part)
-        then(part)
-
-
-def local_kernel(meeting, queries_ref, held_ref, codes_ref, relation_ref, same_ref, base_ref, coeffs_ref, grad_ref, next_ref, scores_ref):
-    edges = queries_ref.shape[0]
-    then = lambda part: fill_gradient(coeffs_ref, held_ref, grad_ref, part)
-    meeting_body(queries_ref[...], held_ref, codes_ref, CODE_ROWS * meeting, coeffs_ref, scores_ref, then)
-    summed = dot(same_ref[...], grad_ref[...], ((1,), (0,)))
-    high = summed.astype(jnp.bfloat16)
-    low = (summed - high.astype(jnp.float32)).astype(jnp.bfloat16)
-    change = dot(high, relation_ref[...], ((1,), (1,))) + dot(low, relation_ref[...], ((1,), (1,)))
-    next_ref[edges:, :] = codes_ref[CODE_ROWS * (meeting + 1):CODE_ROWS * (meeting + 2), :]
-    next_ref[:edges, :] = (base_ref[...].astype(jnp.float32) - LR_EMBED * change).astype(jnp.bfloat16)
-
-
-def held_kernel(picked_ref, held_ref, relation_ref, new_ref, coeffs_ref, scores_ref):
-    edges = coeffs_ref.shape[1]
-    queries = dot(picked_ref[:edges, :], relation_ref[...], ((1,), (0,))).astype(jnp.bfloat16)
-    meeting_body(queries, held_ref, picked_ref, edges, coeffs_ref, scores_ref, lambda part: None)
-    held_grad = dot(coeffs_ref[...], queries, ((1,), (0,)))
+            scores_of(queries_ref[...], held_ref, scores_ref, parts[k + 1])
+        fill_coeffs(codes_ref, code + k, code + len(parts) + k, coeffs_ref, scores_ref, part)
+        fill_gradient(coeffs_ref, held_ref, grad_ref, part)
+    for part, next_ref in zip(parts, (first_ref, second_ref)):
+        summed = dot(same_ref[part, :], grad_ref[...], ((1,), (0,)))
+        high = summed.astype(jnp.bfloat16)
+        low = (summed - high.astype(jnp.float32)).astype(jnp.bfloat16)
+        change = dot(high, relation_ref[...], ((1,), (1,))) + dot(low, relation_ref[...], ((1,), (1,)))
+        next_ref[TE:, :] = codes_ref[code + CODE_ROWS:code + 2 * CODE_ROWS, :]
+        next_ref[:TE, :] = (base_ref[part, :].astype(jnp.float32) - LR_EMBED * change).astype(jnp.bfloat16)
+
+
+def half_of_meeting(half, picked_ref, held_ref, relation_ref, coeffs_ref, scores_ref):
+    queries = dot(picked_ref[:TE, :], relation_ref[...], ((1,), (0,))).astype(jnp.bfloat16)
+    part = slice(0, TE)
+    scores_of(queries, held_ref, scores_ref, part)
+    fill_coeffs(picked_ref, TE + half, TE + 2 + half, coeffs_ref, scores_ref, part)
+    return queries
+
+
+def first_kernel(picked_ref, held_ref, relation_ref, before_ref, coeffs_ref, queries_ref, grad_ref, after_ref, scores_ref):
+    queries_ref[...] = half_of_meeting(0, picked_ref, held_ref, relation_ref, coeffs_ref, scores_ref)
+    fill_gradient(coeffs_ref, held_ref, grad_ref, slice(0, TE))
+    after_ref[...] = before_ref[...] + dot(picked_ref[:TE, :], grad_ref[...], ((0,), (0,)))
+
+
+def held_kernel(picked_ref, held_ref, relation_ref, coeffs0_ref, queries0_ref, new_ref, coeffs_ref, scores_ref):
+    queries = half_of_meeting(1, picked_ref, held_ref, relation_ref, coeffs_ref, scores_ref)
+    held_grad = dot(coeffs0_ref[...], queries0_ref[...], ((1,), (0,))) + dot(coeffs_ref[...], queries, ((1,), (0,)))
     new_ref[...] = (held_ref[...].astype(jnp.float32) - (LR_EMBED * SCORE_SCALE) * held_grad).astype(jnp.bfloat16)
 
 
 def last_kernel(picked_ref, held_ref, relation_ref, before_ref, pieces_ref, coeffs_ref, grad_ref, queries_ref, scores_ref):
-    edges = coeffs_ref.shape[1]
-    picked = picked_ref[:edges, :]
-    queries = dot(picked, relation_ref[...], ((1,), (0,))).astype(jnp.bfloat16)
-    queries_ref[...] = queries
-    then = lambda part: fill_gradient(coeffs_ref, held_ref, grad_ref, part)
-    meeting_body(queries, held_ref, picked_ref, edges, coeffs_ref, scores_ref, then)
-    total = before_ref[...] + dot(picked, grad_ref[...], ((0,), (0,)))
+    queries_ref[...] = half_of_meeting(1, picked_ref, held_ref, relation_ref, coeffs_ref, scores_ref)
+    fill_gradient(coeffs_ref, held_ref, grad_ref, slice(0, TE))
+    total = before_ref[...] + dot(picked_ref[:TE, :], grad_ref[...], ((0,), (0,)))
     half = total.shape[1] // 2
     pieces_ref[:total.shape[0], :] = total[:, :half].astype(jnp.bfloat16)
     pieces_ref[total.shape[0]:, :] = total[:, half:].astype(jnp.bfloat16)
 
 
-def left_kernel(left_ref, source_ref, grad_ref, relation_ref, out_ref):
+def left_kernel(left_ref, source_ref, relation_ref, *refs):
+    out_ref = refs[-1]
+    grads = jnp.concatenate([ref[...] for ref in refs[:-1]], axis=0)
     rows = left_ref.shape[0]
     for start in range(0, rows, TE):
         part = slice(start, start + TE)
         ids = lax.broadcasted_iota(jnp.int32, (TE, source_ref.shape[1]), 0) + start
         table = (ids == source_ref[...]).astype(jnp.float32).astype(jnp.bfloat16)
-        summed = dot(table, grad_ref[...], ((1,), (0,)))
+        summed = dot(table, grads, ((1,), (0,)))
         high = summed.astype(jnp.bfloat16)
         low = (summed - high.astype(jnp.float32)).astype(jnp.bfloat16)
         change = dot(high, relation_ref[...], ((1,), (1,))) + dot(low, relation_ref[...], ((1,), (1,)))
@@ -154,22 +156,29 @@
 
 def local_meeting(meeting, queries, held, codes, relation, same, base):
     (edges, width), rows = queries.shape, held.shape[0]
-    outs = (vmem(rows, edges), vmem(edges, width), vmem(edges + CODE_ROWS, width))
-    scratch = [VM((rows, edges), jnp.float32)]
-    return call(functools.partial(local_kernel, meeting), outs, queries, held, codes, relation, same, base, scratch=scratch)
-
-
-def held_meeting(picked, held, relation, edges):
+    travel = vmem(TE + CODE_ROWS, width)
+    outs = (vmem(rows, edges), vmem(edges, width), travel, travel)
+    kernel = functools.partial(local_kernel, meeting)
+    return call(kernel, outs, queries, held, codes, relation, same, base, scratch=[VM((rows, edges), jnp.float32)])
+
+
+def first_half(picked, held, relation, before):
     rows, width = held.shape
-    outs = (vmem(rows, width), vmem(rows, edges))
-    return call(held_kernel, outs, picked, held, relation, scratch=[VM((rows, edges), jnp.float32)])
-
-
-def last_meeting(picked, held, relation, before, edges):
+    outs = (vmem(rows, TE), vmem(TE, width), vmem(TE, width), VM(before.shape, jnp.float32))
+    return call(first_kernel, outs, picked, held, relation, before, scratch=[VM((rows, TE), jnp.float32)])
+
+
+def held_half(picked, held, relation, coeffs, queries):
     rows, width = held.shape
-    outs = (vmem(2 * width, width // 2), vmem(rows, edges), vmem(edges, width), vmem(edges, width))
-    scratch = [VM((rows, edges), jnp.float32)]
-    return call(last_kernel, outs, picked, held, relation, before, scratch=scratch)
+    outs = (vmem(rows, width), vmem(rows, TE))
+    scratch = [VM((rows, TE), jnp.float32)]
+    return call(held_kernel, outs, picked, held, relation, coeffs, queries, scratch=scratch)
+
+
+def last_half(picked, held, relation, before):
+    rows, width = held.shape
+    outs = (vmem(2 * width, width // 2), vmem(rows, TE), vmem(TE, width), vmem(TE, width))
+    return call(last_kernel, outs, picked, held, relation, before, scratch=[VM((rows, TE), jnp.float32)])
 
 
 def exchanged(pieces, axes, groups):
@@ -212,8 +221,8 @@
     return dot(picked, relation, ((1,), (0,))).astype(jnp.bfloat16)
 
 
-def updated_holding(holding, coeffs, queries):
-    held_grad = dot(coeffs, queries, ((1,), (0,)))
+def updated_holding(holding, *products):
+    held_grad = functools.reduce(jnp.add, [dot(coeffs, queries, ((1,), (0,))) for coeffs, queries in products])
     return (holding.astype(jnp.float32) - (LR_EMBED * SCORE_SCALE) * held_grad).astype(jnp.bfloat16)
 
 
@@ -225,8 +234,8 @@
     return dot(picked, query_grad, ((0,), (0,)))
 
 
-def updated_left(left_block, source, query_grad, relation, out):
-    return call(left_kernel, out, left_block, source.reshape(1, -1), query_grad, relation)
+def updated_left(left_block, source, query_grads, relation, out):
+    return call(left_kernel, out, left_block, source.reshape(1, -1), relation, *query_grads)
 
 
 def coded(targets):
@@ -251,35 +260,39 @@
     queries0 = queries_of(picked0, relation)
     base = picked_rows(left_part, tables[1])
     same = same_source(sources[1], sources[0])
-    coeffs, query_grad, picked1 = local_meeting(0, queries0, held, codes, relation, same, base)
-
-    rows1 = moved(picked1, 2)
-    held = updated_holding(held, coeffs, queries0)
-    left = updated_left(left_part, sources[0], query_grad, relation, vmem(*left_part.shape))
+    coeffs, query_grad, first, second = local_meeting(0, queries0, held, codes, relation, same, base)
+
+    first, second = moved(first, 2), moved(second, 2)
+    held = updated_holding(held, (coeffs, queries0))
+    left = updated_left(left_part, sources[0], [query_grad], relation, vmem(*left_part.shape))
     relation_grad = relation_gradient(picked0, query_grad)
-    new_held, coeffs = held_meeting(rows1, held, relation, edges)
+    coeffs, queries, grad_a, relation_grad = first_half(first, held, relation, relation_grad)
+    new_held, coeffs = held_half(second, held, relation, coeffs, queries)
     arriving = moved(new_held, 6)
-    query_grad = query_gradient(coeffs, held)
-    relation_grad = relation_grad + relation_gradient(rows1[:edges], query_grad)
-    left = updated_left(left, sources[1], moved(query_grad, 2), relation, vmem(*left.shape))
+    grad_b = query_gradient(coeffs, held)
+    relation_grad = relation_grad + relation_gradient(second[:TE], grad_b)
+    grads = [moved(grad_a, 2), moved(grad_b, 2)]
+    left = updated_left(left, sources[1], grads, relation, vmem(*left.shape))
 
     held = arriving
     picked2 = picked_rows(left, tables[2])
     queries2 = queries_of(picked2, relation)
     base = picked_rows(left, tables[3])
     same = same_source(sources[3], sources[2])
-    coeffs, query_grad, picked3 = local_meeting(2, queries2, held, codes, relation, same, base)
-
-    rows3 = moved(picked3, 8)
-    held = updated_holding(held, coeffs, queries2)
-    left = updated_left(left, sources[2], query_grad, relation, vmem(*left.shape))
+    coeffs, query_grad, first, second = local_meeting(2, queries2, held, codes, relation, same, base)
+
+    first, second = moved(first, 8), moved(second, 8)
+    held = updated_holding(held, (coeffs, queries2))
+    left = updated_left(left, sources[2], [query_grad], relation, vmem(*left.shape))
     relation_grad = relation_grad + relation_gradient(picked2, query_grad)
-    pieces, coeffs, query_grad, queries3 = last_meeting(rows3, held, relation, relation_grad, edges)
+    coeffs_a, queries_a, grad_a, relation_grad = first_half(first, held, relation, relation_grad)
+    pieces, coeffs_b, grad_b, queries_b = last_half(second, held, relation, relation_grad)
     sums = shared_sums(pieces)
-    held = updated_holding(held, coeffs, queries3)
+    held = updated_holding(held, (coeffs_a, queries_a), (coeffs_b, queries_b))
     held = moved(held, 8)
+    grads = [moved(grad_a, 8), moved(grad_b, 8)]
     last = jax.ShapeDtypeStruct(left.shape, left.dtype)
-    left = updated_left(left, sources[3], moved(query_grad, 8), relation, last)
+    left = updated_left(left, sources[3], grads, relation, last)
     held = call(copy_kernel, jax.ShapeDtypeStruct(held.shape, held.dtype), held)
     relation, held, left = lax.optimization_barrier((relation, held, left))
     relation_out = call(finish_kernel, jax.ShapeDtypeStruct(relation.shape, jnp.float32), sums, relation)

time: 125 us -> 123 us (0.984)
  blocking collectives: 13.9 us -> 18.5 us
  waiting for transfers between devices: 51.5 us -> 47.1 us
  starting transfers between devices: 32.8 us -> 29 us
  Pallas kernels: 15.9 us -> 18.1 us
    all_to_all x1, blocking collectives: 13.9 us -> 18.5 us  [exchanged(): lax.all_to_all(pieces, axes, 0, 0, axis_index_groups=groups)]
    all_to_all x2, starting transfers between devices: 15.1 us -> 10.9 us  [exchanged(): lax.all_to_all(pieces, axes, 0, 0, axis_index_groups=groups)]
    all_to_all x2, waiting for transfers between devices: 12.3 us -> 9.71 us  [exchanged(): lax.all_to_all(pieces, axes, 0, 0, axis_index_groups=groups)]
    pallas_call x12 -> x14, Pallas kernels: 15.9 us -> 18.1 us  [call(): pl.pallas_call(kernel, out_shape=outs, in_specs=[spec] * len(args), out_s...]
    ppermute x7 -> x11, waiting for transfers between devices: 39.2 us -> 37.4 us  [moved(): return lax.ppermute(value, 'inner', pairs)]
    ppermute x7 -> x11, starting transfers between devices: 17.6 us -> 18.1 us  [moved(): return lax.ppermute(value, 'inner', pairs)]
    dot_general x13 -> x14, matrix products: 6.14 us -> 6.17 us  [dot(): lax.dot_general(a, b, (dims, ((), ())), preferred_element_type=jnp.float32)]
  transfers between devices with their start and end apart: 9 -> 13, of which waited for: 7 -> 8; matrix products, arithmetic and copies ran while one was open for 6% -> 7% of each run, Pallas kernels for 5% -> 9%
where the time goes in v6:
time: 123 us
  waiting for transfers between devices  47.1 us (38%)
  starting transfers between devices  29 us (24%)
  blocking collectives  18.5 us (15%)
  Pallas kernels  18.1 us (15%)
  matrix products  6.17 us (5%)
  local copies, waits for them, and re-layouts  2.04 us (2%)
    ppermute x11, waiting for transfers between devices, moved(): return lax.ppermute(value, 'inner', pairs)  37.4 us
    all_to_all x1, blocking collectives, exchanged(): lax.all_to_all(pieces, axes, 0, 0, axis_index_groups=groups)  18.5 us
    pallas_call x14, Pallas kernels, call(): pl.pallas_call(kernel, out_shape=outs, in_specs=[spec] * len(args), out_s...  18.1 us
    ppermute x11, starting transfers between devices, moved(): return lax.ppermute(value, 'inner', pairs)  18.1 us
    all_to_all x2, starting transfers between devices, exchanged(): lax.all_to_all(pieces, axes, 0, 0, axis_index_groups=groups)  10.9 us
    all_to_all x2, waiting for transfers between devices, exchanged(): lax.all_to_all(pieces, axes, 0, 0, axis_index_groups=groups)  9.71 us
    dot_general x14, matrix products, dot(): lax.dot_general(a, b, (dims, ((), ())), preferred_element_type=jnp.float32)  6.17 us
  transfers between devices with their start and end apart: 13, of which 8 were waited for; matrix products, arithmetic and copies ran while one was open for 7% of the time, Pallas kernels for 9%

profile of v6, /device:TPU:1, one launch (start us, length us, event | category | flops | bytes accessed | tf_op | source)
XLA Modules:
  0.0 123.0 jit_solution(3689430518332522136)
XLA Ops:
  0.6 2.5 %collective-permute-start = (bf16[1024,256]{1,0:T(8,128)(2,1)}, bf16[1024,256]{1,0:T(8,128)(2,1)S(1)}, u32[]{:S(2)}, u32[]{:S(2)}) collective-permute-start(bf16[1024,256]{1,0:T(8,128)(2,1)} %param.7), channel_id=1, source_target_pairs={{0,1},{1,0},{2,3},{3,2},{4,5},{5,4},{6,7},{7,6},{8,9},{9,8},{10,11... | collective-permute-start | bytes 1572872 | tf_op jit(solution)/shard_map/ppermute | solution.py:205
  5.5 1.6 %fusion.8 = bf16[512,256]{1,0:T(8,128)(2,1)S(1)} fusion(bf16[1024,256]{1,0:T(8,128)(2,1)} %left_ref.1, s32[512]{0:T(512)S(1)} %bitcast.55), kind=kOutput, calls=%fused_computation.15 | convolution fusion | flops 269090816 | bytes 788480 | tf_op jit(solution)/shard_map/dot_general | solution.py:20
  8.7 5.4 %collective-permute-done.held_ref = bf16[1024,256]{1,0:T(8,128)(2,1)S(1)} collective-permute-done((bf16[1024,256]{1,0:T(8,128)(2,1)}, bf16[1024,256]{1,0:T(8,128)(2,1)S(1)}, u32[]{:S(2)}, u32[]{:S(2)}) %collective-permute-start) | collective-permute-done | bytes 524320 | tf_op jit(solution)/shard_map/ppermute | solution.py:205
  14.1 2.3 %shard_map.85 = (bf16[1024,512]{1,0:T(8,128)(2,1)S(1)}, bf16[512,256]{1,0:T(8,128)(2,1)S(1)}, bf16[272,256]{1,0:T(8,128)(2,1)S(1)}, bf16[272,256]{1,0:T(8,128)(2,1)S(1)}) custom-call(bf16[512,256]{1,0:T(8,128)(2,1)S(1)} %convolution_convert_fusion.1.queries_ref, bf16[1024,256]{1,0:T(8,128)(2,1)S(1)} %collective-permute-done.held_ref, ...), custom_call_target="tpu_custom_call" | custom-call | tf_op jit(solution)/shard_map/pallas_call | solution.py:143
  16.4 3.9 %collective-permute-start.1 = (bf16[272,256]{1,0:T(8,128)(2,1)S(1)}, bf16[272,256]{1,0:T(8,128)(2,1)S(1)}, u32[]{:S(2)}, u32[]{:S(2)}) collective-permute-start(bf16[272,256]{1,0:T(8,128)(2,1)S(1)} %get-tuple-element.28), channel_id=1, source_target_pairs={{0,2},{1,3},{2,0},{3,1},{4,6},{5,7},{6,4},{7,5},{8,10},{9,11},{10,... | collective-permute-start | bytes 417800 | tf_op jit(solution)/shard_map/ppermute | solution.py:205
  22.0 10.4 %collective-permute-done.2.picked_ref = bf16[272,256]{1,0:T(8,128)(2,1)S(1)} collective-permute-done((bf16[272,256]{1,0:T(8,128)(2,1)S(1)}, bf16[272,256]{1,0:T(8,128)(2,1)S(1)}, u32[]{:S(2)}, u32[]{:S(2)}) %collective-permute-start.2) | collective-permute-done | bytes 139296 | tf_op jit(solution)/shard_map/ppermute | solution.py:205
  32.3 1.6 %shard_map.86 = (bf16[1024,256]{1,0:T(8,128)(2,1)S(1)}, bf16[256,256]{1,0:T(8,128)(2,1)S(1)}, bf16[256,256]{1,0:T(8,128)(2,1)S(1)}, f32[256,256]{1,0:T(8,128)S(1)}) custom-call(bf16[272,256]{1,0:T(8,128)(2,1)S(1)} %collective-permute-done.2.picked_ref, bf16[1024,256]{1,0:T(8,128)(2,1)S(1)} %subtract_convert_fusion.2.held_ref, bf16[256,256]{1,0:T(8,128)(2,1)S(1)} %copy-done, ...), custom_call_target="tpu_custom_call" | custom-call | tf_op jit(solution)/shard_map/pallas_call | solution.py:143
  34.1 1.5 %shard_map.87 = (bf16[1024,256]{1,0:T(8,128)(2,1)S(1)}, bf16[1024,256]{1,0:T(8,128)(2,1)S(1)}) custom-call(bf16[272,256]{1,0:T(8,128)(2,1)S(1)} %collective-permute-done.1.picked_ref, bf16[1024,256]{1,0:T(8,128)(2,1)S(1)} %subtract_convert_fusion.2.held_ref, bf16[256,256]{1,0:T(8,128)(2,1)S(1)} %copy-done, ...), custom_call_target="tpu_custom_call" | custom-call | tf_op jit(solution)/shard_map/pallas_call | solution.py:143
  35.9 2.4 %collective-permute-start.5 = (bf16[256,256]{1,0:T(8,128)(2,1)S(1)}, bf16[256,256]{1,0:T(8,128)(2,1)S(1)}, u32[]{:S(2)}, u32[]{:S(2)}) collective-permute-start(bf16[256,256]{1,0:T(8,128)(2,1)S(1)} %fusion.9), channel_id=1, source_target_pairs={{0,2},{1,3},{2,0},{3,1},{4,6},{5,7},{6,4},{7,5},{8,10},{9,11},{10,... | collective-permute-start | bytes 393224 | tf_op jit(solution)/shard_map/ppermute | solution.py:205
  38.3 4.7 %collective-permute-start.3 = (bf16[1024,256]{1,0:T(8,128)(2,1)S(1)}, bf16[1024,256]{1,0:T(8,128)(2,1)S(1)}, u32[]{:S(2)}, u32[]{:S(2)}) collective-permute-start(bf16[1024,256]{1,0:T(8,128)(2,1)S(1)} %get-tuple-element.34), channel_id=1, source_target_pairs={{0,6},{1,7},{2,4},{3,5},{4,2},{5,3},{6,0},{7,1},{8,14},{9,15},{10,... | collective-permute-start | bytes 1572872 | tf_op jit(solution)/shard_map/ppermute | solution.py:205
  43.2 4.3 %collective-permute-done.5.refs_1_ = bf16[256,256]{1,0:T(8,128)(2,1)S(1)} collective-permute-done((bf16[256,256]{1,0:T(8,128)(2,1)S(1)}, bf16[256,256]{1,0:T(8,128)(2,1)S(1)}, u32[]{:S(2)}, u32[]{:S(2)}) %collective-permute-start.5) | collective-permute-done | bytes 131104 | tf_op jit(solution)/shard_map/ppermute | solution.py:205
  49.7 14.8 %collective-permute-done.3.held_ref = bf16[1024,256]{1,0:T(8,128)(2,1)S(1)} collective-permute-done((bf16[1024,256]{1,0:T(8,128)(2,1)S(1)}, bf16[1024,256]{1,0:T(8,128)(2,1)S(1)}, u32[]{:S(2)}, u32[]{:S(2)}) %collective-permute-start.3) | collective-permute-done | bytes 524320 | tf_op jit(solution)/shard_map/ppermute | solution.py:205
  64.5 2.3 %shard_map.90 = (bf16[1024,512]{1,0:T(8,128)(2,1)S(1)}, bf16[512,256]{1,0:T(8,128)(2,1)S(1)}, bf16[272,256]{1,0:T(8,128)(2,1)S(1)}, bf16[272,256]{1,0:T(8,128)(2,1)S(1)}) custom-call(bf16[512,256]{1,0:T(8,128)(2,1)S(1)} %convolution_convert_fusion.queries_ref, bf16[1024,256]{1,0:T(8,128)(2,1)S(1)} %collective-permute-done.3.held_ref, ...), custom_call_target="tpu_custom_call" | custom-call | tf_op jit(solution)/shard_map/pallas_call | solution.py:143
  69.1 1.7 %collective-permute-done.6.picked_ref = bf16[272,256]{1,0:T(8,128)(2,1)S(1)} collective-permute-done((bf16[272,256]{1,0:T(8,128)(2,1)S(1)}, bf16[272,256]{1,0:T(8,128)(2,1)S(1)}, u32[]{:S(2)}, u32[]{:S(2)}) %collective-permute-start.6) | collective-permute-done | bytes 139296 | tf_op jit(solution)/shard_map/ppermute | solution.py:205
  70.8 1.6 %shard_map.91 = (bf16[1024,256]{1,0:T(8,128)(2,1)S(1)}, bf16[256,256]{1,0:T(8,128)(2,1)S(1)}, bf16[256,256]{1,0:T(8,128)(2,1)S(1)}, f32[256,256]{1,0:T(8,128)S(1)}) custom-call(bf16[272,256]{1,0:T(8,128)(2,1)S(1)} %collective-permute-done.6.picked_ref, bf16[1024,256]{1,0:T(8,128)(2,1)S(1)} %subtract_convert_fusion.1.held_ref, bf16[256,256]{1,0:T(8,128)(2,1)S(1)} %copy-done, ...), custom_call_target="tpu_custom_call" | custom-call | tf_op jit(solution)/shard_map/pallas_call | solution.py:143
  73.2 1.6 %shard_map.92 = (bf16[512,128]{1,0:T(8,128)(2,1)S(1)}, bf16[1024,256]{1,0:T(8,128)(2,1)S(1)}, bf16[256,256]{1,0:T(8,128)(2,1)S(1)}, bf16[256,256]{1,0:T(8,128)(2,1)S(1)}) custom-call(bf16[272,256]{1,0:T(8,128)(2,1)S(1)} %collective-permute-done.7.picked_ref, bf16[1024,256]{1,0:T(8,128)(2,1)S(1)} %subtract_convert_fusion.1.held_ref, ...), custom_call_target="tpu_custom_call" | custom-call | tf_op jit(solution)/shard_map/pallas_call | solution.py:143
  75.5 1.4 %collective-permute-start.8 = (bf16[1024,256]{1,0:T(8,128)(2,1)S(1)}, bf16[1024,256]{1,0:T(8,128)(2,1)S(1)}, u32[]{:S(2)}, u32[]{:S(2)}) collective-permute-start(bf16[1024,256]{1,0:T(8,128)(2,1)S(1)} %subtract_convert_fusion), channel_id=1, source_target_pairs={{0,8},{1,9},{2,10},{3,11},{4,12},{5,13},{6,14},{7,15},{8,0},{9,1},... | collective-permute-start | bytes 1572872 | tf_op jit(solution)/shard_map/ppermute | solution.py:205
  76.9 18.5 %all_to_all.15 = bf16[32,16,128]{2,1,0:T(8,128)(2,1)S(1)} all-to-all(bf16[32,16,128]{2,1,0:T(8,128)(2,1)S(1)} %bitcast.48), channel_id=1, replica_groups={{0,8,16,24,32,40,48,56,64,72,80,88,96,104,112,120,128,136,144,152,160,1..., dimensions={0} | all-to-all | bytes 262144 | tf_op jit(solution)/shard_map/all_to_all | solution.py:187
  96.0 5.7 %all-to-all-start.1 = ((bf16[8,16,128]{2,1,0:T(8,128)(2,1)}), bf16[8,16,128]{2,1,0:T(8,128)(2,1)S(1)}, u32[]{:S(2)}, u32[]{:S(2)}) async-start(bf16[8,16,128]{2,1,0:T(8,128)(2,1)} %bitcast.12), calls=%async_computation.1 | async-start | bytes 65536 | tf_op jit(solution)/shard_map/all_to_all | solution.py:187
  101.7 1.5 %collective-permute-start.10 = (bf16[256,256]{1,0:T(8,128)(2,1)S(1)}, bf16[256,256]{1,0:T(8,128)(2,1)S(1)}, u32[]{:S(2)}, u32[]{:S(2)}) collective-permute-start(bf16[256,256]{1,0:T(8,128)(2,1)S(1)} %get-tuple-element.48), channel_id=1, source_target_pairs={{0,8},{1,9},{2,10},{3,11},{4,12},{5,13},{6,14},{7,15},{8,0},{9,1},... | collective-permute-start | bytes 393224 | tf_op jit(solution)/shard_map/ppermute | solution.py:205
  103.2 5.4 %all-to-all-done.1 = bf16[8,16,128]{2,1,0:T(8,128)(2,1)S(1)} async-done(((bf16[8,16,128]{2,1,0:T(8,128)(2,1)}), bf16[8,16,128]{2,1,0:T(8,128)(2,1)S(1)}, u32[]{:S(2)}, u32[]{:S(2)}) %all-to-all-start.1) | async-done | bytes 32800 | tf_op jit(solution)/shard_map/all_to_all | solution.py:187
  109.3 5.2 %all-to-all-start.2 = ((bf16[32,16,128]{2,1,0:T(8,128)(2,1)}), bf16[32,16,128]{2,1,0:T(8,128)(2,1)S(1)}, u32[]{:S(2)}, u32[]{:S(2)}) async-start(bf16[32,16,128]{2,1,0:T(8,128)(2,1)} %bitcast.14), calls=%async_computation.2 | async-start | bytes 262144 | tf_op jit(solution)/shard_map/all_to_all | solution.py:187
  115.4 1.7 %shard_map.95 = bf16[1024,256]{1,0:T(8,128)(2,1)} custom-call(bf16[1024,256]{1,0:T(8,128)(2,1)S(1)} %shard_map.94.left_ref, s32[1,512]{1,0:T(1,128)S(1)} %get-tuple-element.55.source_ref, bf16[256,256]{1,0:T(8,128)(2,1)S(1)} %copy-done, bf16[256,256]{1,0:T(8,128)(2,1)S(1)} %collective-permute-done.9.refs_0_, bf16[256,256]{1,0:T(8,128)(2,1)S(1)} %collective-permute-done.10.refs_1_), custom_call_target="tpu_custom_call" | custom-call | tf_op jit(solution)/shard_map/pallas_call | solution.py:143
  117.9 4.3 %all-to-all-done.2 = bf16[32,16,128]{2,1,0:T(8,128)(2,1)S(1)} async-done(((bf16[32,16,128]{2,1,0:T(8,128)(2,1)}), bf16[32,16,128]{2,1,0:T(8,128)(2,1)S(1)}, u32[]{:S(2)}, u32[]{:S(2)}) %all-to-all-start.2) | async-done | bytes 131104 | tf_op jit(solution)/shard_map/all_to_all | solution.py:187
  (43 shorter events, 15.8 us)
Async XLA Ops:
  0.6 13.5 %collective-permute-start = (bf16[1024,256]{1,0:T(8,128)(2,1)}, bf16[1024,256]{1,0:T(8,128)(2,1)S(1)}, u32[]{:S(2)}, u32[]{:S(2)}) collective-permute-start(bf16[1024,256]{1,0:T(8,128)(2,1)} %param.7), channel_id=1, source_target_pairs={{0,1},{1,0},{2,3},{3,2},{4,5},{5,4},{6,7},{7,6},{8,9},{9,8},{10,11... | collective-permute-start | bytes 1572872 | tf_op jit(solution)/shard_map/ppermute | solution.py:205
  5.5 2.0 %copy-start = (bf16[256,256]{1,0:T(8,128)(2,1)S(1)}, bf16[256,256]{1,0:T(8,128)(2,1)}, u32[]{:S(2)}) copy-start(bf16[256,256]{1,0:T(8,128)(2,1)} %relation_ref.20) | copy-start | bytes 393220
  7.1 1.0 copy-start.1
  16.4 17.7 %collective-permute-start.1 = (bf16[272,256]{1,0:T(8,128)(2,1)S(1)}, bf16[272,256]{1,0:T(8,128)(2,1)S(1)}, u32[]{:S(2)}, u32[]{:S(2)}) collective-permute-start(bf16[272,256]{1,0:T(8,128)(2,1)S(1)} %get-tuple-element.28), channel_id=1, source_target_pairs={{0,2},{1,3},{2,0},{3,1},{4,6},{5,7},{6,4},{7,5},{8,10},{9,11},{10,... | collective-permute-start | bytes 417800 | tf_op jit(solution)/shard_map/ppermute | solution.py:205
  20.3 12.1 %collective-permute-start.2 = (bf16[272,256]{1,0:T(8,128)(2,1)S(1)}, bf16[272,256]{1,0:T(8,128)(2,1)S(1)}, u32[]{:S(2)}, u32[]{:S(2)}) collective-permute-start(bf16[272,256]{1,0:T(8,128)(2,1)S(1)} %get-tuple-element.30), channel_id=1, source_target_pairs={{0,2},{1,3},{2,0},{3,1},{4,6},{5,7},{6,4},{7,5},{8,10},{9,11},{10,... | collective-permute-start | bytes 417800 | tf_op jit(solution)/shard_map/ppermute | solution.py:205
  34.0 9.3 %collective-permute-start.4 = (bf16[256,256]{1,0:T(8,128)(2,1)S(1)}, bf16[256,256]{1,0:T(8,128)(2,1)S(1)}, u32[]{:S(2)}, u32[]{:S(2)}) collective-permute-start(bf16[256,256]{1,0:T(8,128)(2,1)S(1)} %get-tuple-element.35), channel_id=1, source_target_pairs={{0,2},{1,3},{2,0},{3,1},{4,6},{5,7},{6,4},{7,5},{8,10},{9,11},{10,... | collective-permute-start | bytes 393224 | tf_op jit(solution)/shard_map/ppermute | solution.py:205
  35.9 11.6 %collective-permute-start.5 = (bf16[256,256]{1,0:T(8,128)(2,1)S(1)}, bf16[256,256]{1,0:T(8,128)(2,1)S(1)}, u32[]{:S(2)}, u32[]{:S(2)}) collective-permute-start(bf16[256,256]{1,0:T(8,128)(2,1)S(1)} %fusion.9), channel_id=1, source_target_pairs={{0,2},{1,3},{2,0},{3,1},{4,6},{5,7},{6,4},{7,5},{8,10},{9,11},{10,... | collective-permute-start | bytes 393224 | tf_op jit(solution)/shard_map/ppermute | solution.py:205
  38.3 26.2 %collective-permute-start.3 = (bf16[1024,256]{1,0:T(8,128)(2,1)S(1)}, bf16[1024,256]{1,0:T(8,128)(2,1)S(1)}, u32[]{:S(2)}, u32[]{:S(2)}) collective-permute-start(bf16[1024,256]{1,0:T(8,128)(2,1)S(1)} %get-tuple-element.34), channel_id=1, source_target_pairs={{0,6},{1,7},{2,4},{3,5},{4,2},{5,3},{6,0},{7,1},{8,14},{9,15},{10,... | collective-permute-start | bytes 1572872 | tf_op jit(solution)/shard_map/ppermute | solution.py:205
  66.8 4.0 %collective-permute-start.6 = (bf16[272,256]{1,0:T(8,128)(2,1)S(1)}, bf16[272,256]{1,0:T(8,128)(2,1)S(1)}, u32[]{:S(2)}, u32[]{:S(2)}) collective-permute-start(bf16[272,256]{1,0:T(8,128)(2,1)S(1)} %get-tuple-element.38), channel_id=1, source_target_pairs={{0,8},{1,9},{2,10},{3,11},{4,12},{5,13},{6,14},{7,15},{8,0},{9,1},... | collective-permute-start | bytes 417800 | tf_op jit(solution)/shard_map/ppermute | solution.py:205
  68.1 5.1 %collective-permute-start.7 = (bf16[272,256]{1,0:T(8,128)(2,1)S(1)}, bf16[272,256]{1,0:T(8,128)(2,1)S(1)}, u32[]{:S(2)}, u32[]{:S(2)}) collective-permute-start(bf16[272,256]{1,0:T(8,128)(2,1)S(1)} %get-tuple-element.43), channel_id=1, source_target_pairs={{0,8},{1,9},{2,10},{3,11},{4,12},{5,13},{6,14},{7,15},{8,0},{9,1},... | collective-permute-start | bytes 417800 | tf_op jit(solution)/shard_map/ppermute | solution.py:205
  75.5 41.6 %collective-permute-start.8 = (bf16[1024,256]{1,0:T(8,128)(2,1)S(1)}, bf16[1024,256]{1,0:T(8,128)(2,1)S(1)}, u32[]{:S(2)}, u32[]{:S(2)}) collective-permute-start(bf16[1024,256]{1,0:T(8,128)(2,1)S(1)} %subtract_convert_fusion), channel_id=1, source_target_pairs={{0,8},{1,9},{2,10},{3,11},{4,12},{5,13},{6,14},{7,15},{8,0},{9,1},... | collective-permute-start | bytes 1572872 | tf_op jit(solution)/shard_map/ppermute | solution.py:205
  96.0 12.6 %all-to-all-start.1 = ((bf16[8,16,128]{2,1,0:T(8,128)(2,1)}), bf16[8,16,128]{2,1,0:T(8,128)(2,1)S(1)}, u32[]{:S(2)}, u32[]{:S(2)}) async-start(bf16[8,16,128]{2,1,0:T(8,128)(2,1)} %bitcast.12), calls=%async_computation.1 | async-start | bytes 65536 | tf_op jit(solution)/shard_map/all_to_all | solution.py:187
  101.7 13.7 %collective-permute-start.9 = (bf16[256,256]{1,0:T(8,128)(2,1)S(1)}, bf16[256,256]{1,0:T(8,128)(2,1)S(1)}, u32[]{:S(2)}, u32[]{:S(2)}) collective-permute-start(bf16[256,256]{1,0:T(8,128)(2,1)S(1)} %get-tuple-element.47), channel_id=1, source_target_pairs={{0,8},{1,9},{2,10},{3,11},{4,12},{5,13},{6,14},{7,15},{8,0},{9,1},... | collective-permute-start | bytes 393224 | tf_op jit(solution)/shard_map/ppermute | solution.py:205
  101.7 13.7 %collective-permute-start.10 = (bf16[256,256]{1,0:T(8,128)(2,1)S(1)}, bf16[256,256]{1,0:T(8,128)(2,1)S(1)}, u32[]{:S(2)}, u32[]{:S(2)}) collective-permute-start(bf16[256,256]{1,0:T(8,128)(2,1)S(1)} %get-tuple-element.48), channel_id=1, source_target_pairs={{0,8},{1,9},{2,10},{3,11},{4,12},{5,13},{6,14},{7,15},{8,0},{9,1},... | collective-permute-start | bytes 393224 | tf_op jit(solution)/shard_map/ppermute | solution.py:205
  109.3 12.9 %all-to-all-start.2 = ((bf16[32,16,128]{2,1,0:T(8,128)(2,1)}), bf16[32,16,128]{2,1,0:T(8,128)(2,1)S(1)}, u32[]{:S(2)}, u32[]{:S(2)}) async-start(bf16[32,16,128]{2,1,0:T(8,128)(2,1)} %bitcast.14), calls=%async_computation.2 | async-start | bytes 262144 | tf_op jit(solution)/shard_map/all_to_all | solution.py:187

commit v7 on v5

--- a/solution.py
+++ b/solution.py
@@ -81,12 +81,22 @@
     next_ref[:edges, :] = (base_ref[...].astype(jnp.float32) - LR_EMBED * change).astype(jnp.bfloat16)
 
 
-def held_kernel(picked_ref, held_ref, relation_ref, new_ref, coeffs_ref, scores_ref):
+def coeffs_of(picked_ref, held_ref, relation_ref, coeffs_ref, scores_ref, then):
     edges = coeffs_ref.shape[1]
     queries = dot(picked_ref[:edges, :], relation_ref[...], ((1,), (0,))).astype(jnp.bfloat16)
-    meeting_body(queries, held_ref, picked_ref, edges, coeffs_ref, scores_ref, lambda part: None)
+    meeting_body(queries, held_ref, picked_ref, edges, coeffs_ref, scores_ref, then)
+    return queries
+
+
+def held_kernel(picked_ref, held_ref, relation_ref, new_ref, scores_ref, coeffs_ref):
+    queries = coeffs_of(picked_ref, held_ref, relation_ref, coeffs_ref, scores_ref, lambda part: None)
     held_grad = dot(coeffs_ref[...], queries, ((1,), (0,)))
     new_ref[...] = (held_ref[...].astype(jnp.float32) - (LR_EMBED * SCORE_SCALE) * held_grad).astype(jnp.bfloat16)
+
+
+def grad_kernel(picked_ref, held_ref, relation_ref, grad_ref, scores_ref, coeffs_ref):
+    then = lambda part: fill_gradient(coeffs_ref, held_ref, grad_ref, part)
+    coeffs_of(picked_ref, held_ref, relation_ref, coeffs_ref, scores_ref, then)
 
 
 def last_kernel(picked_ref, held_ref, relation_ref, before_ref, pieces_ref, coeffs_ref, grad_ref, queries_ref, scores_ref):
@@ -159,10 +169,19 @@
     return call(functools.partial(local_kernel, meeting), outs, queries, held, codes, relation, same, base, scratch=scratch)
 
 
-def held_meeting(picked, held, relation, edges):
-    rows, width = held.shape
-    outs = (vmem(rows, width), vmem(rows, edges))
-    return call(held_kernel, outs, picked, held, relation, scratch=[VM((rows, edges), jnp.float32)])
+def row_kernel(kernel, out, picked, held, relation):
+    rows, edges = held.shape[0], picked.shape[0] - CODE_ROWS
+    scratch = [VM((rows, edges), jnp.float32), vmem(rows, edges)]
+    return call(kernel, out, picked, held, relation, scratch=scratch)
+
+
+def replayed(picked, held, relation):
+    return row_kernel(held_kernel, vmem(*held.shape), picked, held, relation)
+
+
+def gradient_at_host(picked, held, relation):
+    out = vmem(picked.shape[0] - CODE_ROWS, held.shape[1])
+    return row_kernel(grad_kernel, out, picked, held, relation)
 
 
 def last_meeting(picked, held, relation, before, edges):
@@ -217,10 +236,6 @@
     return (holding.astype(jnp.float32) - (LR_EMBED * SCORE_SCALE) * held_grad).astype(jnp.bfloat16)
 
 
-def query_gradient(coeffs, holding):
-    return (dot(coeffs, holding, ((0,), (0,))) * SCORE_SCALE).astype(jnp.bfloat16)
-
-
 def relation_gradient(picked, query_grad):
     return dot(picked, query_grad, ((0,), (0,)))
 
@@ -243,11 +258,13 @@
     sources = src_index[0]
 
     held = moved(right_part, 1)
+    far = moved(right_part, 7)
     slots = jnp.arange(edges, dtype=jnp.int32)
     targets = jnp.where(slots[None, :] < lengths[0][:, None], dst_index[0], -1)
     codes = coded(targets)
     tables = [source_table(sources[meeting], rows) for meeting in range(4)]
     picked0 = picked_rows(left_part, tables[0])
+    rows0 = moved(jnp.concatenate([picked0, codes[:CODE_ROWS]], axis=0), 6)
     queries0 = queries_of(picked0, relation)
     base = picked_rows(left_part, tables[1])
     same = same_source(sources[1], sources[0])
@@ -257,13 +274,13 @@
     held = updated_holding(held, coeffs, queries0)
     left = updated_left(left_part, sources[0], query_grad, relation, vmem(*left_part.shape))
     relation_grad = relation_gradient(picked0, query_grad)
-    new_held, coeffs = held_meeting(rows1, held, relation, edges)
-    arriving = moved(new_held, 6)
-    query_grad = query_gradient(coeffs, held)
+    query_grad = gradient_at_host(rows1, held, relation)
+    back1 = moved(query_grad, 2)
+    onward = moved(rows1, 6)
     relation_grad = relation_grad + relation_gradient(rows1[:edges], query_grad)
-    left = updated_left(left, sources[1], moved(query_grad, 2), relation, vmem(*left.shape))
-
-    held = arriving
+    left = updated_left(left, sources[1], back1, relation, vmem(*left.shape))
+
+    held = replayed(onward, replayed(rows0, far, relation), relation)
     picked2 = picked_rows(left, tables[2])
     queries2 = queries_of(picked2, relation)
     base = picked_rows(left, tables[3])

time: 125 us -> 126 us (level)
  waiting for transfers between devices: 51.5 us -> 56.8 us
  blocking collectives: 13.9 us -> 9.24 us
  Pallas kernels: 15.9 us -> 18.5 us
    all_to_all x1, blocking collectives: 13.9 us -> 9.24 us  [exchanged(): lax.all_to_all(pieces, axes, 0, 0, axis_index_groups=groups)]
    ppermute x7 -> x9, waiting for transfers between devices: 39.2 us -> 42.5 us  [moved(): return lax.ppermute(value, 'inner', pairs)]
    pallas_call x12 -> x14, Pallas kernels: 15.9 us -> 18.5 us  [call(): pl.pallas_call(kernel, out_shape=outs, in_specs=[spec] * len(args), out_s...]
    all_to_all x2, waiting for transfers between devices: 12.3 us -> 14.3 us  [exchanged(): lax.all_to_all(pieces, axes, 0, 0, axis_index_groups=groups)]
    dot_general x13 -> x12, matrix products: 6.14 us -> 5.65 us  [dot(): lax.dot_general(a, b, (dims, ((), ())), preferred_element_type=jnp.float32)]
    ppermute x7 -> x9, starting transfers between devices: 17.6 us -> 17.6 us  [moved(): return lax.ppermute(value, 'inner', pairs)]
  transfers between devices with their start and end apart: 9 -> 11, of which waited for: 7 -> 8; matrix products, arithmetic and copies ran while one was open for 6% -> 6% of each run, Pallas kernels for 5% -> 8%
where the time goes in v7:
time: 126 us
  waiting for transfers between devices  56.8 us (45%)
  starting transfers between devices  31.7 us (25%)
  Pallas kernels  18.5 us (15%)
  blocking collectives  9.24 us (7%)
  matrix products  5.65 us (4%)
  local copies, waits for them, and re-layouts  1.93 us (2%)
    ppermute x9, waiting for transfers between devices, moved(): return lax.ppermute(value, 'inner', pairs)  42.5 us
    pallas_call x14, Pallas kernels, call(): pl.pallas_call(kernel, out_shape=outs, in_specs=[spec] * len(args), out_s...  18.5 us
    ppermute x9, starting transfers between devices, moved(): return lax.ppermute(value, 'inner', pairs)  17.6 us
    all_to_all x2, waiting for transfers between devices, exchanged(): lax.all_to_all(pieces, axes, 0, 0, axis_index_groups=groups)  14.3 us
    all_to_all x2, starting transfers between devices, exchanged(): lax.all_to_all(pieces, axes, 0, 0, axis_index_groups=groups)  14 us
    all_to_all x1, blocking collectives, exchanged(): lax.all_to_all(pieces, axes, 0, 0, axis_index_groups=groups)  9.24 us
    dot_general x12, matrix products, dot(): lax.dot_general(a, b, (dims, ((), ())), preferred_element_type=jnp.float32)  5.65 us
  transfers between devices with their start and end apart: 11, of which 8 were waited for; matrix products, arithmetic and copies ran while one was open for 6% of the time, Pallas kernels for 8%

profile of v7, /device:TPU:1, one launch (start us, length us, event | category | flops | bytes accessed | tf_op | source)
XLA Modules:
  0.0 125.8 jit_solution(16507347873952705426)
XLA Ops:
  0.6 6.5 %collective-permute-start.4 = (bf16[1024,256]{1,0:T(8,128)(2,1)}, bf16[1024,256]{1,0:T(8,128)(2,1)S(1)}, u32[]{:S(2)}, u32[]{:S(2)}) collective-permute-start(bf16[1024,256]{1,0:T(8,128)(2,1)} %param.7), channel_id=1, source_target_pairs={{0,7},{1,6},{2,5},{3,4},{4,3},{5,2},{6,1},{7,0},{8,15},{9,14},{10,... | collective-permute-start | bytes 1572872 | tf_op jit(solution)/shard_map/ppermute | solution.py:215
  7.1 1.6 %collective-permute-start = (bf16[1024,256]{1,0:T(8,128)(2,1)}, bf16[1024,256]{1,0:T(8,128)(2,1)S(1)}, u32[]{:S(2)}, u32[]{:S(2)}) collective-permute-start(bf16[1024,256]{1,0:T(8,128)(2,1)} %param.7), channel_id=1, source_target_pairs={{0,1},{1,0},{2,3},{3,2},{4,5},{5,4},{6,7},{7,6},{8,9},{9,8},{10,11... | collective-permute-start | bytes 1572872 | tf_op jit(solution)/shard_map/ppermute | solution.py:215
  11.1 1.6 %fusion.7 = bf16[512,256]{1,0:T(8,128)(2,1)S(1)} fusion(bf16[1024,256]{1,0:T(8,128)(2,1)} %left_ref.1, s32[512]{0:T(512)S(1)} %bitcast.53), kind=kOutput, calls=%fused_computation.14 | convolution fusion | flops 269090816 | bytes 788480 | tf_op jit(solution)/shard_map/dot_general | solution.py:20
  14.3 17.3 %collective-permute-done.held_ref = bf16[1024,256]{1,0:T(8,128)(2,1)S(1)} collective-permute-done((bf16[1024,256]{1,0:T(8,128)(2,1)}, bf16[1024,256]{1,0:T(8,128)(2,1)S(1)}, u32[]{:S(2)}, u32[]{:S(2)}) %collective-permute-start) | collective-permute-done | bytes 524320 | tf_op jit(solution)/shard_map/ppermute | solution.py:215
  31.6 2.3 %shard_map.85 = (bf16[1024,512]{1,0:T(8,128)(2,1)S(1)}, bf16[512,256]{1,0:T(8,128)(2,1)S(1)}, bf16[528,256]{1,0:T(8,128)(2,1)S(1)}) custom-call(bf16[512,256]{1,0:T(8,128)(2,1)S(1)} %convolution_convert_fusion.1.queries_ref, bf16[1024,256]{1,0:T(8,128)(2,1)S(1)} %collective-permute-done.held_ref, bf16[64,256]{1,0:T(8,128)(2,1)S(1)} %bitcast.43, ...), custom_call_target="tpu_custom_call" | custom-call | tf_op jit(solution)/shard_map/pallas_call | solution.py:151
  34.0 2.0 %collective-permute-start.1 = (bf16[528,256]{1,0:T(8,128)(2,1)S(1)}, bf16[528,256]{1,0:T(8,128)(2,1)S(1)}, u32[]{:S(2)}, u32[]{:S(2)}) collective-permute-start(bf16[528,256]{1,0:T(8,128)(2,1)S(1)} %get-tuple-element.16), channel_id=1, source_target_pairs={{0,2},{1,3},{2,0},{3,1},{4,6},{5,7},{6,4},{7,5},{8,10},{9,11},{10,... | collective-permute-start | bytes 811016 | tf_op jit(solution)/shard_map/ppermute | solution.py:215
  36.8 3.9 %collective-permute-done.3.picked_ref = bf16[528,256]{1,0:T(8,128)(2,1)S(1)} collective-permute-done((bf16[528,256]{1,0:T(8,128)(2,1)S(1)}, bf16[528,256]{1,0:T(8,128)(2,1)S(1)}, u32[]{:S(2)}, u32[]{:S(2)}) %collective-permute-start.3) | collective-permute-done | bytes 270368 | tf_op jit(solution)/shard_map/ppermute | solution.py:215
  40.8 1.5 %shard_map.86.held_ref = bf16[1024,256]{1,0:T(8,128)(2,1)S(1)} custom-call(bf16[528,256]{1,0:T(8,128)(2,1)S(1)} %collective-permute-done.3.picked_ref, bf16[1024,256]{1,0:T(8,128)(2,1)S(1)} %collective-permute-done.4.held_ref, bf16[256,256]{1,0:T(8,128)(2,1)S(1)} %copy-done), custom_call_target="tpu_custom_call" | custom-call | tf_op jit(solution)/shard_map/pallas_call | solution.py:151
  42.7 3.6 %collective-permute-done.1.picked_ref = bf16[528,256]{1,0:T(8,128)(2,1)S(1)} collective-permute-done((bf16[528,256]{1,0:T(8,128)(2,1)S(1)}, bf16[528,256]{1,0:T(8,128)(2,1)S(1)}, u32[]{:S(2)}, u32[]{:S(2)}) %collective-permute-start.1) | collective-permute-done | bytes 270368 | tf_op jit(solution)/shard_map/ppermute | solution.py:215
  46.3 1.5 %shard_map.89 = bf16[512,256]{1,0:T(8,128)(2,1)S(1)} custom-call(bf16[528,256]{1,0:T(8,128)(2,1)S(1)} %collective-permute-done.1.picked_ref, bf16[1024,256]{1,0:T(8,128)(2,1)S(1)} %subtract_convert_fusion.2.held_ref, bf16[256,256]{1,0:T(8,128)(2,1)S(1)} %copy-done), custom_call_target="tpu_custom_call" | custom-call | tf_op jit(solution)/shard_map/pallas_call | solution.py:151
  47.8 3.2 %collective-permute-start.5 = (bf16[512,256]{1,0:T(8,128)(2,1)S(1)}, bf16[512,256]{1,0:T(8,128)(2,1)S(1)}, u32[]{:S(2)}, u32[]{:S(2)}) collective-permute-start(bf16[512,256]{1,0:T(8,128)(2,1)S(1)} %shard_map.89), channel_id=1, source_target_pairs={{0,2},{1,3},{2,0},{3,1},{4,6},{5,7},{6,4},{7,5},{8,10},{9,11},{10,... | collective-permute-start | bytes 786440 | tf_op jit(solution)/shard_map/ppermute | solution.py:215
  51.8 9.6 %collective-permute-done.5.grad_ref = bf16[512,256]{1,0:T(8,128)(2,1)S(1)} collective-permute-done((bf16[512,256]{1,0:T(8,128)(2,1)S(1)}, bf16[512,256]{1,0:T(8,128)(2,1)S(1)}, u32[]{:S(2)}, u32[]{:S(2)}) %collective-permute-start.5) | collective-permute-done | bytes 262176 | tf_op jit(solution)/shard_map/ppermute | solution.py:215
  63.5 2.8 %collective-permute-done.2.picked_ref = bf16[528,256]{1,0:T(8,128)(2,1)S(1)} collective-permute-done((bf16[528,256]{1,0:T(8,128)(2,1)S(1)}, bf16[528,256]{1,0:T(8,128)(2,1)S(1)}, u32[]{:S(2)}, u32[]{:S(2)}) %collective-permute-start.2) | collective-permute-done | bytes 270368 | tf_op jit(solution)/shard_map/ppermute | solution.py:215
  66.4 1.5 %shard_map.87.held_ref = bf16[1024,256]{1,0:T(8,128)(2,1)S(1)} custom-call(bf16[528,256]{1,0:T(8,128)(2,1)S(1)} %collective-permute-done.2.picked_ref, bf16[1024,256]{1,0:T(8,128)(2,1)S(1)} %shard_map.86.held_ref, bf16[256,256]{1,0:T(8,128)(2,1)S(1)} %copy-done), custom_call_target="tpu_custom_call" | custom-call | tf_op jit(solution)/shard_map/pallas_call | solution.py:151
  67.9 2.3 %shard_map.91 = (bf16[1024,512]{1,0:T(8,128)(2,1)S(1)}, bf16[512,256]{1,0:T(8,128)(2,1)S(1)}, bf16[528,256]{1,0:T(8,128)(2,1)S(1)}) custom-call(bf16[512,256]{1,0:T(8,128)(2,1)S(1)} %convolution_convert_fusion.queries_ref, bf16[1024,256]{1,0:T(8,128)(2,1)S(1)} %shard_map.87.held_ref, bf16[64,256]{1,0:T(8,128)(2,1)S(1)} %bitcast.44, ...), custom_call_target="tpu_custom_call" | custom-call | tf_op jit(solution)/shard_map/pallas_call | solution.py:151
  72.2 5.2 %collective-permute-done.6.picked_ref = bf16[528,256]{1,0:T(8,128)(2,1)S(1)} collective-permute-done((bf16[528,256]{1,0:T(8,128)(2,1)S(1)}, bf16[528,256]{1,0:T(8,128)(2,1)S(1)}, u32[]{:S(2)}, u32[]{:S(2)}) %collective-permute-start.6) | collective-permute-done | bytes 270368 | tf_op jit(solution)/shard_map/ppermute | solution.py:215
  77.5 2.7 %shard_map.92 = (bf16[512,128]{1,0:T(8,128)(2,1)}, bf16[1024,512]{1,0:T(8,128)(2,1)S(1)}, bf16[512,256]{1,0:T(8,128)(2,1)S(1)}, bf16[512,256]{1,0:T(8,128)(2,1)S(1)}) custom-call(bf16[528,256]{1,0:T(8,128)(2,1)S(1)} %collective-permute-done.6.picked_ref, bf16[1024,256]{1,0:T(8,128)(2,1)S(1)} %subtract_convert_fusion.1.held_ref, ...), custom_call_target="tpu_custom_call" | custom-call | tf_op jit(solution)/shard_map/pallas_call | solution.py:151
  81.9 8.8 %all-to-all-start = ((bf16[32,16,128]{2,1,0:T(8,128)(2,1)}), bf16[32,16,128]{2,1,0:T(8,128)(2,1)S(1)}, u32[]{:S(2)}, u32[]{:S(2)}) async-start(bf16[32,16,128]{2,1,0:T(8,128)(2,1)} %bitcast.11), calls=%async_computation | async-start | bytes 262144 | tf_op jit(solution)/shard_map/all_to_all | solution.py:197
  90.7 1.4 %collective-permute-start.8 = (bf16[512,256]{1,0:T(8,128)(2,1)S(1)}, bf16[512,256]{1,0:T(8,128)(2,1)S(1)}, u32[]{:S(2)}, u32[]{:S(2)}) collective-permute-start(bf16[512,256]{1,0:T(8,128)(2,1)S(1)} %get-tuple-element.24), channel_id=1, source_target_pairs={{0,8},{1,9},{2,10},{3,11},{4,12},{5,13},{6,14},{7,15},{8,0},{9,1},... | collective-permute-start | bytes 786440 | tf_op jit(solution)/shard_map/ppermute | solution.py:215
  92.1 10.2 %all-to-all-done = bf16[32,16,128]{2,1,0:T(8,128)(2,1)S(1)} async-done(((bf16[32,16,128]{2,1,0:T(8,128)(2,1)}), bf16[32,16,128]{2,1,0:T(8,128)(2,1)S(1)}, u32[]{:S(2)}, u32[]{:S(2)}) %all-to-all-start) | async-done | bytes 131104 | tf_op jit(solution)/shard_map/all_to_all | solution.py:197
  102.3 9.2 %all_to_all.15 = bf16[8,16,128]{2,1,0:T(8,128)(2,1)S(1)} all-to-all(bf16[8,16,128]{2,1,0:T(8,128)(2,1)S(1)} %bitcast.45), channel_id=1, replica_groups={{0,1,2,3,4,5,6,7},{8,9,10,11,12,13,14,15},{16,17,18,19,20,21,22,23},{24..., dimensions={0} | all-to-all | bytes 65536 | tf_op jit(solution)/shard_map/all_to_all | solution.py:197
  112.2 5.2 %all-to-all-start.2 = ((bf16[32,16,128]{2,1,0:T(8,128)(2,1)}), bf16[32,16,128]{2,1,0:T(8,128)(2,1)S(1)}, u32[]{:S(2)}, u32[]{:S(2)}) async-start(bf16[32,16,128]{2,1,0:T(8,128)(2,1)} %bitcast.15), calls=%async_computation.2 | async-start | bytes 262144 | tf_op jit(solution)/shard_map/all_to_all | solution.py:197
  118.4 1.7 %shard_map.95 = bf16[1024,256]{1,0:T(8,128)(2,1)} custom-call(bf16[1024,256]{1,0:T(8,128)(2,1)S(1)} %shard_map.94.left_ref, s32[1,512]{1,0:T(1,128)S(1)} %get-tuple-element.31.source_ref, bf16[512,256]{1,0:T(8,128)(2,1)S(1)} %collective-permute-done.8.grad_ref, bf16[256,256]{1,0:T(8,128)(2,1)S(1)} %copy-done), custom_call_target="tpu_custom_call" | custom-call | tf_op jit(solution)/shard_map/pallas_call | solution.py:151
  120.9 4.2 %all-to-all-done.2 = bf16[32,16,128]{2,1,0:T(8,128)(2,1)S(1)} async-done(((bf16[32,16,128]{2,1,0:T(8,128)(2,1)}), bf16[32,16,128]{2,1,0:T(8,128)(2,1)S(1)}, u32[]{:S(2)}, u32[]{:S(2)}) %all-to-all-start.2) | async-done | bytes 131104 | tf_op jit(solution)/shard_map/all_to_all | solution.py:197
  (39 shorter events, 15.0 us)
Async XLA Ops:
  0.6 40.1 %collective-permute-start.4 = (bf16[1024,256]{1,0:T(8,128)(2,1)}, bf16[1024,256]{1,0:T(8,128)(2,1)S(1)}, u32[]{:S(2)}, u32[]{:S(2)}) collective-permute-start(bf16[1024,256]{1,0:T(8,128)(2,1)} %param.7), channel_id=1, source_target_pairs={{0,7},{1,6},{2,5},{3,4},{4,3},{5,2},{6,1},{7,0},{8,15},{9,14},{10,... | collective-permute-start | bytes 1572872 | tf_op jit(solution)/shard_map/ppermute | solution.py:215
  7.1 24.5 %collective-permute-start = (bf16[1024,256]{1,0:T(8,128)(2,1)}, bf16[1024,256]{1,0:T(8,128)(2,1)S(1)}, u32[]{:S(2)}, u32[]{:S(2)}) collective-permute-start(bf16[1024,256]{1,0:T(8,128)(2,1)} %param.7), channel_id=1, source_target_pairs={{0,1},{1,0},{2,3},{3,2},{4,5},{5,4},{6,7},{7,6},{8,9},{9,8},{10,11... | collective-permute-start | bytes 1572872 | tf_op jit(solution)/shard_map/ppermute | solution.py:215
  11.1 1.7 %copy-start = (bf16[256,256]{1,0:T(8,128)(2,1)S(1)}, bf16[256,256]{1,0:T(8,128)(2,1)}, u32[]{:S(2)}) copy-start(bf16[256,256]{1,0:T(8,128)(2,1)} %relation_ref.20) | copy-start | bytes 393220
  12.7 1.0 copy-start.1
  12.8 28.0 %collective-permute-start.3 = (bf16[528,256]{1,0:T(8,128)(2,1)S(1)}, bf16[528,256]{1,0:T(8,128)(2,1)S(1)}, u32[]{:S(2)}, u32[]{:S(2)}) collective-permute-start(bf16[528,256]{1,0:T(8,128)(2,1)S(1)} %pad_maximum_fusion), channel_id=1, source_target_pairs={{0,6},{1,7},{2,4},{3,5},{4,2},{5,3},{6,0},{7,1},{8,14},{9,15},{10,... | collective-permute-start | bytes 811016 | tf_op jit(solution)/shard_map/ppermute | solution.py:215
  34.0 12.4 %collective-permute-start.1 = (bf16[528,256]{1,0:T(8,128)(2,1)S(1)}, bf16[528,256]{1,0:T(8,128)(2,1)S(1)}, u32[]{:S(2)}, u32[]{:S(2)}) collective-permute-start(bf16[528,256]{1,0:T(8,128)(2,1)S(1)} %get-tuple-element.16), channel_id=1, source_target_pairs={{0,2},{1,3},{2,0},{3,1},{4,6},{5,7},{6,4},{7,5},{8,10},{9,11},{10,... | collective-permute-start | bytes 811016 | tf_op jit(solution)/shard_map/ppermute | solution.py:215
  47.8 13.6 %collective-permute-start.5 = (bf16[512,256]{1,0:T(8,128)(2,1)S(1)}, bf16[512,256]{1,0:T(8,128)(2,1)S(1)}, u32[]{:S(2)}, u32[]{:S(2)}) collective-permute-start(bf16[512,256]{1,0:T(8,128)(2,1)S(1)} %shard_map.89), channel_id=1, source_target_pairs={{0,2},{1,3},{2,0},{3,1},{4,6},{5,7},{6,4},{7,5},{8,10},{9,11},{10,... | collective-permute-start | bytes 786440 | tf_op jit(solution)/shard_map/ppermute | solution.py:215
  51.3 15.1 %collective-permute-start.2 = (bf16[528,256]{1,0:T(8,128)(2,1)S(1)}, bf16[528,256]{1,0:T(8,128)(2,1)S(1)}, u32[]{:S(2)}, u32[]{:S(2)}) collective-permute-start(bf16[528,256]{1,0:T(8,128)(2,1)S(1)} %collective-permute-done.1.picked_ref), channel_id=1, source_target_pairs={{0,6},{1,7},{2,4},{3,5},{4,2},{5,3},{6,0},{7,1},{8,14},{9,15},{10,... | collective-permute-start | bytes 811016 | tf_op jit(solution)/shard_map/ppermute | solution.py:215
  70.2 7.2 %collective-permute-start.6 = (bf16[528,256]{1,0:T(8,128)(2,1)S(1)}, bf16[528,256]{1,0:T(8,128)(2,1)S(1)}, u32[]{:S(2)}, u32[]{:S(2)}) collective-permute-start(bf16[528,256]{1,0:T(8,128)(2,1)S(1)} %get-tuple-element.20), channel_id=1, source_target_pairs={{0,8},{1,9},{2,10},{3,11},{4,12},{5,13},{6,14},{7,15},{8,0},{9,1},... | collective-permute-start | bytes 811016 | tf_op jit(solution)/shard_map/ppermute | solution.py:215
  80.6 39.4 %collective-permute-start.7 = (bf16[1024,256]{1,0:T(8,128)(2,1)S(1)}, bf16[1024,256]{1,0:T(8,128)(2,1)S(1)}, u32[]{:S(2)}, u32[]{:S(2)}) collective-permute-start(bf16[1024,256]{1,0:T(8,128)(2,1)S(1)} %subtract_convert_fusion), channel_id=1, source_target_pairs={{0,8},{1,9},{2,10},{3,11},{4,12},{5,13},{6,14},{7,15},{8,0},{9,1},... | collective-permute-start | bytes 1572872 | tf_op jit(solution)/shard_map/ppermute | solution.py:215
  81.9 20.4 %all-to-all-start = ((bf16[32,16,128]{2,1,0:T(8,128)(2,1)}), bf16[32,16,128]{2,1,0:T(8,128)(2,1)S(1)}, u32[]{:S(2)}, u32[]{:S(2)}) async-start(bf16[32,16,128]{2,1,0:T(8,128)(2,1)} %bitcast.11), calls=%async_computation | async-start | bytes 262144 | tf_op jit(solution)/shard_map/all_to_all | solution.py:197
  90.7 27.7 %collective-permute-start.8 = (bf16[512,256]{1,0:T(8,128)(2,1)S(1)}, bf16[512,256]{1,0:T(8,128)(2,1)S(1)}, u32[]{:S(2)}, u32[]{:S(2)}) collective-permute-start(bf16[512,256]{1,0:T(8,128)(2,1)S(1)} %get-tuple-element.24), channel_id=1, source_target_pairs={{0,8},{1,9},{2,10},{3,11},{4,12},{5,13},{6,14},{7,15},{8,0},{9,1},... | collective-permute-start | bytes 786440 | tf_op jit(solution)/shard_map/ppermute | solution.py:215
  112.2 12.8 %all-to-all-start.2 = ((bf16[32,16,128]{2,1,0:T(8,128)(2,1)}), bf16[32,16,128]{2,1,0:T(8,128)(2,1)S(1)}, u32[]{:S(2)}, u32[]{:S(2)}) async-start(bf16[32,16,128]{2,1,0:T(8,128)(2,1)} %bitcast.15), calls=%async_computation.2 | async-start | bytes 262144 | tf_op jit(solution)/shard_map/all_to_all | solution.py:197

commit v8 on v7

--- a/solution.py
+++ b/solution.py
@@ -94,9 +94,21 @@
     new_ref[...] = (held_ref[...].astype(jnp.float32) - (LR_EMBED * SCORE_SCALE) * held_grad).astype(jnp.bfloat16)
 
 
-def grad_kernel(picked_ref, held_ref, relation_ref, grad_ref, scores_ref, coeffs_ref):
+def host_kernel(picked_ref, held_ref, relation_ref, new_ref, grad_ref, scores_ref, coeffs_ref):
     then = lambda part: fill_gradient(coeffs_ref, held_ref, grad_ref, part)
-    coeffs_of(picked_ref, held_ref, relation_ref, coeffs_ref, scores_ref, then)
+    queries = coeffs_of(picked_ref, held_ref, relation_ref, coeffs_ref, scores_ref, then)
+    held_grad = dot(coeffs_ref[...], queries, ((1,), (0,)))
+    new_ref[...] = (held_ref[...].astype(jnp.float32) - (LR_EMBED * SCORE_SCALE) * held_grad).astype(jnp.bfloat16)
+
+
+def choice_kernel(flag_ref, picked_ref, held_ref, relation_ref, arrived_ref, new_ref, scores_ref, coeffs_ref):
+    @pl.when(flag_ref[0] == 1)
+    def _():
+        held_kernel(picked_ref, held_ref, relation_ref, new_ref, scores_ref, coeffs_ref)
+
+    @pl.when(flag_ref[0] == 0)
+    def _():
+        new_ref[...] = arrived_ref[...]
 
 
 def last_kernel(picked_ref, held_ref, relation_ref, before_ref, pieces_ref, coeffs_ref, grad_ref, queries_ref, scores_ref):
@@ -148,10 +160,11 @@
 
 def call(kernel, outs, *args, scratch=()):
     spec = pl.BlockSpec(memory_space=VM)
+    flags = pl.BlockSpec(memory_space=pltpu.SMEM)
     return pl.pallas_call(
         kernel,
         out_shape=outs,
-        in_specs=[spec] * len(args),
+        in_specs=[flags if arg.ndim == 1 else spec for arg in args],
         out_specs=jax.tree.map(lambda _: spec, outs),
         scratch_shapes=list(scratch),
         compiler_params=pltpu.CompilerParams(vmem_limit_bytes=16 << 20),
@@ -169,19 +182,15 @@
     return call(functools.partial(local_kernel, meeting), outs, queries, held, codes, relation, same, base, scratch=scratch)
 
 
-def row_kernel(kernel, out, picked, held, relation):
+def row_kernel(kernel, out, picked, held, relation, flag=(), arrived=()):
     rows, edges = held.shape[0], picked.shape[0] - CODE_ROWS
     scratch = [VM((rows, edges), jnp.float32), vmem(rows, edges)]
-    return call(kernel, out, picked, held, relation, scratch=scratch)
-
-
-def replayed(picked, held, relation):
-    return row_kernel(held_kernel, vmem(*held.shape), picked, held, relation)
-
-
-def gradient_at_host(picked, held, relation):
-    out = vmem(picked.shape[0] - CODE_ROWS, held.shape[1])
-    return row_kernel(grad_kernel, out, picked, held, relation)
+    return call(kernel, out, *flag, picked, held, relation, *arrived, scratch=scratch)
+
+
+def host_meeting(picked, held, relation):
+    outs = (vmem(*held.shape), vmem(picked.shape[0] - CODE_ROWS, held.shape[1]))
+    return row_kernel(host_kernel, outs, picked, held, relation)
 
 
 def last_meeting(picked, held, relation, before, edges):
@@ -210,8 +219,13 @@
     return exchanged(copies, AXES, planes)
 
 
-def moved(value, mask):
-    pairs = [(source, source ^ mask) for source in range(lax.axis_size("inner"))]
+def direct(place):
+    return ((place ^ (place >> 1)) & 1) == 0
+
+
+def moved(value, mask, senders=lambda place: True):
+    places = range(lax.axis_size("inner"))
+    pairs = [(source, source ^ mask) for source in places if senders(source)]
     return lax.ppermute(value, "inner", pairs)
 
 
@@ -258,13 +272,13 @@
     sources = src_index[0]
 
     held = moved(right_part, 1)
-    far = moved(right_part, 7)
+    far = moved(right_part, 7, direct)
     slots = jnp.arange(edges, dtype=jnp.int32)
     targets = jnp.where(slots[None, :] < lengths[0][:, None], dst_index[0], -1)
     codes = coded(targets)
     tables = [source_table(sources[meeting], rows) for meeting in range(4)]
     picked0 = picked_rows(left_part, tables[0])
-    rows0 = moved(jnp.concatenate([picked0, codes[:CODE_ROWS]], axis=0), 6)
+    rows0 = moved(jnp.concatenate([picked0, codes[:CODE_ROWS]], axis=0), 6, lambda place: not direct(place))
     queries0 = queries_of(picked0, relation)
     base = picked_rows(left_part, tables[1])
     same = same_source(sources[1], sources[0])
@@ -274,13 +288,16 @@
     held = updated_holding(held, coeffs, queries0)
     left = updated_left(left_part, sources[0], query_grad, relation, vmem(*left_part.shape))
     relation_grad = relation_gradient(picked0, query_grad)
-    query_grad = gradient_at_host(rows1, held, relation)
+    onward = moved(rows1, 6, lambda place: not direct(place))
+    new_held, query_grad = host_meeting(rows1, held, relation)
     back1 = moved(query_grad, 2)
-    onward = moved(rows1, 6)
+    arriving = moved(new_held, 6, direct)
     relation_grad = relation_grad + relation_gradient(rows1[:edges], query_grad)
     left = updated_left(left, sources[1], back1, relation, vmem(*left.shape))
 
-    held = replayed(onward, replayed(rows0, far, relation), relation)
+    flag = direct(lax.axis_index("inner")).astype(jnp.int32).reshape(1)
+    far = row_kernel(held_kernel, vmem(*far.shape), rows0, far, relation)
+    held = row_kernel(choice_kernel, vmem(*far.shape), onward, far, relation, [flag], [arriving])
     picked2 = picked_rows(left, tables[2])
     queries2 = queries_of(picked2, relation)
     base = picked_rows(left, tables[3])

time: 126 us -> 123 us (0.976)
  waiting for transfers between devices: 56.8 us -> 46.2 us
  starting transfers between devices: 31.7 us -> 34.9 us
  blocking collectives: 9.24 us -> 12.1 us
    ppermute x9 -> x10, waiting for transfers between devices: 42.5 us -> 33.5 us  [moved(): return lax.ppermute(value, 'inner', pairs)]
    all_to_all x1, blocking collectives: 9.24 us -> 12.1 us  [exchanged(): lax.all_to_all(pieces, axes, 0, 0, axis_index_groups=groups)]
    ppermute x9 -> x10, starting transfers between devices: 17.6 us -> 19.6 us  [moved(): return lax.ppermute(value, 'inner', pairs)]
    all_to_all x2, waiting for transfers between devices: 14.3 us -> 12.7 us  [exchanged(): lax.all_to_all(pieces, axes, 0, 0, axis_index_groups=groups)]
  transfers between devices with their start and end apart: 11 -> 12, of which waited for: 8 -> 9; matrix products, arithmetic and copies ran while one was open for 6% -> 7% of each run, Pallas kernels for 8% -> 8%
where the time goes in v8:
time: 123 us; the launch traced here: 122 us
  waiting for transfers between devices  46.2 us (38%)
  starting transfers between devices  34.9 us (28%)
  Pallas kernels  18.9 us (15%)
  blocking collectives  12.1 us (10%)
  matrix products  5.67 us (5%)
  other arithmetic  1.81 us (1%)
  local copies, waits for them, and re-layouts  1.6 us (1%)
    ppermute x10, waiting for transfers between devices, moved(): return lax.ppermute(value, 'inner', pairs)  33.5 us
    ppermute x10, starting transfers between devices, moved(): return lax.ppermute(value, 'inner', pairs)  19.6 us
    pallas_call x14, Pallas kernels, call(): pl.pallas_call(kernel, out_shape=outs, in_specs=[flags if arg.ndim == 1 e...  18.9 us
    all_to_all x2, starting transfers between devices, exchanged(): lax.all_to_all(pieces, axes, 0, 0, axis_index_groups=groups)  15.3 us
    all_to_all x2, waiting for transfers between devices, exchanged(): lax.all_to_all(pieces, axes, 0, 0, axis_index_groups=groups)  12.7 us
    all_to_all x1, blocking collectives, exchanged(): lax.all_to_all(pieces, axes, 0, 0, axis_index_groups=groups)  12.1 us
    dot_general x12, matrix products, dot(): lax.dot_general(a, b, (dims, ((), ())), preferred_element_type=jnp.float32)  5.67 us
  transfers between devices with their start and end apart: 12, of which 9 were waited for; matrix products, arithmetic and copies ran while one was open for 7% of the time, Pallas kernels for 8%

profile of v8, /device:TPU:1, one launch (start us, length us, event | category | flops | bytes accessed | tf_op | source)
XLA Modules:
  0.0 122.2 jit_solution(15655765195674111890)
XLA Ops:
  0.6 8.3 %collective-permute-start.4 = (bf16[1024,256]{1,0:T(8,128)(2,1)}, bf16[1024,256]{1,0:T(8,128)(2,1)S(1)}, u32[]{:S(2)}, u32[]{:S(2)}) collective-permute-start(bf16[1024,256]{1,0:T(8,128)(2,1)} %param.7), channel_id=1, source_target_pairs={{0,7},{3,4},{4,3},{7,0},{8,15},{11,12},{12,11},{15,8},{16,23},{19,... | collective-permute-start | bytes 1572872 | tf_op jit(solution)/shard_map/ppermute | solution.py:229
  11.4 1.6 %fusion.7 = bf16[512,256]{1,0:T(8,128)(2,1)S(1)} fusion(bf16[1024,256]{1,0:T(8,128)(2,1)} %left_ref.1, s32[512]{0:T(512)S(1)} %bitcast.54), kind=kOutput, calls=%fused_computation.14 | convolution fusion | flops 269090816 | bytes 788480 | tf_op jit(solution)/shard_map/dot_general | solution.py:20
  16.2 5.6 %collective-permute-done.held_ref = bf16[1024,256]{1,0:T(8,128)(2,1)S(1)} collective-permute-done((bf16[1024,256]{1,0:T(8,128)(2,1)}, bf16[1024,256]{1,0:T(8,128)(2,1)S(1)}, u32[]{:S(2)}, u32[]{:S(2)}) %collective-permute-start) | collective-permute-done | bytes 524320 | tf_op jit(solution)/shard_map/ppermute | solution.py:229
  21.8 2.3 %shard_map.85 = (bf16[1024,512]{1,0:T(8,128)(2,1)S(1)}, bf16[512,256]{1,0:T(8,128)(2,1)S(1)}, bf16[528,256]{1,0:T(8,128)(2,1)S(1)}) custom-call(bf16[512,256]{1,0:T(8,128)(2,1)S(1)} %convolution_convert_fusion.1.queries_ref, bf16[1024,256]{1,0:T(8,128)(2,1)S(1)} %collective-permute-done.held_ref, bf16[64,256]{1,0:T(8,128)(2,1)S(1)} %bitcast.44, ...), custom_call_target="tpu_custom_call" | custom-call | tf_op jit(solution)/shard_map/pallas_call | solution.py:164
  25.8 1.8 %collective-permute-done.3.picked_ref = bf16[528,256]{1,0:T(8,128)(2,1)S(1)} collective-permute-done((bf16[528,256]{1,0:T(8,128)(2,1)}, bf16[528,256]{1,0:T(8,128)(2,1)S(1)}, u32[]{:S(2)}, u32[]{:S(2)}) %collective-permute-start.3) | collective-permute-done | bytes 270368 | tf_op jit(solution)/shard_map/ppermute | solution.py:229
  27.6 1.5 %shard_map.86.held_ref = bf16[1024,256]{1,0:T(8,128)(2,1)S(1)} custom-call(bf16[528,256]{1,0:T(8,128)(2,1)S(1)} %collective-permute-done.3.picked_ref, bf16[1024,256]{1,0:T(8,128)(2,1)S(1)} %collective-permute-done.4.held_ref, bf16[256,256]{1,0:T(8,128)(2,1)S(1)} %copy-done), custom_call_target="tpu_custom_call" | custom-call | tf_op jit(solution)/shard_map/pallas_call | solution.py:164
  29.5 9.7 %collective-permute-done.1.picked_ref = bf16[528,256]{1,0:T(8,128)(2,1)S(1)} collective-permute-done((bf16[528,256]{1,0:T(8,128)(2,1)S(1)}, bf16[528,256]{1,0:T(8,128)(2,1)S(1)}, u32[]{:S(2)}, u32[]{:S(2)}) %collective-permute-start.1) | collective-permute-done | bytes 270368 | tf_op jit(solution)/shard_map/ppermute | solution.py:229
  39.3 1.8 %shard_map.87 = (bf16[1024,256]{1,0:T(8,128)(2,1)S(1)}, bf16[512,256]{1,0:T(8,128)(2,1)S(1)}) custom-call(bf16[528,256]{1,0:T(8,128)(2,1)S(1)} %collective-permute-done.1.picked_ref, bf16[1024,256]{1,0:T(8,128)(2,1)S(1)} %subtract_convert_fusion.2.held_ref, bf16[256,256]{1,0:T(8,128)(2,1)S(1)} %copy-done), custom_call_target="tpu_custom_call" | custom-call | tf_op jit(solution)/shard_map/pallas_call | solution.py:164
  41.2 3.7 %collective-permute-start.5 = (bf16[1024,256]{1,0:T(8,128)(2,1)S(1)}, bf16[1024,256]{1,0:T(8,128)(2,1)S(1)}, u32[]{:S(2)}, u32[]{:S(2)}) collective-permute-start(bf16[1024,256]{1,0:T(8,128)(2,1)S(1)} %get-tuple-element.20), channel_id=1, source_target_pairs={{0,6},{3,5},{4,2},{7,1},{8,14},{11,13},{12,10},{15,9},{16,22},{19,... | collective-permute-start | bytes 1572872 | tf_op jit(solution)/shard_map/ppermute | solution.py:229
  46.8 8.4 %collective-permute-done.6.grad_ref = bf16[512,256]{1,0:T(8,128)(2,1)S(1)} collective-permute-done((bf16[512,256]{1,0:T(8,128)(2,1)S(1)}, bf16[512,256]{1,0:T(8,128)(2,1)S(1)}, u32[]{:S(2)}, u32[]{:S(2)}) %collective-permute-start.6) | collective-permute-done | bytes 262176 | tf_op jit(solution)/shard_map/ppermute | solution.py:229
  57.4 3.6 %collective-permute-done.2.picked_ref = bf16[528,256]{1,0:T(8,128)(2,1)S(1)} collective-permute-done((bf16[528,256]{1,0:T(8,128)(2,1)S(1)}, bf16[528,256]{1,0:T(8,128)(2,1)S(1)}, u32[]{:S(2)}, u32[]{:S(2)}) %collective-permute-start.2) | collective-permute-done | bytes 270368 | tf_op jit(solution)/shard_map/ppermute | solution.py:229
  61.1 1.5 %shard_map.88.held_ref = bf16[1024,256]{1,0:T(8,128)(2,1)S(1)} custom-call(s32[1]{0:T(128)} %bitcast.flag_ref, bf16[528,256]{1,0:T(8,128)(2,1)S(1)} %collective-permute-done.2.picked_ref, bf16[1024,256]{1,0:T(8,128)(2,1)S(1)} %shard_map.86.held_ref, bf16[256,256]{1,0:T(8,128)(2,1)S(1)} %copy-done, bf16[1024,256]{1,0:T(8,128)(2,1)S(1)} %collective-permute-done.5.arrived_ref), custom_call_target="tpu_custom_call" | custom-call | tf_op jit(solution)/shard_map/pallas_call | solution.py:164
  62.6 2.4 %shard_map.91 = (bf16[1024,512]{1,0:T(8,128)(2,1)S(1)}, bf16[512,256]{1,0:T(8,128)(2,1)S(1)}, bf16[528,256]{1,0:T(8,128)(2,1)S(1)}) custom-call(bf16[512,256]{1,0:T(8,128)(2,1)S(1)} %convolution_convert_fusion.queries_ref, bf16[1024,256]{1,0:T(8,128)(2,1)S(1)} %shard_map.88.held_ref, bf16[64,256]{1,0:T(8,128)(2,1)S(1)} %bitcast.45, ...), custom_call_target="tpu_custom_call" | custom-call | tf_op jit(solution)/shard_map/pallas_call | solution.py:164
  65.0 1.3 %collective-permute-start.7 = (bf16[528,256]{1,0:T(8,128)(2,1)S(1)}, bf16[528,256]{1,0:T(8,128)(2,1)S(1)}, u32[]{:S(2)}, u32[]{:S(2)}) collective-permute-start(bf16[528,256]{1,0:T(8,128)(2,1)S(1)} %get-tuple-element.24), channel_id=1, source_target_pairs={{0,8},{1,9},{2,10},{3,11},{4,12},{5,13},{6,14},{7,15},{8,0},{9,1},... | collective-permute-start | bytes 811016 | tf_op jit(solution)/shard_map/ppermute | solution.py:229
  67.0 4.3 %collective-permute-done.7.picked_ref = bf16[528,256]{1,0:T(8,128)(2,1)S(1)} collective-permute-done((bf16[528,256]{1,0:T(8,128)(2,1)S(1)}, bf16[528,256]{1,0:T(8,128)(2,1)S(1)}, u32[]{:S(2)}, u32[]{:S(2)}) %collective-permute-start.7) | collective-permute-done | bytes 270368 | tf_op jit(solution)/shard_map/ppermute | solution.py:229
  71.3 2.7 %shard_map.92 = (bf16[512,128]{1,0:T(8,128)(2,1)}, bf16[1024,512]{1,0:T(8,128)(2,1)S(1)}, bf16[512,256]{1,0:T(8,128)(2,1)S(1)}, bf16[512,256]{1,0:T(8,128)(2,1)S(1)}) custom-call(bf16[528,256]{1,0:T(8,128)(2,1)S(1)} %collective-permute-done.7.picked_ref, bf16[1024,256]{1,0:T(8,128)(2,1)S(1)} %subtract_convert_fusion.1.held_ref, ...), custom_call_target="tpu_custom_call" | custom-call | tf_op jit(solution)/shard_map/pallas_call | solution.py:164
  74.5 1.3 %collective-permute-start.8 = (bf16[1024,256]{1,0:T(8,128)(2,1)S(1)}, bf16[1024,256]{1,0:T(8,128)(2,1)S(1)}, u32[]{:S(2)}, u32[]{:S(2)}) collective-permute-start(bf16[1024,256]{1,0:T(8,128)(2,1)S(1)} %subtract_convert_fusion), channel_id=1, source_target_pairs={{0,8},{1,9},{2,10},{3,11},{4,12},{5,13},{6,14},{7,15},{8,0},{9,1},... | collective-permute-start | bytes 1572872 | tf_op jit(solution)/shard_map/ppermute | solution.py:229
  75.8 9.7 %all-to-all-start = ((bf16[32,16,128]{2,1,0:T(8,128)(2,1)}), bf16[32,16,128]{2,1,0:T(8,128)(2,1)S(1)}, u32[]{:S(2)}, u32[]{:S(2)}) async-start(bf16[32,16,128]{2,1,0:T(8,128)(2,1)} %bitcast.12), calls=%async_computation | async-start | bytes 262144 | tf_op jit(solution)/shard_map/all_to_all | solution.py:206
  85.5 1.4 %collective-permute-start.9 = (bf16[512,256]{1,0:T(8,128)(2,1)S(1)}, bf16[512,256]{1,0:T(8,128)(2,1)S(1)}, u32[]{:S(2)}, u32[]{:S(2)}) collective-permute-start(bf16[512,256]{1,0:T(8,128)(2,1)S(1)} %get-tuple-element.28), channel_id=1, source_target_pairs={{0,8},{1,9},{2,10},{3,11},{4,12},{5,13},{6,14},{7,15},{8,0},{9,1},... | collective-permute-start | bytes 786440 | tf_op jit(solution)/shard_map/ppermute | solution.py:229
  86.9 8.5 %all-to-all-done = bf16[32,16,128]{2,1,0:T(8,128)(2,1)S(1)} async-done(((bf16[32,16,128]{2,1,0:T(8,128)(2,1)}), bf16[32,16,128]{2,1,0:T(8,128)(2,1)S(1)}, u32[]{:S(2)}, u32[]{:S(2)}) %all-to-all-start) | async-done | bytes 131104 | tf_op jit(solution)/shard_map/all_to_all | solution.py:206
  95.5 12.1 %all_to_all.15 = bf16[8,16,128]{2,1,0:T(8,128)(2,1)S(1)} all-to-all(bf16[8,16,128]{2,1,0:T(8,128)(2,1)S(1)} %bitcast.46), channel_id=1, replica_groups={{0,1,2,3,4,5,6,7},{8,9,10,11,12,13,14,15},{16,17,18,19,20,21,22,23},{24..., dimensions={0} | all-to-all | bytes 65536 | tf_op jit(solution)/shard_map/all_to_all | solution.py:206
  108.3 5.6 %all-to-all-start.2 = ((bf16[32,16,128]{2,1,0:T(8,128)(2,1)}), bf16[32,16,128]{2,1,0:T(8,128)(2,1)S(1)}, u32[]{:S(2)}, u32[]{:S(2)}) async-start(bf16[32,16,128]{2,1,0:T(8,128)(2,1)} %bitcast.16), calls=%async_computation.2 | async-start | bytes 262144 | tf_op jit(solution)/shard_map/all_to_all | solution.py:206
  114.7 1.7 %shard_map.95 = bf16[1024,256]{1,0:T(8,128)(2,1)} custom-call(bf16[1024,256]{1,0:T(8,128)(2,1)S(1)} %shard_map.94.left_ref, s32[1,512]{1,0:T(1,128)S(1)} %get-tuple-element.35.source_ref, bf16[512,256]{1,0:T(8,128)(2,1)S(1)} %collective-permute-done.9.grad_ref, bf16[256,256]{1,0:T(8,128)(2,1)S(1)} %copy-done), custom_call_target="tpu_custom_call" | custom-call | tf_op jit(solution)/shard_map/pallas_call | solution.py:164
  117.2 4.2 %all-to-all-done.2 = bf16[32,16,128]{2,1,0:T(8,128)(2,1)S(1)} async-done(((bf16[32,16,128]{2,1,0:T(8,128)(2,1)}), bf16[32,16,128]{2,1,0:T(8,128)(2,1)S(1)}, u32[]{:S(2)}, u32[]{:S(2)}) %all-to-all-start.2) | async-done | bytes 131104 | tf_op jit(solution)/shard_map/all_to_all | solution.py:206
  (45 shorter events, 16.1 us)
Async XLA Ops:
  0.6 26.9 %collective-permute-start.4 = (bf16[1024,256]{1,0:T(8,128)(2,1)}, bf16[1024,256]{1,0:T(8,128)(2,1)S(1)}, u32[]{:S(2)}, u32[]{:S(2)}) collective-permute-start(bf16[1024,256]{1,0:T(8,128)(2,1)} %param.7), channel_id=1, source_target_pairs={{0,7},{3,4},{4,3},{7,0},{8,15},{11,12},{12,11},{15,8},{16,23},{19,... | collective-permute-start | bytes 1572872 | tf_op jit(solution)/shard_map/ppermute | solution.py:229
  8.9 12.8 %collective-permute-start = (bf16[1024,256]{1,0:T(8,128)(2,1)}, bf16[1024,256]{1,0:T(8,128)(2,1)S(1)}, u32[]{:S(2)}, u32[]{:S(2)}) collective-permute-start(bf16[1024,256]{1,0:T(8,128)(2,1)} %param.7), channel_id=1, source_target_pairs={{0,1},{1,0},{2,3},{3,2},{4,5},{5,4},{6,7},{7,6},{8,9},{9,8},{10,11... | collective-permute-start | bytes 1572872 | tf_op jit(solution)/shard_map/ppermute | solution.py:229
  11.4 3.6 %copy-start = (bf16[256,256]{1,0:T(8,128)(2,1)S(1)}, bf16[256,256]{1,0:T(8,128)(2,1)}, u32[]{:S(2)}) copy-start(bf16[256,256]{1,0:T(8,128)(2,1)} %relation_ref.20) | copy-start | bytes 393220
  13.0 2.4 %copy-start.2 = (bf16[512,256]{1,0:T(8,128)(2,1)}, bf16[512,256]{1,0:T(8,128)(2,1)S(1)}, u32[]{:S(2)}) copy-start(bf16[512,256]{1,0:T(8,128)(2,1)S(1)} %fusion.7) | copy-start | bytes 786436
  13.1 2.6 %copy-start.1 = (bf16[1024,256]{1,0:T(8,128)(2,1)S(1)}, bf16[1024,256]{1,0:T(8,128)(2,1)}, u32[]{:S(2)}) copy-start(bf16[1024,256]{1,0:T(8,128)(2,1)} %left_ref.1) | copy-start | bytes 1572868
  13.8 13.8 %collective-permute-start.3 = (bf16[528,256]{1,0:T(8,128)(2,1)}, bf16[528,256]{1,0:T(8,128)(2,1)S(1)}, u32[]{:S(2)}, u32[]{:S(2)}) collective-permute-start(bf16[528,256]{1,0:T(8,128)(2,1)} %pad_maximum_fusion), channel_id=1, source_target_pairs={{1,7},{2,4},{5,3},{6,0},{9,15},{10,12},{13,11},{14,8},{17,23},{18,... | collective-permute-start | bytes 811016 | tf_op jit(solution)/shard_map/ppermute | solution.py:229
  24.1 15.2 %collective-permute-start.1 = (bf16[528,256]{1,0:T(8,128)(2,1)S(1)}, bf16[528,256]{1,0:T(8,128)(2,1)S(1)}, u32[]{:S(2)}, u32[]{:S(2)}) collective-permute-start(bf16[528,256]{1,0:T(8,128)(2,1)S(1)} %get-tuple-element.18), channel_id=1, source_target_pairs={{0,2},{1,3},{2,0},{3,1},{4,6},{5,7},{6,4},{7,5},{8,10},{9,11},{10,... | collective-permute-start | bytes 811016 | tf_op jit(solution)/shard_map/ppermute | solution.py:229
  29.5 17.0 %copy-start.3 = (bf16[512,256]{1,0:T(8,128)(2,1)S(1)}, bf16[512,256]{1,0:T(8,128)(2,1)}, u32[]{:S(2)}) copy-start(bf16[512,256]{1,0:T(8,128)(2,1)} %copy-done.2) | copy-start | bytes 786436
  41.1 14.1 %collective-permute-start.6 = (bf16[512,256]{1,0:T(8,128)(2,1)S(1)}, bf16[512,256]{1,0:T(8,128)(2,1)S(1)}, u32[]{:S(2)}, u32[]{:S(2)}) collective-permute-start(bf16[512,256]{1,0:T(8,128)(2,1)S(1)} %get-tuple-element.22), channel_id=1, source_target_pairs={{0,2},{1,3},{2,0},{3,1},{4,6},{5,7},{6,4},{7,5},{8,10},{9,11},{10,... | collective-permute-start | bytes 786440 | tf_op jit(solution)/shard_map/ppermute | solution.py:229
  41.2 19.8 %collective-permute-start.5 = (bf16[1024,256]{1,0:T(8,128)(2,1)S(1)}, bf16[1024,256]{1,0:T(8,128)(2,1)S(1)}, u32[]{:S(2)}, u32[]{:S(2)}) collective-permute-start(bf16[1024,256]{1,0:T(8,128)(2,1)S(1)} %get-tuple-element.20), channel_id=1, source_target_pairs={{0,6},{3,5},{4,2},{7,1},{8,14},{11,13},{12,10},{15,9},{16,22},{19,... | collective-permute-start | bytes 1572872 | tf_op jit(solution)/shard_map/ppermute | solution.py:229
  45.2 15.7 %collective-permute-start.2 = (bf16[528,256]{1,0:T(8,128)(2,1)S(1)}, bf16[528,256]{1,0:T(8,128)(2,1)S(1)}, u32[]{:S(2)}, u32[]{:S(2)}) collective-permute-start(bf16[528,256]{1,0:T(8,128)(2,1)S(1)} %collective-permute-done.1.picked_ref), channel_id=1, source_target_pairs={{1,7},{2,4},{5,3},{6,0},{9,15},{10,12},{13,11},{14,8},{17,23},{18,... | collective-permute-start | bytes 811016 | tf_op jit(solution)/shard_map/ppermute | solution.py:229
  65.0 6.3 %collective-permute-start.7 = (bf16[528,256]{1,0:T(8,128)(2,1)S(1)}, bf16[528,256]{1,0:T(8,128)(2,1)S(1)}, u32[]{:S(2)}, u32[]{:S(2)}) collective-permute-start(bf16[528,256]{1,0:T(8,128)(2,1)S(1)} %get-tuple-element.24), channel_id=1, source_target_pairs={{0,8},{1,9},{2,10},{3,11},{4,12},{5,13},{6,14},{7,15},{8,0},{9,1},... | collective-permute-start | bytes 811016 | tf_op jit(solution)/shard_map/ppermute | solution.py:229
  74.5 42.0 %collective-permute-start.8 = (bf16[1024,256]{1,0:T(8,128)(2,1)S(1)}, bf16[1024,256]{1,0:T(8,128)(2,1)S(1)}, u32[]{:S(2)}, u32[]{:S(2)}) collective-permute-start(bf16[1024,256]{1,0:T(8,128)(2,1)S(1)} %subtract_convert_fusion), channel_id=1, source_target_pairs={{0,8},{1,9},{2,10},{3,11},{4,12},{5,13},{6,14},{7,15},{8,0},{9,1},... | collective-permute-start | bytes 1572872 | tf_op jit(solution)/shard_map/ppermute | solution.py:229
  75.8 19.6 %all-to-all-start = ((bf16[32,16,128]{2,1,0:T(8,128)(2,1)}), bf16[32,16,128]{2,1,0:T(8,128)(2,1)S(1)}, u32[]{:S(2)}, u32[]{:S(2)}) async-start(bf16[32,16,128]{2,1,0:T(8,128)(2,1)} %bitcast.12), calls=%async_computation | async-start | bytes 262144 | tf_op jit(solution)/shard_map/all_to_all | solution.py:206
  85.5 29.2 %collective-permute-start.9 = (bf16[512,256]{1,0:T(8,128)(2,1)S(1)}, bf16[512,256]{1,0:T(8,128)(2,1)S(1)}, u32[]{:S(2)}, u32[]{:S(2)}) collective-permute-start(bf16[512,256]{1,0:T(8,128)(2,1)S(1)} %get-tuple-element.28), channel_id=1, source_target_pairs={{0,8},{1,9},{2,10},{3,11},{4,12},{5,13},{6,14},{7,15},{8,0},{9,1},... | collective-permute-start | bytes 786440 | tf_op jit(solution)/shard_map/ppermute | solution.py:229
  108.3 13.2 %all-to-all-start.2 = ((bf16[32,16,128]{2,1,0:T(8,128)(2,1)}), bf16[32,16,128]{2,1,0:T(8,128)(2,1)S(1)}, u32[]{:S(2)}, u32[]{:S(2)}) async-start(bf16[32,16,128]{2,1,0:T(8,128)(2,1)} %bitcast.16), calls=%async_computation.2 | async-start | bytes 262144 | tf_op jit(solution)/shard_map/all_to_all | solution.py:206

commit v9 on v8

--- a/solution.py
+++ b/solution.py
@@ -94,11 +94,9 @@
     new_ref[...] = (held_ref[...].astype(jnp.float32) - (LR_EMBED * SCORE_SCALE) * held_grad).astype(jnp.bfloat16)
 
 
-def host_kernel(picked_ref, held_ref, relation_ref, new_ref, grad_ref, scores_ref, coeffs_ref):
+def grad_kernel(picked_ref, held_ref, relation_ref, grad_ref, scores_ref, coeffs_ref):
     then = lambda part: fill_gradient(coeffs_ref, held_ref, grad_ref, part)
-    queries = coeffs_of(picked_ref, held_ref, relation_ref, coeffs_ref, scores_ref, then)
-    held_grad = dot(coeffs_ref[...], queries, ((1,), (0,)))
-    new_ref[...] = (held_ref[...].astype(jnp.float32) - (LR_EMBED * SCORE_SCALE) * held_grad).astype(jnp.bfloat16)
+    coeffs_of(picked_ref, held_ref, relation_ref, coeffs_ref, scores_ref, then)
 
 
 def choice_kernel(flag_ref, picked_ref, held_ref, relation_ref, arrived_ref, new_ref, scores_ref, coeffs_ref):
@@ -186,11 +184,6 @@
     rows, edges = held.shape[0], picked.shape[0] - CODE_ROWS
     scratch = [VM((rows, edges), jnp.float32), vmem(rows, edges)]
     return call(kernel, out, *flag, picked, held, relation, *arrived, scratch=scratch)
-
-
-def host_meeting(picked, held, relation):
-    outs = (vmem(*held.shape), vmem(picked.shape[0] - CODE_ROWS, held.shape[1]))
-    return row_kernel(host_kernel, outs, picked, held, relation)
 
 
 def last_meeting(picked, held, relation, before, edges):
@@ -288,16 +281,18 @@
     held = updated_holding(held, coeffs, queries0)
     left = updated_left(left_part, sources[0], query_grad, relation, vmem(*left_part.shape))
     relation_grad = relation_gradient(picked0, query_grad)
-    onward = moved(rows1, 6, lambda place: not direct(place))
-    new_held, query_grad = host_meeting(rows1, held, relation)
+    middle = moved(held, 6, direct)
+    grad_shape = vmem(edges, held.shape[1])
+    query_grad = row_kernel(grad_kernel, grad_shape, rows1, held, relation)
     back1 = moved(query_grad, 2)
-    arriving = moved(new_held, 6, direct)
+    onward = moved(rows1, 6)
     relation_grad = relation_grad + relation_gradient(rows1[:edges], query_grad)
     left = updated_left(left, sources[1], back1, relation, vmem(*left.shape))
 
     flag = direct(lax.axis_index("inner")).astype(jnp.int32).reshape(1)
-    far = row_kernel(held_kernel, vmem(*far.shape), rows0, far, relation)
-    held = row_kernel(choice_kernel, vmem(*far.shape), onward, far, relation, [flag], [arriving])
+    shape = vmem(*far.shape)
+    far = row_kernel(choice_kernel, shape, rows0, far, relation, [flag], [middle])
+    held = row_kernel(held_kernel, shape, onward, far, relation)
     picked2 = picked_rows(left, tables[2])
     queries2 = queries_of(picked2, relation)
     base = picked_rows(left, tables[3])

time: 123 us -> 119 us (0.967)
  waiting for transfers between devices: 46.2 us -> 34.7 us
  blocking collectives: 12.1 us -> 15.6 us
  starting transfers between devices: 34.9 us -> 36.9 us
  Pallas kernels: 18.9 us -> 20.4 us
    ppermute x10, waiting for transfers between devices: 33.5 us -> 23.9 us  [moved(): return lax.ppermute(value, 'inner', pairs)]
    all_to_all x1, blocking collectives: 12.1 us -> 15.6 us  [exchanged(): lax.all_to_all(pieces, axes, 0, 0, axis_index_groups=groups)]
    all_to_all x2, starting transfers between devices: 15.3 us -> 17.5 us  [exchanged(): lax.all_to_all(pieces, axes, 0, 0, axis_index_groups=groups)]
    all_to_all x2, waiting for transfers between devices: 12.7 us -> 10.7 us  [exchanged(): lax.all_to_all(pieces, axes, 0, 0, axis_index_groups=groups)]
    pallas_call x14, Pallas kernels: 18.9 us -> 20.4 us  [call(): pl.pallas_call(kernel, out_shape=outs, in_specs=[flags if arg.ndim == 1 e...]
  transfers between devices with their start and end apart: 12 -> 12, of which waited for: 9 -> 7; matrix products, arithmetic and copies ran while one was open for 7% -> 8% of each run, Pallas kernels for 8% -> 11%
where the time goes in v9:
time: 119 us; the launch traced here: 118 us
  starting transfers between devices  36.9 us (31%)
  waiting for transfers between devices  34.7 us (29%)
  Pallas kernels  20.4 us (17%)
  blocking collectives  15.6 us (13%)
  matrix products  5.64 us (5%)
  local copies, waits for them, and re-layouts  2.19 us (2%)
  other arithmetic  1.81 us (2%)
    ppermute x10, waiting for transfers between devices, moved(): return lax.ppermute(value, 'inner', pairs)  23.9 us
    pallas_call x14, Pallas kernels, call(): pl.pallas_call(kernel, out_shape=outs, in_specs=[flags if arg.ndim == 1 e...  20.4 us
    ppermute x10, starting transfers between devices, moved(): return lax.ppermute(value, 'inner', pairs)  19.4 us
    all_to_all x2, starting transfers between devices, exchanged(): lax.all_to_all(pieces, axes, 0, 0, axis_index_groups=groups)  17.5 us
    all_to_all x1, blocking collectives, exchanged(): lax.all_to_all(pieces, axes, 0, 0, axis_index_groups=groups)  15.6 us
    all_to_all x2, waiting for transfers between devices, exchanged(): lax.all_to_all(pieces, axes, 0, 0, axis_index_groups=groups)  10.7 us
    dot_general x12, matrix products, dot(): lax.dot_general(a, b, (dims, ((), ())), preferred_element_type=jnp.float32)  5.64 us
  transfers between devices with their start and end apart: 12, of which 7 were waited for; matrix products, arithmetic and copies ran while one was open for 8% of the time, Pallas kernels for 11%

profile of v9, /device:TPU:1, one launch (start us, length us, event | category | flops | bytes accessed | tf_op | source)
XLA Modules:
  0.0 118.3 jit_solution(4651528601235242013)
XLA Ops:
  0.6 8.3 %collective-permute-start.4 = (bf16[1024,256]{1,0:T(8,128)(2,1)}, bf16[1024,256]{1,0:T(8,128)(2,1)S(1)}, u32[]{:S(2)}, u32[]{:S(2)}) collective-permute-start(bf16[1024,256]{1,0:T(8,128)(2,1)} %param.7), channel_id=1, source_target_pairs={{0,7},{3,4},{4,3},{7,0},{8,15},{11,12},{12,11},{15,8},{16,23},{19,... | collective-permute-start | bytes 1572872 | tf_op jit(solution)/shard_map/ppermute | solution.py:222
  10.5 1.4 %slice_bitcast_fusion.1 = (s32[1,512]{1,0:T(1,128)S(1)}, s32[1,512]{1,0:T(1,128)S(1)}, s32[1,512]{1,0:T(1,128)}, s32[1,512]{1,0:T(1,128)S(1)}, s32[1,1,512]{2,1,...) fusion(s32[1,4,512]{2,1,0:T(4,128)} %param.9), kind=kLoop, calls=%fused_computation.47 | loop fusion | bytes 24576 | tf_op jit(solution)/shard_map/slice | solution.py:299
  12.0 1.6 %fusion.7 = bf16[512,256]{1,0:T(8,128)(2,1)S(1)} fusion(bf16[1024,256]{1,0:T(8,128)(2,1)} %left_ref.1, s32[512]{0:T(512)S(1)} %bitcast.54), kind=kOutput, calls=%fused_computation.14 | convolution fusion | flops 269090816 | bytes 788480 | tf_op jit(solution)/shard_map/dot_general | solution.py:20
  16.6 5.2 %collective-permute-done.held_ref = bf16[1024,256]{1,0:T(8,128)(2,1)S(1)} collective-permute-done((bf16[1024,256]{1,0:T(8,128)(2,1)}, bf16[1024,256]{1,0:T(8,128)(2,1)S(1)}, u32[]{:S(2)}, u32[]{:S(2)}) %collective-permute-start) | collective-permute-done | bytes 524320 | tf_op jit(solution)/shard_map/ppermute | solution.py:222
  21.8 3.1 %shard_map.85 = (bf16[1024,512]{1,0:T(8,128)(2,1)S(1)}, bf16[512,256]{1,0:T(8,128)(2,1)S(1)}, bf16[528,256]{1,0:T(8,128)(2,1)}) custom-call(bf16[512,256]{1,0:T(8,128)(2,1)S(1)} %convolution_convert_fusion.1.queries_ref, bf16[1024,256]{1,0:T(8,128)(2,1)S(1)} %collective-permute-done.held_ref, bf16[64,256]{1,0:T(8,128)(2,1)S(1)} %bitcast.44, ...), custom_call_target="tpu_custom_call" | custom-call | tf_op jit(solution)/shard_map/pallas_call | solution.py:162
  26.0 3.0 %collective-permute-start.5 = (bf16[1024,256]{1,0:T(8,128)(2,1)S(1)}, bf16[1024,256]{1,0:T(8,128)(2,1)S(1)}, u32[]{:S(2)}, u32[]{:S(2)}) collective-permute-start(bf16[1024,256]{1,0:T(8,128)(2,1)S(1)} %subtract_convert_fusion.2.held_ref), channel_id=1, source_target_pairs={{0,6},{3,5},{4,2},{7,1},{8,14},{11,13},{12,10},{15,9},{16,22},{19,... | collective-permute-start | bytes 1572872 | tf_op jit(solution)/shard_map/ppermute | solution.py:222
  30.1 9.7 %collective-permute-done.1.picked_ref = bf16[528,256]{1,0:T(8,128)(2,1)S(1)} collective-permute-done((bf16[528,256]{1,0:T(8,128)(2,1)}, bf16[528,256]{1,0:T(8,128)(2,1)S(1)}, u32[]{:S(2)}, u32[]{:S(2)}) %collective-permute-start.1) | collective-permute-done | bytes 270368 | tf_op jit(solution)/shard_map/ppermute | solution.py:222
  39.8 1.5 %shard_map.89 = bf16[512,256]{1,0:T(8,128)(2,1)S(1)} custom-call(bf16[528,256]{1,0:T(8,128)(2,1)S(1)} %collective-permute-done.1.picked_ref, bf16[1024,256]{1,0:T(8,128)(2,1)S(1)} %subtract_convert_fusion.2.held_ref, bf16[256,256]{1,0:T(8,128)(2,1)S(1)} %copy-done), custom_call_target="tpu_custom_call" | custom-call | tf_op jit(solution)/shard_map/pallas_call | solution.py:162
  41.7 1.9 %collective-permute-start.2 = (bf16[528,256]{1,0:T(8,128)(2,1)S(1)}, bf16[528,256]{1,0:T(8,128)(2,1)S(1)}, u32[]{:S(2)}, u32[]{:S(2)}) collective-permute-start(bf16[528,256]{1,0:T(8,128)(2,1)S(1)} %collective-permute-done.1.picked_ref), channel_id=1, source_target_pairs={{0,6},{1,7},{2,4},{3,5},{4,2},{5,3},{6,0},{7,1},{8,14},{9,15},{10,... | collective-permute-start | bytes 811016 | tf_op jit(solution)/shard_map/ppermute | solution.py:222
  43.9 2.7 %shard_map.86.held_ref = bf16[1024,256]{1,0:T(8,128)(2,1)S(1)} custom-call(s32[1]{0:T(128)} %bitcast.4.flag_ref, bf16[528,256]{1,0:T(8,128)(2,1)} %collective-permute-done.3.picked_ref, bf16[1024,256]{1,0:T(8,128)(2,1)S(1)} %collective-permute-done.4.held_ref, bf16[256,256]{1,0:T(8,128)(2,1)S(1)} %copy-done, ...), custom_call_target="tpu_custom_call" | custom-call | tf_op jit(solution)/shard_map/pallas_call | solution.py:162
  46.6 5.1 %collective-permute-done.6.grad_ref = bf16[512,256]{1,0:T(8,128)(2,1)S(1)} collective-permute-done((bf16[512,256]{1,0:T(8,128)(2,1)S(1)}, bf16[512,256]{1,0:T(8,128)(2,1)S(1)}, u32[]{:S(2)}, u32[]{:S(2)}) %collective-permute-start.6) | collective-permute-done | bytes 262176 | tf_op jit(solution)/shard_map/ppermute | solution.py:222
  54.4 1.5 %shard_map.87.held_ref = bf16[1024,256]{1,0:T(8,128)(2,1)S(1)} custom-call(bf16[528,256]{1,0:T(8,128)(2,1)S(1)} %collective-permute-done.2.picked_ref, bf16[1024,256]{1,0:T(8,128)(2,1)S(1)} %shard_map.86.held_ref, bf16[256,256]{1,0:T(8,128)(2,1)S(1)} %copy-done), custom_call_target="tpu_custom_call" | custom-call | tf_op jit(solution)/shard_map/pallas_call | solution.py:162
  55.9 2.3 %shard_map.91 = (bf16[1024,512]{1,0:T(8,128)(2,1)S(1)}, bf16[512,256]{1,0:T(8,128)(2,1)S(1)}, bf16[528,256]{1,0:T(8,128)(2,1)S(1)}) custom-call(bf16[512,256]{1,0:T(8,128)(2,1)S(1)} %convolution_convert_fusion.queries_ref, bf16[1024,256]{1,0:T(8,128)(2,1)S(1)} %shard_map.87.held_ref, bf16[64,256]{1,0:T(8,128)(2,1)S(1)} %bitcast.45, ...), custom_call_target="tpu_custom_call" | custom-call | tf_op jit(solution)/shard_map/pallas_call | solution.py:162
  58.3 1.3 %collective-permute-start.7 = (bf16[528,256]{1,0:T(8,128)(2,1)S(1)}, bf16[528,256]{1,0:T(8,128)(2,1)S(1)}, u32[]{:S(2)}, u32[]{:S(2)}) collective-permute-start(bf16[528,256]{1,0:T(8,128)(2,1)S(1)} %get-tuple-element.20), channel_id=1, source_target_pairs={{0,8},{1,9},{2,10},{3,11},{4,12},{5,13},{6,14},{7,15},{8,0},{9,1},... | collective-permute-start | bytes 811016 | tf_op jit(solution)/shard_map/ppermute | solution.py:222
  60.3 3.4 %collective-permute-done.7.picked_ref = bf16[528,256]{1,0:T(8,128)(2,1)S(1)} collective-permute-done((bf16[528,256]{1,0:T(8,128)(2,1)S(1)}, bf16[528,256]{1,0:T(8,128)(2,1)S(1)}, u32[]{:S(2)}, u32[]{:S(2)}) %collective-permute-start.7) | collective-permute-done | bytes 270368 | tf_op jit(solution)/shard_map/ppermute | solution.py:222
  63.7 2.7 %shard_map.92 = (bf16[512,128]{1,0:T(8,128)(2,1)}, bf16[1024,512]{1,0:T(8,128)(2,1)S(1)}, bf16[512,256]{1,0:T(8,128)(2,1)S(1)}, bf16[512,256]{1,0:T(8,128)(2,1)S(1)}) custom-call(bf16[528,256]{1,0:T(8,128)(2,1)S(1)} %collective-permute-done.7.picked_ref, bf16[1024,256]{1,0:T(8,128)(2,1)S(1)} %subtract_convert_fusion.1.held_ref, ...), custom_call_target="tpu_custom_call" | custom-call | tf_op jit(solution)/shard_map/pallas_call | solution.py:162
  66.8 1.3 %collective-permute-start.8 = (bf16[1024,256]{1,0:T(8,128)(2,1)S(1)}, bf16[1024,256]{1,0:T(8,128)(2,1)S(1)}, u32[]{:S(2)}, u32[]{:S(2)}) collective-permute-start(bf16[1024,256]{1,0:T(8,128)(2,1)S(1)} %subtract_convert_fusion), channel_id=1, source_target_pairs={{0,8},{1,9},{2,10},{3,11},{4,12},{5,13},{6,14},{7,15},{8,0},{9,1},... | collective-permute-start | bytes 1572872 | tf_op jit(solution)/shard_map/ppermute | solution.py:222
  68.1 11.9 %all-to-all-start = ((bf16[32,16,128]{2,1,0:T(8,128)(2,1)}), bf16[32,16,128]{2,1,0:T(8,128)(2,1)S(1)}, u32[]{:S(2)}, u32[]{:S(2)}) async-start(bf16[32,16,128]{2,1,0:T(8,128)(2,1)} %bitcast.12), calls=%async_computation | async-start | bytes 262144 | tf_op jit(solution)/shard_map/all_to_all | solution.py:199
  80.0 1.4 %collective-permute-start.9 = (bf16[512,256]{1,0:T(8,128)(2,1)S(1)}, bf16[512,256]{1,0:T(8,128)(2,1)S(1)}, u32[]{:S(2)}, u32[]{:S(2)}) collective-permute-start(bf16[512,256]{1,0:T(8,128)(2,1)S(1)} %get-tuple-element.24), channel_id=1, source_target_pairs={{0,8},{1,9},{2,10},{3,11},{4,12},{5,13},{6,14},{7,15},{8,0},{9,1},... | collective-permute-start | bytes 786440 | tf_op jit(solution)/shard_map/ppermute | solution.py:222
  81.4 6.5 %all-to-all-done = bf16[32,16,128]{2,1,0:T(8,128)(2,1)S(1)} async-done(((bf16[32,16,128]{2,1,0:T(8,128)(2,1)}), bf16[32,16,128]{2,1,0:T(8,128)(2,1)S(1)}, u32[]{:S(2)}, u32[]{:S(2)}) %all-to-all-start) | async-done | bytes 131104 | tf_op jit(solution)/shard_map/all_to_all | solution.py:199
  88.0 15.6 %all_to_all.15 = bf16[8,16,128]{2,1,0:T(8,128)(2,1)S(1)} all-to-all(bf16[8,16,128]{2,1,0:T(8,128)(2,1)S(1)} %bitcast.46), channel_id=1, replica_groups={{0,1,2,3,4,5,6,7},{8,9,10,11,12,13,14,15},{16,17,18,19,20,21,22,23},{24..., dimensions={0} | all-to-all | bytes 65536 | tf_op jit(solution)/shard_map/all_to_all | solution.py:199
  104.3 5.6 %all-to-all-start.2 = ((bf16[32,16,128]{2,1,0:T(8,128)(2,1)}), bf16[32,16,128]{2,1,0:T(8,128)(2,1)S(1)}, u32[]{:S(2)}, u32[]{:S(2)}) async-start(bf16[32,16,128]{2,1,0:T(8,128)(2,1)} %bitcast.16), calls=%async_computation.2 | async-start | bytes 262144 | tf_op jit(solution)/shard_map/all_to_all | solution.py:199
  110.8 1.7 %shard_map.95 = bf16[1024,256]{1,0:T(8,128)(2,1)} custom-call(bf16[1024,256]{1,0:T(8,128)(2,1)S(1)} %shard_map.94.left_ref, s32[1,512]{1,0:T(1,128)S(1)} %get-tuple-element.31.source_ref, bf16[512,256]{1,0:T(8,128)(2,1)S(1)} %collective-permute-done.9.grad_ref, bf16[256,256]{1,0:T(8,128)(2,1)S(1)} %copy-done), custom_call_target="tpu_custom_call" | custom-call | tf_op jit(solution)/shard_map/pallas_call | solution.py:162
  113.4 4.2 %all-to-all-done.2 = bf16[32,16,128]{2,1,0:T(8,128)(2,1)S(1)} async-done(((bf16[32,16,128]{2,1,0:T(8,128)(2,1)}), bf16[32,16,128]{2,1,0:T(8,128)(2,1)S(1)}, u32[]{:S(2)}, u32[]{:S(2)}) %all-to-all-start.2) | async-done | bytes 131104 | tf_op jit(solution)/shard_map/all_to_all | solution.py:199
  (59 shorter events, 14.3 us)
Async XLA Ops:
  0.6 43.2 %collective-permute-start.4 = (bf16[1024,256]{1,0:T(8,128)(2,1)}, bf16[1024,256]{1,0:T(8,128)(2,1)S(1)}, u32[]{:S(2)}, u32[]{:S(2)}) collective-permute-start(bf16[1024,256]{1,0:T(8,128)(2,1)} %param.7), channel_id=1, source_target_pairs={{0,7},{3,4},{4,3},{7,0},{8,15},{11,12},{12,11},{15,8},{16,23},{19,... | collective-permute-start | bytes 1572872 | tf_op jit(solution)/shard_map/ppermute | solution.py:222
  8.9 12.8 %collective-permute-start = (bf16[1024,256]{1,0:T(8,128)(2,1)}, bf16[1024,256]{1,0:T(8,128)(2,1)S(1)}, u32[]{:S(2)}, u32[]{:S(2)}) collective-permute-start(bf16[1024,256]{1,0:T(8,128)(2,1)} %param.7), channel_id=1, source_target_pairs={{0,1},{1,0},{2,3},{3,2},{4,5},{5,4},{6,7},{7,6},{8,9},{9,8},{10,11... | collective-permute-start | bytes 1572872 | tf_op jit(solution)/shard_map/ppermute | solution.py:222
  12.0 17.1 %copy-start.7 = (s32[1,1,512]{2,1,0:T(1,128)}, s32[1,1,512]{2,1,0:T(1,128)S(1)}, u32[]{:S(2)}) copy-start(s32[1,1,512]{2,1,0:T(1,128)S(1)} %get-tuple-element.37) | copy-start | bytes 6148
  12.0 17.1 %copy-start.9 = (s32[1,1,512]{2,1,0:T(1,128)}, s32[1,1,512]{2,1,0:T(1,128)S(1)}, u32[]{:S(2)}) copy-start(s32[1,1,512]{2,1,0:T(1,128)S(1)} %get-tuple-element.38) | copy-start | bytes 6148
  12.0 9.8 %copy-start.2 = (bf16[4,16,256]{2,1,0:T(8,128)(2,1)}, bf16[4,16,256]{2,1,0:T(8,128)(2,1)S(1)}, u32[]{:S(2)}) copy-start(bf16[4,16,256]{2,1,0:T(8,128)(2,1)S(1)} %fusion.16) | copy-start | bytes 98308
  12.0 3.8 %copy-start = (bf16[256,256]{1,0:T(8,128)(2,1)S(1)}, bf16[256,256]{1,0:T(8,128)(2,1)}, u32[]{:S(2)}) copy-start(bf16[256,256]{1,0:T(8,128)(2,1)} %relation_ref.20) | copy-start | bytes 393220
  13.6 3.0 %copy-start.5 = (bf16[512,256]{1,0:T(8,128)(2,1)}, bf16[512,256]{1,0:T(8,128)(2,1)S(1)}, u32[]{:S(2)}) copy-start(bf16[512,256]{1,0:T(8,128)(2,1)S(1)} %fusion.7) | copy-start | bytes 786436
  13.6 2.4 %copy-start.1 = (bf16[1024,256]{1,0:T(8,128)(2,1)S(1)}, bf16[1024,256]{1,0:T(8,128)(2,1)}, u32[]{:S(2)}) copy-start(bf16[1024,256]{1,0:T(8,128)(2,1)} %left_ref.1) | copy-start | bytes 1572868
  14.4 29.5 %collective-permute-start.3 = (bf16[528,256]{1,0:T(8,128)(2,1)}, bf16[528,256]{1,0:T(8,128)(2,1)}, u32[]{:S(2)}, u32[]{:S(2)}) collective-permute-start(bf16[528,256]{1,0:T(8,128)(2,1)} %pad_maximum_fusion), channel_id=1, source_target_pairs={{1,7},{2,4},{5,3},{6,0},{9,15},{10,12},{13,11},{14,8},{17,23},{18,... | collective-permute-start | bytes 811016 | tf_op jit(solution)/shard_map/ppermute | solution.py:222
  24.8 15.0 %collective-permute-start.1 = (bf16[528,256]{1,0:T(8,128)(2,1)}, bf16[528,256]{1,0:T(8,128)(2,1)S(1)}, u32[]{:S(2)}, u32[]{:S(2)}) collective-permute-start(bf16[528,256]{1,0:T(8,128)(2,1)} %get-tuple-element.16), channel_id=1, source_target_pairs={{0,2},{1,3},{2,0},{3,1},{4,6},{5,7},{6,4},{7,5},{8,10},{9,11},{10,... | collective-permute-start | bytes 811016 | tf_op jit(solution)/shard_map/ppermute | solution.py:222
  26.0 17.9 %collective-permute-start.5 = (bf16[1024,256]{1,0:T(8,128)(2,1)S(1)}, bf16[1024,256]{1,0:T(8,128)(2,1)S(1)}, u32[]{:S(2)}, u32[]{:S(2)}) collective-permute-start(bf16[1024,256]{1,0:T(8,128)(2,1)S(1)} %subtract_convert_fusion.2.held_ref), channel_id=1, source_target_pairs={{0,6},{3,5},{4,2},{7,1},{8,14},{11,13},{12,10},{15,9},{16,22},{19,... | collective-permute-start | bytes 1572872 | tf_op jit(solution)/shard_map/ppermute | solution.py:222
  30.1 13.5 %copy-start.6 = (bf16[512,256]{1,0:T(8,128)(2,1)S(1)}, bf16[512,256]{1,0:T(8,128)(2,1)}, u32[]{:S(2)}) copy-start(bf16[512,256]{1,0:T(8,128)(2,1)} %copy-done.5) | copy-start | bytes 786436
  41.3 10.3 %collective-permute-start.6 = (bf16[512,256]{1,0:T(8,128)(2,1)S(1)}, bf16[512,256]{1,0:T(8,128)(2,1)S(1)}, u32[]{:S(2)}, u32[]{:S(2)}) collective-permute-start(bf16[512,256]{1,0:T(8,128)(2,1)S(1)} %shard_map.89), channel_id=1, source_target_pairs={{0,2},{1,3},{2,0},{3,1},{4,6},{5,7},{6,4},{7,5},{8,10},{9,11},{10,... | collective-permute-start | bytes 786440 | tf_op jit(solution)/shard_map/ppermute | solution.py:222
  41.7 12.7 %collective-permute-start.2 = (bf16[528,256]{1,0:T(8,128)(2,1)S(1)}, bf16[528,256]{1,0:T(8,128)(2,1)S(1)}, u32[]{:S(2)}, u32[]{:S(2)}) collective-permute-start(bf16[528,256]{1,0:T(8,128)(2,1)S(1)} %collective-permute-done.1.picked_ref), channel_id=1, source_target_pairs={{0,6},{1,7},{2,4},{3,5},{4,2},{5,3},{6,0},{7,1},{8,14},{9,15},{10,... | collective-permute-start | bytes 811016 | tf_op jit(solution)/shard_map/ppermute | solution.py:222
  43.8 7.8 %copy-start.4 = (s32[1,512]{1,0:T(1,128)S(1)}, s32[1,512]{1,0:T(1,128)}, u32[]{:S(2)}) copy-start(s32[1,512]{1,0:T(1,128)} %get-tuple-element.33.source_ref) | copy-start | bytes 6148
  46.5 6.0 %copy-start.10 = (s32[1,1,512]{2,1,0:T(1,128)S(1)}, s32[1,1,512]{2,1,0:T(1,128)}, u32[]{:S(2)}) copy-start(s32[1,1,512]{2,1,0:T(1,128)} %copy-done.9) | copy-start | bytes 6148
  52.5 0.8 copy-start.8
  53.8 2.1 %copy-start.3 = (bf16[4,16,256]{2,1,0:T(8,128)(2,1)S(1)}, bf16[4,16,256]{2,1,0:T(8,128)(2,1)}, u32[]{:S(2)}) copy-start(bf16[4,16,256]{2,1,0:T(8,128)(2,1)} %copy-done.2) | copy-start | bytes 98308
  58.3 5.4 %collective-permute-start.7 = (bf16[528,256]{1,0:T(8,128)(2,1)S(1)}, bf16[528,256]{1,0:T(8,128)(2,1)S(1)}, u32[]{:S(2)}, u32[]{:S(2)}) collective-permute-start(bf16[528,256]{1,0:T(8,128)(2,1)S(1)} %get-tuple-element.20), channel_id=1, source_target_pairs={{0,8},{1,9},{2,10},{3,11},{4,12},{5,13},{6,14},{7,15},{8,0},{9,1},... | collective-permute-start | bytes 811016 | tf_op jit(solution)/shard_map/ppermute | solution.py:222
  66.8 45.7 %collective-permute-start.8 = (bf16[1024,256]{1,0:T(8,128)(2,1)S(1)}, bf16[1024,256]{1,0:T(8,128)(2,1)S(1)}, u32[]{:S(2)}, u32[]{:S(2)}) collective-permute-start(bf16[1024,256]{1,0:T(8,128)(2,1)S(1)} %subtract_convert_fusion), channel_id=1, source_target_pairs={{0,8},{1,9},{2,10},{3,11},{4,12},{5,13},{6,14},{7,15},{8,0},{9,1},... | collective-permute-start | bytes 1572872 | tf_op jit(solution)/shard_map/ppermute | solution.py:222
  68.1 19.9 %all-to-all-start = ((bf16[32,16,128]{2,1,0:T(8,128)(2,1)}), bf16[32,16,128]{2,1,0:T(8,128)(2,1)S(1)}, u32[]{:S(2)}, u32[]{:S(2)}) async-start(bf16[32,16,128]{2,1,0:T(8,128)(2,1)} %bitcast.12), calls=%async_computation | async-start | bytes 262144 | tf_op jit(solution)/shard_map/all_to_all | solution.py:199
  80.0 30.8 %collective-permute-start.9 = (bf16[512,256]{1,0:T(8,128)(2,1)S(1)}, bf16[512,256]{1,0:T(8,128)(2,1)S(1)}, u32[]{:S(2)}, u32[]{:S(2)}) collective-permute-start(bf16[512,256]{1,0:T(8,128)(2,1)S(1)} %get-tuple-element.24), channel_id=1, source_target_pairs={{0,8},{1,9},{2,10},{3,11},{4,12},{5,13},{6,14},{7,15},{8,0},{9,1},... | collective-permute-start | bytes 786440 | tf_op jit(solution)/shard_map/ppermute | solution.py:222
  104.3 13.2 %all-to-all-start.2 = ((bf16[32,16,128]{2,1,0:T(8,128)(2,1)}), bf16[32,16,128]{2,1,0:T(8,128)(2,1)S(1)}, u32[]{:S(2)}, u32[]{:S(2)}) async-start(bf16[32,16,128]{2,1,0:T(8,128)(2,1)} %bitcast.16), calls=%async_computation.2 | async-start | bytes 262144 | tf_op jit(solution)/shard_map/all_to_all | solution.py:199
